TPU v7x, 32 devices: a whole 2x2x4 slice. The times are simulated.
32 devices in a mesh: groups: 2 (over x), face: 8 (over z, y), sub: 2 (over core).
Axes of the slice: x: 2, y: 2, z: 4, core: 2. Of those that a mesh axis runs over, the one named last changes fastest.
Arguments:
- features: bfloat16 [65536, 64], P(('groups', 'face', 'sub')), parts along dimension 0
- links_fine: int32 [9, 32768], P(None, ('face', 'sub')), may hold values from 0 to 2175, as said below
- sends_fine: int32 [16, 2, 64], P(('face', 'sub')), may hold values from 0 to 2047, as said below
- links_mid: int32 [9, 8192], P(None, ('face', 'sub')), may hold values from 0 to 575, as said below
- sends_mid: int32 [16, 2, 32], P(('face', 'sub')), may hold values from 0 to 511, as said below
- links_coarse: int32 [9, 2048], P(None, ('face', 'sub')), may hold values from 0 to 159, as said below
- sends_coarse: int32 [16, 2, 16], P(('face', 'sub')), may hold values from 0 to 127, as said below
- kernel_enter: bfloat16 [9, 64, 128], replicated, may hold values from -0.25 to 0.25
- gain_enter: float32 [128], replicated, may hold values from 0.5 to 1.5
- shift_enter: float32 [128], replicated, may hold values from -2.5 to 2.5
- kernel_fine: bfloat16 [9, 128, 128], replicated, may hold values from -0.1875 to 0.1875
- gain_fine: float32 [128], replicated, may hold values from 0.5 to 1.5
- shift_fine: float32 [128], replicated, may hold values from -2.5 to 2.5
- kernel_widen: bfloat16 [9, 128, 256], replicated, may hold values from -0.1875 to 0.1875
- gain_widen: float32 [256], replicated, may hold values from 0.5 to 1.5
- shift_widen: float32 [256], replicated, may hold values from -2.5 to 2.5
- kernel_mid: bfloat16 [9, 256, 256], replicated, may hold values from -0.125 to 0.125
- gain_mid: float32 [256], replicated, may hold values from 0.5 to 1.5
- shift_mid: float32 [256], replicated, may hold values from -2.5 to 2.5
- kernel_deep: bfloat16 [9, 256, 512], replicated, may hold values from -0.125 to 0.125
- gain_deep: float32 [512], replicated, may hold values from 0.5 to 1.5
- shift_deep: float32 [512], replicated, may hold values from -2.5 to 2.5
Outputs:
- skip_fine: bfloat16 [65536, 128], P(('groups', 'face', 'sub')), parts along dimension 0
- skip_mid: bfloat16 [16384, 256], P(('groups', 'face', 'sub')), parts along dimension 0
- bottleneck: bfloat16 [4096, 512], P(('groups', 'face', 'sub')), parts along dimension 0
There are 2 independent parts, one for each index of `groups`. A program takes and returns all parts, laid end to end along the dimension named above; an argument that names none is the same for every part. Nothing has to cross between parts.
Inputs may be any that keep to these rules, and one draw needn't show every extreme that they name: links_fine[0, p] is p's own row within its range; every entry below 2048 is a row of the own range, entries from 2048 on index the padded block's received rows. sends_fine[g, 0] lists range g's first 64 rows in some order, sends_fine[g, 1] its last 64 rows in some order. links_mid[0, p] is p's own row within its range; entries from 512 on index the padded block's received rows. sends_mid[g, 0] lists range g's first 32 rows in some order, sends_mid[g, 1] its last 32 rows in some order. links_coarse[0, p] is p's own row within its range; entries from 128 on index the padded block's received rows. sends_coarse[g, 0] lists range g's first 16 rows in some order, sends_coarse[g, 1] its last 16 rows in some order.
All inputs are finite; a program needn't handle non-finite values.
Results may differ from a plain program's by a relative error of at most 0.011.
Values may be sent and summed in bfloat16 or wider, within the bound.
No kernel may reach another device: no remote copies, remote signals or barrier semaphores. Data moves between devices by JAX's collectives and lax.ppermute only.
A program may use at most 64 MiB of HBM per device.

v0:
```python
import jax
import jax.numpy as jnp
from jax import lax
from jax.sharding import PartitionSpec as P


def shifted(value, axis, steps):
    count = lax.axis_size(axis)
    pairs = [(source, (source + steps) % count) for source in range(count)]
    return lax.ppermute(value, axis, pairs)


def unchanged(vector):
    return vector


def pad_block(feat, sends):
    to_left = feat[sends[0, 0]]
    to_right = feat[sends[0, 1]]
    from_left = shifted(to_right, ("face", "sub"), 1)
    from_right = shifted(to_left, ("face", "sub"), -1)
    return jnp.concatenate([feat, from_left, from_right], axis=0)


def convolve(feat, sends, links, kernel):
    padded = pad_block(feat, sends)
    total = jnp.zeros((feat.shape[0], kernel.shape[2]), jnp.float32)
    for tap in range(9):
        total = total + jnp.dot(padded[links[tap]], kernel[tap], preferred_element_type=jnp.float32)
    return total


def normalize(total, gain, shift, count, spread, pick):
    summed = lax.psum(spread(jnp.sum(total, axis=0)), ("face", "sub"))
    mean = pick(summed) / count
    centered = total - mean
    squared = lax.psum(spread(jnp.sum(centered * centered, axis=0)), ("face", "sub"))
    var = pick(squared) / count
    normed = centered * lax.rsqrt(var + 1e-05) * gain + shift
    return jax.nn.gelu(normed, approximate=False).astype(jnp.bfloat16)


def pooling(act):
    return jnp.mean(act.reshape(-1, 4, act.shape[1]).astype(jnp.float32), axis=1).astype(
        jnp.bfloat16
    )


def sharded_layer(feat, sends, links, kernel, gain, shift):
    total = convolve(feat, sends, links, kernel)
    count = float(total.shape[0] * lax.axis_size("face") * lax.axis_size("sub"))
    return normalize(total, gain, shift, count, unchanged, unchanged)


def per_device(
    features,
    links_fine,
    sends_fine,
    links_mid,
    sends_mid,
    links_coarse,
    sends_coarse,
    kernel_enter,
    gain_enter,
    shift_enter,
    kernel_fine,
    gain_fine,
    shift_fine,
    kernel_widen,
    gain_widen,
    shift_widen,
    kernel_mid,
    gain_mid,
    shift_mid,
    kernel_deep,
    gain_deep,
    shift_deep,
):
    first_fine = sharded_layer(
        features, sends_fine, links_fine, kernel_enter, gain_enter, shift_enter
    )
    skip_fine = sharded_layer(
        first_fine, sends_fine, links_fine, kernel_fine, gain_fine, shift_fine
    )
    pooled_mid = pooling(skip_fine)
    first_mid = sharded_layer(
        pooled_mid, sends_mid, links_mid, kernel_widen, gain_widen, shift_widen
    )
    skip_mid = sharded_layer(first_mid, sends_mid, links_mid, kernel_mid, gain_mid, shift_mid)
    pooled_coarse = pooling(skip_mid)
    bottleneck = sharded_layer(
        pooled_coarse, sends_coarse, links_coarse, kernel_deep, gain_deep, shift_deep
    )
    return (skip_fine, skip_mid, bottleneck)


def solution(mesh):
    return jax.shard_map(
        per_device,
        mesh=mesh,
        in_specs=(
            P(("groups", "face", "sub"), None),
            P(None, ("face", "sub")),
            P(("face", "sub"), None, None),
            P(None, ("face", "sub")),
            P(("face", "sub"), None, None),
            P(None, ("face", "sub")),
            P(("face", "sub"), None, None),
            P(),
            P(),
            P(),
            P(),
            P(),
            P(),
            P(),
            P(),
            P(),
            P(),
            P(),
            P(),
            P(),
            P(),
            P(),
        ),
        out_specs=(
            P(("groups", "face", "sub"), None),
            P(("groups", "face", "sub"), None),
            P(("groups", "face", "sub"), None),
        ),
        check_vma=False,
    )
```

profile of v0, /device:TPU:0, one launch (start us, length us, event | category | flops | bytes accessed | tf_op | source)
XLA Modules:
  0.0 590.2 jit_solution(10003050943090886935)
XLA Ops:
  4.5 5.0 collective-permute-start.1
  9.6 1.4 compare_select_fusion.8
  14.8 6.2 %gather_fusion.10 = bf16[2048,64]{1,0:T(8,128)(2,1)S(1)} fusion(bf16[2176,64]{1,0:T(8,128)(2,1)S(1)} %pad_maximum_fusion, s32[2048]{0:T(1024)S(1)} %broadcast_clamp_fusion), kind=kCustom, calls=%fused_computation.10 | custom fusion | bytes 532480 | tf_op jit(solution)/shard_map/gather | solution.py:29
  21.0 8.1 %gather_fusion.9 = bf16[2048,64]{1,0:T(8,128)(2,1)} fusion(bf16[2176,64]{1,0:T(8,128)(2,1)S(1)} %pad_maximum_fusion, s32[2048]{0:T(1024)S(1)} %broadcast_clamp_fusion.1), kind=kCustom, calls=%fused_computation.9 | custom fusion | bytes 532480 | tf_op jit(solution)/shard_map/gather | solution.py:29
  30.4 8.1 %gather_fusion.8 = bf16[2048,64]{1,0:T(8,128)(2,1)} fusion(bf16[2176,64]{1,0:T(8,128)(2,1)S(1)} %pad_maximum_fusion, s32[2048]{0:T(1024)S(1)} %broadcast_clamp_fusion.2), kind=kCustom, calls=%fused_computation.8 | custom fusion | bytes 532480 | tf_op jit(solution)/shard_map/gather | solution.py:29
  38.4 2.3 fusion.193
  40.7 8.0 %gather_fusion.7 = bf16[2048,64]{1,0:T(8,128)(2,1)} fusion(bf16[2176,64]{1,0:T(8,128)(2,1)S(1)} %pad_maximum_fusion, s32[2048]{0:T(1024)S(1)} %broadcast_clamp_fusion.3), kind=kCustom, calls=%fused_computation.7 | custom fusion | bytes 532480 | tf_op jit(solution)/shard_map/gather | solution.py:29
  48.8 2.3 fusion.195
  51.1 8.0 %gather_fusion.6 = bf16[2048,64]{1,0:T(8,128)(2,1)} fusion(bf16[2176,64]{1,0:T(8,128)(2,1)S(1)} %pad_maximum_fusion, s32[2048]{0:T(1024)S(1)} %broadcast_clamp_fusion.4), kind=kCustom, calls=%fused_computation.6 | custom fusion | bytes 532480 | tf_op jit(solution)/shard_map/gather | solution.py:29
  59.1 2.3 fusion.197
  61.4 8.0 %gather_fusion.5 = bf16[2048,64]{1,0:T(8,128)(2,1)} fusion(bf16[2176,64]{1,0:T(8,128)(2,1)S(1)} %pad_maximum_fusion, s32[2048]{0:T(1024)S(1)} %broadcast_clamp_fusion.5), kind=kCustom, calls=%fused_computation.5 | custom fusion | bytes 532480 | tf_op jit(solution)/shard_map/gather | solution.py:29
  69.5 2.3 fusion.199
  71.8 8.0 %gather_fusion.4 = bf16[2048,64]{1,0:T(8,128)(2,1)} fusion(bf16[2176,64]{1,0:T(8,128)(2,1)S(1)} %pad_maximum_fusion, s32[2048]{0:T(1024)S(1)} %broadcast_clamp_fusion.6), kind=kCustom, calls=%fused_computation.4 | custom fusion | bytes 532480 | tf_op jit(solution)/shard_map/gather | solution.py:29
  79.8 2.3 fusion.201
  82.1 8.0 %gather_fusion.3 = bf16[2048,64]{1,0:T(8,128)(2,1)} fusion(bf16[2176,64]{1,0:T(8,128)(2,1)S(1)} %pad_maximum_fusion, s32[2048]{0:T(1024)S(1)} %broadcast_clamp_fusion.7), kind=kCustom, calls=%fused_computation.3 | custom fusion | bytes 532480 | tf_op jit(solution)/shard_map/gather | solution.py:29
  90.2 2.3 fusion.203
  92.5 8.0 %gather_fusion.2 = bf16[2048,64]{1,0:T(8,128)(2,1)} fusion(bf16[2176,64]{1,0:T(8,128)(2,1)S(1)} %pad_maximum_fusion, s32[2048]{0:T(1024)S(1)} %broadcast_clamp_fusion.8), kind=kCustom, calls=%fused_computation.2 | custom fusion | bytes 532480 | tf_op jit(solution)/shard_map/gather | solution.py:29
  100.5 3.5 fusion.230
  104.0 30.2 %psum.70 = f32[128]{0:T(128)S(1)} all-reduce(f32[128]{0:T(128)S(1)} %get-tuple-element.36), channel_id=1, replica_groups=mesh['groups'=2,'face'=8,'sub'=2] {'face','sub'}, use_global_device_ids=true, to_apply=%region_1.0 | all-reduce | flops 128 | bytes 1024 | tf_op jit(solution)/shard_map/psum | solution.py:34
  134.5 29.5 %psum.71 = f32[128]{0:T(128)S(1)} all-reduce(f32[128]{0:T(128)S(1)} %multiply_reduce_fusion.1), channel_id=1, replica_groups=mesh['groups'=2,'face'=8,'sub'=2] {'face','sub'}, use_global_device_ids=true, to_apply=%region_3.0 | all-reduce | flops 128 | bytes 1024 | tf_op jit(solution)/shard_map/psum | solution.py:37
  164.0 2.4 fusion.37
  167.8 4.4 collective-permute-start.3
  172.2 1.4 collective-permute-done.2
  173.7 6.2 %gather_fusion.20 = bf16[2048,128]{1,0:T(8,128)(2,1)S(1)} fusion(bf16[2176,128]{1,0:T(8,128)(2,1)S(1)} %pad_maximum_fusion.1, s32[2048]{0:T(1024)S(1)} %broadcast_clamp_fusion.1), kind=kCustom, calls=%fused_computation.20 | custom fusion | bytes 1056768 | tf_op jit(solution)/shard_map/gather | solution.py:29
  179.9 6.2 %gather_fusion.19 = bf16[2048,128]{1,0:T(8,128)(2,1)S(1)} fusion(bf16[2176,128]{1,0:T(8,128)(2,1)S(1)} %pad_maximum_fusion.1, s32[2048]{0:T(1024)S(1)} %broadcast_clamp_fusion.2), kind=kCustom, calls=%fused_computation.19 | custom fusion | bytes 1056768 | tf_op jit(solution)/shard_map/gather | solution.py:29
  186.1 6.2 %gather_fusion.18 = bf16[2048,128]{1,0:T(8,128)(2,1)S(1)} fusion(bf16[2176,128]{1,0:T(8,128)(2,1)S(1)} %pad_maximum_fusion.1, s32[2048]{0:T(1024)S(1)} %broadcast_clamp_fusion.3), kind=kCustom, calls=%fused_computation.18 | custom fusion | bytes 1056768 | tf_op jit(solution)/shard_map/gather | solution.py:29
  192.3 8.0 %gather_fusion.17 = bf16[2048,128]{1,0:T(8,128)(2,1)} fusion(bf16[2176,128]{1,0:T(8,128)(2,1)S(1)} %pad_maximum_fusion.1, s32[2048]{0:T(1024)S(1)} %broadcast_clamp_fusion.4), kind=kCustom, calls=%fused_computation.17 | custom fusion | bytes 1056768 | tf_op jit(solution)/shard_map/gather | solution.py:29
  200.3 8.0 %gather_fusion.16 = bf16[2048,128]{1,0:T(8,128)(2,1)} fusion(bf16[2176,128]{1,0:T(8,128)(2,1)S(1)} %pad_maximum_fusion.1, s32[2048]{0:T(1024)S(1)} %broadcast_clamp_fusion.5), kind=kCustom, calls=%fused_computation.16 | custom fusion | bytes 1056768 | tf_op jit(solution)/shard_map/gather | solution.py:29
  208.2 8.0 %gather_fusion.15 = bf16[2048,128]{1,0:T(8,128)(2,1)} fusion(bf16[2176,128]{1,0:T(8,128)(2,1)S(1)} %pad_maximum_fusion.1, s32[2048]{0:T(1024)S(1)} %broadcast_clamp_fusion.6), kind=kCustom, calls=%fused_computation.15 | custom fusion | bytes 1056768 | tf_op jit(solution)/shard_map/gather | solution.py:29
  216.2 8.0 %gather_fusion.14 = bf16[2048,128]{1,0:T(8,128)(2,1)} fusion(bf16[2176,128]{1,0:T(8,128)(2,1)S(1)} %pad_maximum_fusion.1, s32[2048]{0:T(1024)S(1)} %broadcast_clamp_fusion.7), kind=kCustom, calls=%fused_computation.14 | custom fusion | bytes 1056768 | tf_op jit(solution)/shard_map/gather | solution.py:29
  224.1 8.0 %gather_fusion.21 = bf16[2048,128]{1,0:T(8,128)(2,1)} fusion(bf16[2176,128]{1,0:T(8,128)(2,1)S(1)} %pad_maximum_fusion.1, s32[2048]{0:T(1024)S(1)} %broadcast_clamp_fusion), kind=kCustom, calls=%fused_computation.21 | custom fusion | bytes 1056768 | tf_op jit(solution)/shard_map/gather | solution.py:29
  232.2 6.2 %gather_fusion.13 = bf16[2048,128]{1,0:T(8,128)(2,1)S(1)} fusion(bf16[2176,128]{1,0:T(8,128)(2,1)S(1)} %pad_maximum_fusion.1, s32[2048]{0:T(1024)S(1)} %broadcast_clamp_fusion.8), kind=kCustom, calls=%fused_computation.13 | custom fusion | bytes 1056768 | tf_op jit(solution)/shard_map/gather | solution.py:29
  245.0 33.9 %psum.72 = f32[128]{0:T(128)S(1)} all-reduce(f32[128]{0:T(128)S(1)} %get-tuple-element.38), channel_id=1, replica_groups=mesh['groups'=2,'face'=8,'sub'=2] {'face','sub'}, use_global_device_ids=true, to_apply=%region_5.0 | all-reduce | flops 128 | bytes 1024 | tf_op jit(solution)/shard_map/psum | solution.py:34
  279.2 29.7 %psum.73 = f32[128]{0:T(128)S(1)} all-reduce(f32[128]{0:T(128)S(1)} %multiply_reduce_fusion), channel_id=1, replica_groups=mesh['groups'=2,'face'=8,'sub'=2] {'face','sub'}, use_global_device_ids=true, to_apply=%region_7.0 | all-reduce | flops 128 | bytes 1024 | tf_op jit(solution)/shard_map/psum | solution.py:37
  308.9 2.4 fusion.40
  313.4 4.5 collective-permute-start.5
  319.2 1.3 gather_fusion.32
  320.6 1.3 gather_fusion.31
  324.0 1.3 gather_fusion.30
  326.4 1.3 gather_fusion.29
  328.8 1.3 gather_fusion.28
  331.2 1.3 gather_fusion.27
  332.6 1.8 fusion.147
  335.8 1.9 fusion.149
  339.0 1.9 fusion.151
  342.2 1.7 fusion.232
  343.9 33.9 %psum.74 = f32[256]{0:T(256)S(1)} all-reduce(f32[256]{0:T(256)S(1)} %get-tuple-element.40), channel_id=1, replica_groups=mesh['groups'=2,'face'=8,'sub'=2] {'face','sub'}, use_global_device_ids=true, to_apply=%region_10.0 | all-reduce | flops 256 | bytes 2048 | tf_op jit(solution)/shard_map/psum | solution.py:34
  378.0 29.5 %psum.75 = f32[256]{0:T(256)S(1)} all-reduce(f32[256]{0:T(256)S(1)} %multiply_reduce_fusion.3), channel_id=1, replica_groups=mesh['groups'=2,'face'=8,'sub'=2] {'face','sub'}, use_global_device_ids=true, to_apply=%region_12.0 | all-reduce | flops 256 | bytes 2048 | tf_op jit(solution)/shard_map/psum | solution.py:37
  410.0 4.4 collective-permute-start.7
  415.9 2.0 gather_fusion.42
  417.9 2.0 gather_fusion.41
  419.8 2.0 gather_fusion.40
  421.8 2.0 gather_fusion.39
  423.7 2.0 gather_fusion.38
  425.7 2.0 gather_fusion.37
  427.7 2.6 gather_fusion.36
  430.2 2.6 gather_fusion.43
  432.8 1.9 gather_fusion.35
  437.3 33.9 %psum.76 = f32[256]{0:T(256)S(1)} all-reduce(f32[256]{0:T(256)S(1)} %get-tuple-element.42), channel_id=1, replica_groups=mesh['groups'=2,'face'=8,'sub'=2] {'face','sub'}, use_global_device_ids=true, to_apply=%region_14.0 | all-reduce | flops 256 | bytes 2048 | tf_op jit(solution)/shard_map/psum | solution.py:34
  471.3 29.5 %psum.77 = f32[256]{0:T(256)S(1)} all-reduce(f32[256]{0:T(256)S(1)} %multiply_reduce_fusion.2), channel_id=1, replica_groups=mesh['groups'=2,'face'=8,'sub'=2] {'face','sub'}, use_global_device_ids=true, to_apply=%region_16.0 | all-reduce | flops 256 | bytes 2048 | tf_op jit(solution)/shard_map/psum | solution.py:37
  504.2 4.7 collective-permute-start.9
  524.0 1.5 fusion.234
  525.5 33.9 %psum.78 = f32[512]{0:T(512)S(1)} all-reduce(f32[512]{0:T(512)S(1)} %get-tuple-element.44), channel_id=1, replica_groups=mesh['groups'=2,'face'=8,'sub'=2] {'face','sub'}, use_global_device_ids=true, to_apply=%region_19.0 | all-reduce | flops 512 | bytes 4096 | tf_op jit(solution)/shard_map/psum | solution.py:34
  559.5 29.5 %psum.79 = f32[512]{0:T(512)S(1)} all-reduce(f32[512]{0:T(512)S(1)} %multiply_reduce_fusion.4), channel_id=1, replica_groups=mesh['groups'=2,'face'=8,'sub'=2] {'face','sub'}, use_global_device_ids=true, to_apply=%region_21.0 | all-reduce | flops 512 | bytes 4096 | tf_op jit(solution)/shard_map/psum | solution.py:37
  (194 shorter events, 56.3 us)
Async XLA Ops:
  0.6 10.4 %copy-start.25 = (s32[1,2,32]{2,1,0:T(2,128)S(1)}, s32[1,2,32]{2,1,0:T(2,128)}, u32[]{:S(2)}) copy-start(s32[1,2,32]{2,1,0:T(2,128)} %param.26) | copy-start | bytes 772
  0.6 10.4 %copy-start.14 = (s32[9,512]{1,0:T(8,128)S(1)}, s32[9,512]{1,0:T(8,128)}, u32[]{:S(2)}) copy-start(s32[9,512]{1,0:T(8,128)} %param.25) | copy-start | bytes 55300
  0.7 10.6 %copy-start.26 = (s32[1,2,16]{2,1,0:T(2,128)S(1)}, s32[1,2,16]{2,1,0:T(2,128)}, u32[]{:S(2)}) copy-start(s32[1,2,16]{2,1,0:T(2,128)} %param.28) | copy-start | bytes 388
  0.7 11.1 %copy-start.15 = (s32[9,128]{1,0:T(8,128)S(1)}, s32[9,128]{1,0:T(8,128)}, u32[]{:S(2)}) copy-start(s32[9,128]{1,0:T(8,128)} %param.27) | copy-start | bytes 13828
  3.3 11.3 %collective-permute-start = (bf16[64,64]{1,0:T(8,128)(2,1)S(1)}, bf16[64,64]{1,0:T(8,128)(2,1)S(1)}, u32[]{:S(2)}, u32[]{:S(2)}) collective-permute-start(bf16[64,64]{1,0:T(8,128)(2,1)S(1)} %gather_fusion), channel_id=1, source_target_pairs={{0,1},{1,2},{2,3},{3,4},{4,5},{5,6},{6,7},{7,8},{8,9},{9,10},{10,1... | collective-permute-start | bytes 24584 | tf_op jit(solution)/shard_map/ppermute | solution.py:10
  4.5 10.2 %collective-permute-start.1 = (bf16[64,64]{1,0:T(8,128)(2,1)S(1)}, bf16[64,64]{1,0:T(8,128)(2,1)S(1)}, u32[]{:S(2)}, u32[]{:S(2)}) collective-permute-start(bf16[64,64]{1,0:T(8,128)(2,1)S(1)} %gather_fusion.1), channel_id=1, source_target_pairs={{0,15},{1,0},{2,1},{3,2},{4,3},{5,4},{6,5},{7,6},{8,7},{9,8},{10,9... | collective-permute-start | bytes 24584 | tf_op jit(solution)/shard_map/ppermute | solution.py:10
  21.0 8.1 %copy-start.13 = (bf16[9,64,128]{2,1,0:T(8,128)(2,1)S(1)}, bf16[9,64,128]{2,1,0:T(8,128)(2,1)}, u32[]{:S(2)}) copy-start(bf16[9,64,128]{2,1,0:T(8,128)(2,1)} %param.29) | copy-start | bytes 442372
  29.1 1.0 copy-start.6
  100.5 63.5 %copy-start.27 = (f32[128]{0:T(128)S(1)}, f32[128]{0:T(128)}, u32[]{:S(2)}) copy-start(f32[128]{0:T(128)} %param.31) | copy-start | bytes 1540
  100.5 63.5 %copy-start.28 = (f32[128]{0:T(128)S(1)}, f32[128]{0:T(128)}, u32[]{:S(2)}) copy-start(f32[128]{0:T(128)} %param.30) | copy-start | bytes 1540
  167.7 5.9 %collective-permute-start.2 = (bf16[64,128]{1,0:T(8,128)(2,1)S(1)}, bf16[64,128]{1,0:T(8,128)(2,1)S(1)}, u32[]{:S(2)}, u32[]{:S(2)}) collective-permute-start(bf16[64,128]{1,0:T(8,128)(2,1)S(1)} %gather_fusion.11), channel_id=1, source_target_pairs={{0,1},{1,2},{2,3},{3,4},{4,5},{5,6},{6,7},{7,8},{8,9},{9,10},{10,1... | collective-permute-start | bytes 49160 | tf_op jit(solution)/shard_map/ppermute | solution.py:10
  167.8 5.9 collective-permute-start.3
  232.2 6.2 %copy-start.12 = (bf16[9,128,128]{2,1,0:T(8,128)(2,1)S(1)}, bf16[9,128,128]{2,1,0:T(8,128)(2,1)}, u32[]{:S(2)}) copy-start(bf16[9,128,128]{2,1,0:T(8,128)(2,1)} %param.32) | copy-start | bytes 884740
  238.9 1.0 copy-start.1
  240.0 1.0 copy-start.2
  241.0 1.0 copy-start.3
  242.1 1.0 copy-start.4
  243.1 1.0 copy-start.5
  244.4 64.5 %copy-start.29 = (f32[128]{0:T(128)S(1)}, f32[128]{0:T(128)}, u32[]{:S(2)}) copy-start(f32[128]{0:T(128)} %param.34) | copy-start | bytes 1540
  244.4 64.5 %copy-start.30 = (f32[128]{0:T(128)S(1)}, f32[128]{0:T(128)}, u32[]{:S(2)}) copy-start(f32[128]{0:T(128)} %param.33) | copy-start | bytes 1540
  308.9 9.0 %copy-start.20 = (s32[16]{0:T(128)S(1)}, s32[16]{0:T(128)}, u32[]{:S(2)}) copy-start(s32[16]{0:T(128)} %get-tuple-element.30) | copy-start | bytes 196
  311.3 9.2 %copy-start.7 = (bf16[2048,128]{1,0:T(8,128)(2,1)}, bf16[2048,128]{1,0:T(8,128)(2,1)S(1)}, u32[]{:S(2)}) copy-start(bf16[2048,128]{1,0:T(8,128)(2,1)S(1)} %fusion.40) | copy-start | bytes 1572868
  312.7 5.8 collective-permute-start.4
  313.4 5.8 collective-permute-start.5
  342.2 65.3 %copy-start.21 = (f32[256]{0:T(256)S(1)}, f32[256]{0:T(256)}, u32[]{:S(2)}) copy-start(f32[256]{0:T(256)} %param.37) | copy-start | bytes 3076
  342.2 65.3 %copy-start.22 = (f32[256]{0:T(256)S(1)}, f32[256]{0:T(256)}, u32[]{:S(2)}) copy-start(f32[256]{0:T(256)} %param.36) | copy-start | bytes 3076
  343.9 70.5 %copy-start.19 = (s32[16]{0:T(128)S(1)}, s32[16]{0:T(128)}, u32[]{:S(2)}) copy-start(s32[16]{0:T(128)} %get-tuple-element.31) | copy-start | bytes 196
  409.9 5.9 %collective-permute-start.6 = (bf16[32,256]{1,0:T(8,128)(2,1)S(1)}, bf16[32,256]{1,0:T(8,128)(2,1)S(1)}, u32[]{:S(2)}, u32[]{:S(2)}) collective-permute-start(bf16[32,256]{1,0:T(8,128)(2,1)S(1)} %gather_fusion.33), channel_id=1, source_target_pairs={{0,1},{1,2},{2,3},{3,4},{4,5},{5,6},{6,7},{7,8},{8,9},{9,10},{10,1... | collective-permute-start | bytes 49160 | tf_op jit(solution)/shard_map/ppermute | solution.py:10
  410.0 5.9 collective-permute-start.7
  432.8 2.0 copy-start.8
  435.5 1.0 copy-start.10
  435.7 1.0 copy-start.11
  436.9 63.9 %copy-start.23 = (f32[256]{0:T(256)S(1)}, f32[256]{0:T(256)}, u32[]{:S(2)}) copy-start(f32[256]{0:T(256)} %param.40) | copy-start | bytes 3076
  436.9 63.9 %copy-start.24 = (f32[256]{0:T(256)S(1)}, f32[256]{0:T(256)}, u32[]{:S(2)}) copy-start(f32[256]{0:T(256)} %param.39) | copy-start | bytes 3076
  500.8 8.1 %copy-start.18 = (s32[128]{0:T(128)S(1)}, s32[128]{0:T(128)}, u32[]{:S(2)}) copy-start(s32[128]{0:T(128)} %get-tuple-element.21) | copy-start | bytes 1540
  502.0 9.2 %copy-start.9 = (bf16[512,256]{1,0:T(8,128)(2,1)}, bf16[512,256]{1,0:T(8,128)(2,1)S(1)}, u32[]{:S(2)}) copy-start(bf16[512,256]{1,0:T(8,128)(2,1)S(1)} %fusion.60) | copy-start | bytes 786436
  502.1 10.2 %copy-start = (bf16[9,256,512]{2,1,0:T(8,128)(2,1)S(1)}, bf16[9,256,512]{2,1,0:T(8,128)(2,1)}, u32[]{:S(2)}) copy-start(bf16[9,256,512]{2,1,0:T(8,128)(2,1)} %param.41) | copy-start | bytes 7077892
  503.4 5.8 collective-permute-start.8
  504.2 6.1 %collective-permute-start.9 = (bf16[16,256]{1,0:T(8,128)(2,1)S(1)}, bf16[16,256]{1,0:T(8,128)(2,1)S(1)}, u32[]{:S(2)}, u32[]{:S(2)}) collective-permute-start(bf16[16,256]{1,0:T(8,128)(2,1)S(1)} %gather_fusion.45), channel_id=1, source_target_pairs={{0,15},{1,0},{2,1},{3,2},{4,3},{5,4},{6,5},{7,6},{8,7},{9,8},{10,9... | collective-permute-start | bytes 24584 | tf_op jit(solution)/shard_map/ppermute | solution.py:10
  523.9 65.0 %copy-start.16 = (f32[512]{0:T(512)S(1)}, f32[512]{0:T(512)}, u32[]{:S(2)}) copy-start(f32[512]{0:T(512)} %param.43) | copy-start | bytes 6148
  524.0 65.0 %copy-start.17 = (f32[512]{0:T(512)S(1)}, f32[512]{0:T(512)}, u32[]{:S(2)}) copy-start(f32[512]{0:T(512)} %param.42) | copy-start | bytes 6148
where the time goes:
time: 592 us; the launch traced here: 590 us
  blocking collectives  313 us (53%)
  local copies, waits for them, and re-layouts  188 us (32%)
  matrix products  41.8 us (7%)
  starting transfers between devices  23.9 us (4%)
  other arithmetic  17.6 us (3%)
    gather x45, local copies, waits for them, and re-layouts, convolve(): padded[links[tap]]  175 us
    psum x5, blocking collectives, normalize(): summed = lax.psum(spread(jnp.sum(total, axis=0)), ('face', 'sub'))  166 us
    psum x5, blocking collectives, normalize(): lax.psum(spread(jnp.sum(centered * centered, axis=0)), ('face', 'sub'))  148 us
    dot_general x45, matrix products, convolve(): jnp.dot(padded[links[tap]], kernel[tap], preferred_element_type=jnp.float32)  41.8 us
    ppermute x10, starting transfers between devices, shifted(): return lax.ppermute(value, axis, pairs)  23.9 us
  transfers between devices with their start and end apart: 10, of which 6 were waited for; matrix products, arithmetic and copies ran while one was open for 1% of the time, Pallas kernels for 0%

commit v1 on v0

v1 whole, which is shorter than its diff:
```python
import functools

import jax
import jax.numpy as jnp
from jax import lax
from jax.experimental import pallas as pl
from jax.experimental.pallas import tpu as pltpu
from jax.sharding import PartitionSpec as P

AXES = ("face", "sub")
BLOCK = 128
WINDOW = 256
TAPS = 9
EPS = 1e-05
VM = pl.BlockSpec(memory_space=pltpu.VMEM)
SM = pl.BlockSpec(memory_space=pltpu.SMEM)


def shifted(value, steps):
    count = lax.axis_size(AXES)
    return lax.ppermute(value, AXES, [(source, (source + steps) % count) for source in range(count)])


def picker(column, width, offset=0):
    places = lax.broadcasted_iota(jnp.int32, (column.shape[0], width), 1) + offset
    return jnp.where(column == places, 1.0, 0.0).astype(jnp.bfloat16)


def listed(rows, order, start):
    halo = rows.shape[0]
    column = jnp.transpose(jnp.broadcast_to(order, (BLOCK, BLOCK)))[start : start + halo, :halo]
    places = lax.broadcasted_iota(jnp.int32, (halo, halo), 1).astype(jnp.float32)
    chosen = jnp.where(column == places, 1.0, 0.0).astype(jnp.bfloat16)
    return jnp.dot(chosen, rows, preferred_element_type=jnp.float32).astype(jnp.bfloat16)


def gathered(sources, column_of, start, width):
    parts = []
    if len(sources) == 1:
        window = sources[0][pl.ds(start, width), :]
        for tap in range(1, TAPS):
            hot = picker(column_of(tap), width)
            parts.append(jnp.dot(hot, window, preferred_element_type=jnp.float32).astype(jnp.bfloat16))
        return parts
    low = sources[0][pl.ds(start, width), :]
    high = sources[1][pl.ds(start, width), :]
    parts.append(jnp.dot(picker(column_of(1), width), high, preferred_element_type=jnp.float32))
    for tap in range(2, TAPS, 2):
        pair = jnp.dot(picker(column_of(tap), width), low, preferred_element_type=jnp.float32)
        if tap + 1 < TAPS:
            pair = pair + jnp.dot(picker(column_of(tap + 1), width), high, preferred_element_type=jnp.float32)
        parts.append(pair)
    return [part.astype(jnp.bfloat16) for part in parts]


def convolve(sources, links, spans, weights, total, halo):
    rows, depth = total.shape[0], weights.shape[0]
    padded = sources[0].shape[0]
    paired = len(sources) == 2

    def joined(parts, own):
        if paired:
            parts = [parts[0] + own] + parts[1:]
        else:
            parts = [own] + parts
        return jnp.concatenate(parts, axis=1)[:, :depth]

    def main(block, carry):
        start = pl.multiple_of(block * BLOCK, BLOCK)
        near = links[pl.ds(start, BLOCK), :] - start
        parts = gathered(sources, lambda tap: near[:, tap - 1 : tap], start, WINDOW)
        own = sources[0][pl.ds(pl.multiple_of(start + halo, 16), BLOCK), :]
        total[pl.ds(start, BLOCK), :] = jnp.dot(joined(parts, own), weights[...], preferred_element_type=jnp.float32)
        return carry

    lax.fori_loop(0, rows // BLOCK, main, 0)
    if padded <= WINDOW:
        return

    @pl.when(spans[2, 0] > 0)
    def _():
        def rest(block, carry):
            start = pl.multiple_of(block * BLOCK, BLOCK)

            def chunk(place, inner):
                @pl.when((place < block) | (place > block + 1))
                def _():
                    first = pl.multiple_of(place * BLOCK, BLOCK)
                    near = links[pl.ds(start, BLOCK), :] - first
                    parts = gathered(sources, lambda tap: near[:, tap - 1 : tap], first, BLOCK)
                    own = jnp.zeros((BLOCK, sources[0].shape[1]), jnp.bfloat16)
                    total[pl.ds(start, BLOCK), :] += jnp.dot(
                        joined(parts, own), weights[...], preferred_element_type=jnp.float32
                    )

                return inner

            return lax.fori_loop(spans[0, block], spans[1, block] + 1, chunk, carry)

        lax.fori_loop(0, rows // BLOCK, rest, 0)


def summarize(total, to_next, to_last, stats):
    rows, channels = total.shape
    edge = to_next.shape[0] - 8
    pieces = 8
    size = rows // pieces
    sums = [jnp.sum(total[i * size : (i + 1) * size, :], axis=0, keepdims=True) for i in range(pieces)]
    mean = functools.reduce(jnp.add, sums) / rows
    squares = []
    for i in range(pieces):
        centred = total[i * size : (i + 1) * size, :] - mean
        squares.append(jnp.sum(centred * centred, axis=0, keepdims=True))
    pair = jnp.concatenate([mean, functools.reduce(jnp.add, squares)], axis=0)
    stats[...] = pair
    if edge > 0:
        tail = jnp.concatenate([pair, jnp.zeros((6, channels), jnp.float32)], axis=0)
        to_next[edge:, :] = tail
        to_last[edge:, :] = tail
        to_next[:edge, :] = total[rows - edge :, :]
        to_last[:edge, :] = total[:edge, :]


def enter_kernel(halo, feat, left, right, order, links, spans, weights, total, to_next, to_last, stats, low, high):
    rows, width = feat.shape
    blank = jnp.zeros((rows, width), jnp.bfloat16)
    edge = jnp.zeros((halo, width), jnp.bfloat16)
    before = listed(left[:halo, :], order[0:1, :], 0)
    after = listed(right[:halo, :], order[1:2, :], 0)
    low[halo : halo + rows, :] = jnp.concatenate([feat[...], blank], axis=1)
    high[halo : halo + rows, :] = jnp.concatenate([blank, feat[...]], axis=1)
    low[:halo, :] = jnp.concatenate([before, edge], axis=1)
    high[:halo, :] = jnp.concatenate([edge, before], axis=1)
    low[halo + rows :, :] = jnp.concatenate([after, edge], axis=1)
    high[halo + rows :, :] = jnp.concatenate([edge, after], axis=1)
    convolve((low, high), links, spans, weights, total, halo)
    summarize(total, to_next, to_last, stats)


def combined(pairs, count):
    mean = functools.reduce(jnp.add, [pair[0:1, :] for pair in pairs]) / len(pairs)
    spread = functools.reduce(jnp.add, [(pair[0:1, :] - mean) * (pair[0:1, :] - mean) for pair in pairs])
    squares = functools.reduce(jnp.add, [pair[1:2, :] for pair in pairs]) + count * spread
    return mean, squares


def norm_of(pairs, count, gain, shift):
    mean, squares = combined([pair[...] for pair in pairs], count)
    scale = lax.rsqrt(squares / (count * len(pairs)) + EPS) * gain[...]
    offset = shift[...]

    def act(raw):
        normed = (raw - mean) * scale + offset
        return (normed * (1.0 + lax.erf(normed * 0.7071067811865476)) * 0.5).astype(jnp.bfloat16)

    return act


def pooled(act):
    rows = act.shape[0]
    row = lax.broadcasted_iota(jnp.int32, (rows // 4, rows), 0)
    col = lax.broadcasted_iota(jnp.int32, (rows // 4, rows), 1)
    quarter = jnp.where((col >= 4 * row) & (col < 4 * row + 4), 0.25, 0.0).astype(jnp.bfloat16)
    return jnp.dot(quarter, act, preferred_element_type=jnp.float32).astype(jnp.bfloat16)


def layer_kernel(halo, listing, pool, count, parts, *refs):
    raw, left, right, order, gain, shift, links, spans, weights = refs[:9]
    pairs = refs[9 : 9 + parts]
    outs = refs[9 + parts :]
    if pool:
        skip, outs = outs[0], outs[1:]
    total, to_next, to_last, stats, source = outs
    act = norm_of(pairs, count, gain, shift)
    rows = total.shape[0]
    fold = pooled if pool else (lambda value: value)
    reach = halo * 4 if pool else halo
    source[:halo, :] = listed(fold(act(left[:reach, :])), order[0:1, :], listing)
    source[halo + rows : rows + 2 * halo, :] = listed(fold(act(right[:reach, :])), order[1:2, :], listing)
    if source.shape[0] > rows + 2 * halo:
        source[rows + 2 * halo :, :] = jnp.zeros((source.shape[0] - rows - 2 * halo, source.shape[1]), jnp.bfloat16)
    step = BLOCK
    out_step = step // 4 if pool else step

    def one(i, carry):
        start = pl.multiple_of(i * step, step)
        value = act(raw[pl.ds(start, step), :])
        if pool:
            skip[pl.ds(start, step), :] = value
        source[pl.ds(pl.multiple_of(i * out_step + halo, 16), out_step), :] = fold(value)
        return carry

    lax.fori_loop(0, raw.shape[0] // step, one, 0)
    convolve((source,), links, spans, weights, total, halo)
    summarize(total, to_next, to_last, stats)


def last_kernel(count, parts, *refs):
    raw, gain, shift = refs[:3]
    out = refs[3 + parts]
    out[...] = norm_of(refs[3 : 3 + parts], count, gain, shift)(raw[...])


def call(body, outs, scratch, *args, smem=(), name):
    return pl.pallas_call(
        body,
        out_shape=outs,
        in_specs=[SM if i in smem else VM for i in range(len(args))],
        out_specs=[VM] * len(outs) if isinstance(outs, (list, tuple)) else VM,
        scratch_shapes=scratch,
        compiler_params=pltpu.CompilerParams(vmem_limit_bytes=32 * 1024 * 1024),
        name=name,
    )(*args)


def table(links, rows, halo):
    places = jnp.where(links < rows, links + halo, jnp.where(links < rows + halo, links - rows, links))[1:]
    by_block = places.reshape(TAPS - 1, rows // BLOCK, BLOCK)
    first = jnp.min(by_block, axis=(0, 2)) // BLOCK
    final = jnp.max(by_block, axis=(0, 2)) // BLOCK
    block = jnp.arange(rows // BLOCK)
    outside = jnp.any((first < block) | (final > block + 1)).astype(jnp.int32)
    spans = jnp.stack([first, final, jnp.full_like(first, outside)])
    return jnp.transpose(places), spans


def phases(count):
    steps, stride, left = [], 4, count // 4
    while left > 1:
        radix = 4 if left % 4 == 0 else (2 if left % 2 == 0 else left)
        steps.append([stride * i for i in range(1, radix)])
        stride, left = stride * radix, left // radix
    return steps


def gather_stats(pairs, rows, count):
    held = rows
    for steps in phases(count):
        mean, squares = combined(pairs, held)
        held = held * len(pairs)
        mine = jnp.concatenate([mean, squares], axis=0)
        pairs = [mine] + [shifted(mine, step) for step in steps]
    return pairs, held


def exchange(to_next, to_last, stats, rows, edge):
    count = lax.axis_size(AXES)
    from_left = shifted(to_next, 1)
    from_right = shifted(to_last, -1)
    across = shifted(stats, 2)
    pairs = [stats, from_left[edge : edge + 2], from_right[edge : edge + 2], across]
    pairs, held = gather_stats(pairs, rows, count)
    return from_left, from_right, pairs, held


def stats_only(stats, rows):
    count = lax.axis_size(AXES)
    pairs = [stats, shifted(stats, 1), shifted(stats, -1), shifted(stats, 2)]
    return gather_stats(pairs, rows, count)


def f32(*shape):
    return jax.ShapeDtypeStruct(shape, jnp.float32)


def bf16(*shape):
    return jax.ShapeDtypeStruct(shape, jnp.bfloat16)


def conv_outs(rows, channels, edge):
    return [f32(rows, channels), f32(edge + 8, channels), f32(edge + 8, channels), f32(2, channels)]


def round_up(value, unit):
    return -(-value // unit) * unit


def per_device(
    features,
    links_fine,
    sends_fine,
    links_mid,
    sends_mid,
    links_coarse,
    sends_coarse,
    kernel_enter,
    gain_enter,
    shift_enter,
    kernel_fine,
    gain_fine,
    shift_fine,
    kernel_widen,
    gain_widen,
    shift_widen,
    kernel_mid,
    gain_mid,
    shift_mid,
    kernel_deep,
    gain_deep,
    shift_deep,
):
    rows_a, rows_b, rows_c = links_fine.shape[1], links_mid.shape[1], links_coarse.shape[1]
    halo_a, halo_b, halo_c = sends_fine.shape[2], sends_mid.shape[2], sends_coarse.shape[2]
    width = features.shape[1]
    weights = [
        kernel.reshape(TAPS * kernel.shape[1], kernel.shape[2])
        for kernel in (kernel_enter, kernel_fine, kernel_widen, kernel_mid, kernel_deep)
    ]
    c_a, c_b, c_c = kernel_enter.shape[2], kernel_widen.shape[2], kernel_deep.shape[2]

    def packed(rows, lists):
        flat = jnp.concatenate(lists).astype(jnp.bfloat16)
        flat = jnp.pad(flat, (0, BLOCK - flat.shape[0])).reshape(-1, width)
        return jnp.concatenate([rows, jnp.pad(flat, ((0, 16 - flat.shape[0]), (0, 0)))], axis=0)

    last_lists = [
        sends_fine[0, 1] - (rows_a - halo_a),
        sends_mid[0, 1] - (rows_b - halo_b),
        sends_coarse[0, 1] - (rows_c - halo_c),
    ]
    first_lists = [sends_fine[0, 0], sends_mid[0, 0], sends_coarse[0, 0]]
    left = shifted(packed(features[rows_a - halo_a :], last_lists), 1)
    right = shifted(packed(features[:halo_a], first_lists), -1)
    words = BLOCK // width
    order = jnp.concatenate(
        [side[halo_a : halo_a + words].reshape(1, BLOCK).astype(jnp.float32) for side in (left, right)], axis=0
    )

    places_a, spans_a = table(links_fine, rows_a, halo_a)
    places_b, spans_b = table(links_mid, rows_b, halo_b)
    places_c, spans_c = table(links_coarse, rows_c, halo_c)

    source_a = pltpu.VMEM((round_up(rows_a + 2 * halo_a, BLOCK), 2 * width), jnp.bfloat16)
    total, to_next, to_last, stats = call(
        functools.partial(enter_kernel, halo_a),
        conv_outs(rows_a, c_a, halo_a),
        [source_a, source_a],
        features,
        left,
        right,
        order,
        places_a,
        spans_a,
        weights[0],
        smem=(5,),
        name="enter",
    )

    def layer(total, to_next, to_last, stats, edge, gain, shift, level, kernel, pool, out_edge, name):
        rows, halo, listing, places, spans = level
        raw_rows, channels = total.shape
        from_left, from_right, pairs, held = exchange(to_next, to_last, stats, raw_rows, edge)
        outs = conv_outs(rows, kernel.shape[1], out_edge)
        if pool:
            outs = [bf16(raw_rows, channels)] + outs
        return call(
            functools.partial(layer_kernel, halo, listing, pool, held, len(pairs)),
            outs,
            [pltpu.VMEM((max(round_up(rows + 2 * halo, BLOCK), WINDOW), channels), jnp.bfloat16)],
            total,
            from_left,
            from_right,
            order,
            gain.reshape(1, -1),
            shift.reshape(1, -1),
            places,
            spans,
            kernel,
            *pairs,
            smem=(7,),
            name=name,
        )

    level_a = (rows_a, halo_a, 0, places_a, spans_a)
    level_b = (rows_b, halo_b, halo_a, places_b, spans_b)
    level_c = (rows_c, halo_c, halo_a + halo_b, places_c, spans_c)
    state = (total, to_next, to_last, stats)
    state = layer(*state, halo_a, gain_enter, shift_enter, level_a, weights[1], False, 4 * halo_b, "fine")
    skip_fine, *state = layer(*state, 4 * halo_b, gain_fine, shift_fine, level_b, weights[2], True, halo_b, "widen")
    state = layer(*state, halo_b, gain_widen, shift_widen, level_b, weights[3], False, 4 * halo_c, "mid")
    skip_mid, *state = layer(*state, 4 * halo_c, gain_mid, shift_mid, level_c, weights[4], True, 8, "deep")
    total, _, _, stats = state
    pairs, held = stats_only(stats, rows_c)
    bottleneck = call(
        functools.partial(last_kernel, held, len(pairs)),
        bf16(rows_c, c_c),
        [],
        total,
        gain_deep.reshape(1, -1),
        shift_deep.reshape(1, -1),
        *pairs,
        name="last",
    )
    return (skip_fine, skip_mid, bottleneck)


def solution(mesh):
    split = P(("groups", "face", "sub"), None)
    links, sends = P(None, AXES), P(AXES, None, None)
    return jax.shard_map(
        per_device,
        mesh=mesh,
        in_specs=(split, links, sends, links, sends, links, sends) + (P(),) * 15,
        out_specs=(split, split, split),
        check_vma=False,
    )
```

time: 592 us -> 147 us (0.25)
  blocking collectives: 313 us -> 0 us
  local copies, waits for them, and re-layouts: 188 us -> 13.4 us
  matrix products: 41.8 us -> 0 us
  Pallas kernels: 0 us -> 32.7 us
  waiting for transfers between devices: 4.41 us -> 34.6 us
  starting transfers between devices: 23.9 us -> 47.3 us
  other arithmetic: 17.6 us -> 11.3 us
  between operations: 1.56 us -> 7.64 us
    psum x10 -> x0, blocking collectives: 313 us -> none  [the longest x5 166 us: normalize(): summed = lax.psum(spread(jnp.sum(total, axis=0)), ('face', 'sub'))]
    gather x55 -> x0, local copies, waits for them, and re-layouts: 181 us -> none  [the longest x45 175 us: convolve(): padded[links[tap]]]
    dot_general x45 -> x0, matrix products: 41.8 us -> none  [convolve(): jnp.dot(padded[links[tap]], kernel[tap], preferred_element_type=jnp.float32)]
    pallas_call x0 -> x6, Pallas kernels: none -> 32.7 us  [call(): pl.pallas_call(body, out_shape=outs, in_specs=[SM if i in smem else VM fo...]
    ppermute x10 -> x32, waiting for transfers between devices: 4.41 us -> 34.6 us  [shifted(): lax.ppermute(value, AXES, [(source, (source + steps) % count) for source...]
    ppermute x10 -> x32, starting transfers between devices: 23.9 us -> 47.3 us  [shifted(): lax.ppermute(value, AXES, [(source, (source + steps) % count) for source...]
    convert_element_type x7 -> x0, other arithmetic: 8.58 us -> none  [the longest x5 8.56 us: normalize(): return jax.nn.gelu(normed, approximate=False).astype(jnp.bfloat16)]
  transfers between devices with their start and end apart: 10 -> 32, of which waited for: 6 -> 16; matrix products, arithmetic and copies ran while one was open for 1% -> 11% of each run, Pallas kernels for 0% -> 0%
where the time goes in v1:
time: 147 us
  starting transfers between devices  47.3 us (32%)
  waiting for transfers between devices  34.6 us (24%)
  Pallas kernels  32.7 us (22%)
  local copies, waits for them, and re-layouts  13.4 us (9%)
  other arithmetic  11.3 us (8%)
  between operations  7.64 us (5%)
    ppermute x32, starting transfers between devices, shifted(): lax.ppermute(value, AXES, [(source, (source + steps) % count) for source...  47.3 us
    ppermute x32, waiting for transfers between devices, shifted(): lax.ppermute(value, AXES, [(source, (source + steps) % count) for source...  34.6 us
    pallas_call x6, Pallas kernels, call(): pl.pallas_call(body, out_shape=outs, in_specs=[SM if i in smem else VM fo...  32.7 us
    unnamed x58, local copies, waits for them, and re-layouts  11.7 us
  transfers between devices with their start and end apart: 32, of which 16 were waited for; matrix products, arithmetic and copies ran while one was open for 11% of the time, Pallas kernels for 0%

profile of v1, /device:TPU:0, one launch (start us, length us, event | category | flops | bytes accessed | tf_op | source)
XLA Modules:
  0.0 146.9 jit_solution(2928184696638495191)
XLA Ops:
  0.6 1.2 copy.124.feat
  1.9 0.7 convert.36
  2.6 0.7 convert.35
  3.3 0.7 convert.34
  4.1 5.5 %collective-permute-start.1 = (bf16[80,64]{1,0:T(8,128)(2,1)S(1)}, bf16[80,64]{1,0:T(8,128)(2,1)S(1)}, u32[]{:S(2)}, u32[]{:S(2)}) collective-permute-start(bf16[80,64]{1,0:T(8,128)(2,1)S(1)} %fusion.3), channel_id=1, source_target_pairs={{0,15},{1,0},{2,1},{3,2},{4,3},{5,4},{6,5},{7,6},{8,7},{9,8},{10,9... | collective-permute-start | bytes 30728 | tf_op jit(solution)/shard_map/ppermute | solution.py:21
  9.7 0.7 convert_bitcast_fusion
  10.3 0.7 convert_bitcast_fusion.1
  11.0 0.7 convert_bitcast_fusion.2
  12.0 0.9 broadcast_add_fusion
  12.9 0.9 broadcast_compare_fusion
  13.8 0.9 slice.285
  14.8 0.3 copy.137
  15.1 1.3 copy.139
  16.5 0.4 copy.136
  16.9 0.4 copy.138
  17.4 1.3 copy.140
  18.7 2.3 %fusion.11 = (s32[2048]{0:T(1024)S(1)}, s32[2048]{0:T(1024)S(1)}, s32[8,2048]{0,1:T(8,128)S(1)}) fusion(pred[8,2048]{0,1:T(8,128)(4,1)S(1)} %copy.136, s32[8,2048]{0,1:T(8,128)S(1)} %copy.137, pred[8,2048]{0,1:T(8,128)(4,1)S(1)} %copy.138, s32[8,2048]{0,1:T(8,128)} %copy.139, s32[8,2048]{0,1:T(8,128)} %copy.140), kind=kLoop, calls=%fused_computation.106 | loop fusion | flops 61440 | bytes 311296 | tf_op jit(solution)/shard_map/reduce_min | solution.py:219
  21.2 0.6 or_reduce_fusion.1
  22.8 0.2 copy.141
  23.0 0.2 copy.143
  23.5 0.2 fusion.12
  24.1 9.5 %enter.1 = (f32[2048,128]{1,0:T(8,128)S(1)}, f32[72,128]{1,0:T(8,128)S(1)}, f32[72,128]{1,0:T(8,128)S(1)}, f32[2,128]{1,0:T(2,128)S(1)}) custom-call(bf16[2048,64]{1,0:T(8,128)(2,1)S(1)} %copy.124.feat, bf16[80,64]{1,0:T(8,128)(2,1)S(1)} %collective-permute-done.left, bf16[80,64]{1,0:T(8,128)(2,1)S(1)} %collective-permute-done.1.right, ...), custom_call_target="tpu_custom_call" | custom-call | tf_op jit(solution)/shard_map/enter/pallas_call | solution.py:205
  33.6 4.5 %collective-permute-start.3 = (f32[72,128]{1,0:T(8,128)S(1)}, f32[72,128]{1,0:T(8,128)S(1)}, u32[]{:S(2)}, u32[]{:S(2)}) collective-permute-start(f32[72,128]{1,0:T(8,128)S(1)} %get-tuple-element.25), channel_id=1, source_target_pairs={{0,15},{1,0},{2,1},{3,2},{4,3},{5,4},{6,5},{7,6},{8,7},{9,8},{10,9... | collective-permute-start | bytes 110600 | tf_op jit(solution)/shard_map/ppermute | solution.py:21
  38.1 6.3 %collective-permute-done.4 = f32[2,128]{1,0:T(2,128)S(1)} collective-permute-done((f32[2,128]{1,0:T(2,128)S(1)}, f32[2,128]{1,0:T(2,128)S(1)}, u32[]{:S(2)}, u32[]{:S(2)}) %collective-permute-start.4) | collective-permute-done | bytes 1056 | tf_op jit(solution)/shard_map/ppermute | solution.py:21
  44.6 3.7 %collective-permute-start.7 = (f32[2,128]{1,0:T(2,128)S(1)}, f32[2,128]{1,0:T(2,128)S(1)}, u32[]{:S(2)}, u32[]{:S(2)}) collective-permute-start(f32[2,128]{1,0:T(2,128)S(1)} %pad_maximum_fusion.3.refs_9_), channel_id=1, source_target_pairs={{0,12},{1,13},{2,14},{3,15},{4,0},{5,1},{6,2},{7,3},{8,4},{9,5},{1... | collective-permute-start | bytes 3080 | tf_op jit(solution)/shard_map/ppermute | solution.py:21
  48.3 1.5 %collective-permute-done.5.refs_10_ = f32[2,128]{1,0:T(2,128)S(1)} collective-permute-done((f32[2,128]{1,0:T(2,128)S(1)}, f32[2,128]{1,0:T(2,128)S(1)}, u32[]{:S(2)}, u32[]{:S(2)}) %collective-permute-start.5) | collective-permute-done | bytes 1056 | tf_op jit(solution)/shard_map/ppermute | solution.py:21
  49.8 0.6 collective-permute-done.7.refs_12_
  50.4 9.8 %fine.1 = (f32[2048,128]{1,0:T(8,128)S(1)}, f32[136,128]{1,0:T(8,128)S(1)}, f32[136,128]{1,0:T(8,128)S(1)}, f32[2,128]{1,0:T(2,128)S(1)}) custom-call(f32[2048,128]{1,0:T(8,128)S(1)} %get-tuple-element.23.refs_0_, f32[72,128]{1,0:T(8,128)S(1)} %collective-permute-done.2.refs_1_, f32[72,128]{1,0:T(8,128)S(1)} %collective-permute-done.3.refs_2_, ...), custom_call_target="tpu_custom_call" | custom-call | tf_op jit(solution)/shard_map/fine/pallas_call | solution.py:205
  60.2 1.0 copy-done.2
  61.2 4.4 %collective-permute-start.9 = (f32[136,128]{1,0:T(8,128)S(1)}, f32[136,128]{1,0:T(8,128)S(1)}, u32[]{:S(2)}, u32[]{:S(2)}) collective-permute-start(f32[136,128]{1,0:T(8,128)S(1)} %get-tuple-element.29), channel_id=1, source_target_pairs={{0,15},{1,0},{2,1},{3,2},{4,3},{5,4},{6,5},{7,6},{8,7},{9,8},{10,9... | collective-permute-start | bytes 208904 | tf_op jit(solution)/shard_map/ppermute | solution.py:21
  65.6 0.6 or_reduce_fusion
  67.0 4.9 %collective-permute-done.10 = f32[2,128]{1,0:T(2,128)S(1)} collective-permute-done((f32[2,128]{1,0:T(2,128)S(1)}, f32[2,128]{1,0:T(2,128)S(1)}, u32[]{:S(2)}, u32[]{:S(2)}) %collective-permute-start.10) | collective-permute-done | bytes 1056 | tf_op jit(solution)/shard_map/ppermute | solution.py:21
  72.0 0.2 collective-permute-start.12
  72.2 3.6 %collective-permute-start.13 = (f32[2,128]{1,0:T(2,128)S(1)}, f32[2,128]{1,0:T(2,128)S(1)}, u32[]{:S(2)}, u32[]{:S(2)}) collective-permute-start(f32[2,128]{1,0:T(2,128)S(1)} %pad_maximum_fusion.4.refs_9_), channel_id=1, source_target_pairs={{0,12},{1,13},{2,14},{3,15},{4,0},{5,1},{6,2},{7,3},{8,4},{9,5},{1... | collective-permute-start | bytes 3080 | tf_op jit(solution)/shard_map/ppermute | solution.py:21
  75.9 1.5 %collective-permute-done.11.refs_10_ = f32[2,128]{1,0:T(2,128)S(1)} collective-permute-done((f32[2,128]{1,0:T(2,128)S(1)}, f32[2,128]{1,0:T(2,128)S(1)}, u32[]{:S(2)}, u32[]{:S(2)}) %collective-permute-start.11) | collective-permute-done | bytes 1056 | tf_op jit(solution)/shard_map/ppermute | solution.py:21
  77.4 0.6 collective-permute-done.13.refs_12_
  78.0 1.2 copy-done.3
  79.2 6.3 %widen.1 = (bf16[2048,128]{1,0:T(8,128)(2,1)}, f32[512,256]{1,0:T(8,128)S(1)}, f32[40,256]{1,0:T(8,128)S(1)}, f32[40,256]{1,0:T(8,128)S(1)}, f32[2,256]{1,0:T(2,128)S(1)}) custom-call(f32[2048,128]{1,0:T(8,128)S(1)} %copy-done.3, f32[136,128]{1,0:T(8,128)S(1)} %collective-permute-done.8.refs_1_, f32[136,128]{1,0:T(8,128)S(1)} %collective-permute-done.9.refs_2_, ...), custom_call_target="tpu_custom_call" | custom-call | tf_op jit(solution)/shard_map/widen/pallas_call | solution.py:205
  85.5 0.8 copy-done.5
  86.3 4.4 %collective-permute-start.15 = (f32[40,256]{1,0:T(8,128)S(1)}, f32[40,256]{1,0:T(8,128)S(1)}, u32[]{:S(2)}, u32[]{:S(2)}) collective-permute-start(f32[40,256]{1,0:T(8,128)S(1)} %get-tuple-element.34), channel_id=1, source_target_pairs={{0,15},{1,0},{2,1},{3,2},{4,3},{5,4},{6,5},{7,6},{8,7},{9,8},{10,9... | collective-permute-start | bytes 122888 | tf_op jit(solution)/shard_map/ppermute | solution.py:21
  90.8 6.3 %collective-permute-done.16 = f32[2,256]{1,0:T(2,128)S(1)} collective-permute-done((f32[2,256]{1,0:T(2,128)S(1)}, f32[2,256]{1,0:T(2,128)S(1)}, u32[]{:S(2)}, u32[]{:S(2)}) %collective-permute-start.16) | collective-permute-done | bytes 2080 | tf_op jit(solution)/shard_map/ppermute | solution.py:21
  97.1 0.2 collective-permute-start.18
  97.4 3.6 %collective-permute-start.19 = (f32[2,256]{1,0:T(2,128)S(1)}, f32[2,256]{1,0:T(2,128)S(1)}, u32[]{:S(2)}, u32[]{:S(2)}) collective-permute-start(f32[2,256]{1,0:T(2,128)S(1)} %pad_maximum_fusion.1.refs_9_), channel_id=1, source_target_pairs={{0,12},{1,13},{2,14},{3,15},{4,0},{5,1},{6,2},{7,3},{8,4},{9,5},{1... | collective-permute-start | bytes 6152 | tf_op jit(solution)/shard_map/ppermute | solution.py:21
  101.6 0.9 collective-permute-done.17.refs_10_
  102.5 0.6 collective-permute-done.19.refs_12_
  103.1 1.3 copy-done.1
  104.4 1.0 copy-done.6
  105.4 3.4 %mid.1 = (f32[512,256]{1,0:T(8,128)S(1)}, f32[72,256]{1,0:T(8,128)S(1)}, f32[72,256]{1,0:T(8,128)S(1)}, f32[2,256]{1,0:T(2,128)S(1)}) custom-call(f32[512,256]{1,0:T(8,128)S(1)} %copy-done.6, f32[40,256]{1,0:T(8,128)S(1)} %collective-permute-done.14.refs_1_, f32[40,256]{1,0:T(8,128)S(1)} %collective-permute-done.15.refs_2_, ...), custom_call_target="tpu_custom_call" | custom-call | tf_op jit(solution)/shard_map/mid/pallas_call | solution.py:205
  108.9 4.4 %collective-permute-start.21 = (f32[72,256]{1,0:T(8,128)S(1)}, f32[72,256]{1,0:T(8,128)S(1)}, u32[]{:S(2)}, u32[]{:S(2)}) collective-permute-start(f32[72,256]{1,0:T(8,128)S(1)} %get-tuple-element.38), channel_id=1, source_target_pairs={{0,15},{1,0},{2,1},{3,2},{4,3},{5,4},{6,5},{7,6},{8,7},{9,8},{10,9... | collective-permute-start | bytes 221192 | tf_op jit(solution)/shard_map/ppermute | solution.py:21
  113.3 0.7 fusion.13
  119.2 1.1 collective-permute-done.22
  120.4 1.0 collective-permute-start.24
  121.4 2.8 %collective-permute-start.25 = (f32[2,256]{1,0:T(2,128)S(1)}, f32[2,256]{1,0:T(2,128)S(1)}, u32[]{:S(2)}, u32[]{:S(2)}) collective-permute-start(f32[2,256]{1,0:T(2,128)S(1)} %pad_maximum_fusion.2.refs_9_), channel_id=1, source_target_pairs={{0,12},{1,13},{2,14},{3,15},{4,0},{5,1},{6,2},{7,3},{8,4},{9,5},{1... | collective-permute-start | bytes 6152 | tf_op jit(solution)/shard_map/ppermute | solution.py:21
  124.4 1.4 collective-permute-done.23.refs_10_
  125.8 0.6 collective-permute-done.25.refs_12_
  126.3 3.0 %deep.1 = (bf16[512,256]{1,0:T(8,128)(2,1)}, f32[128,512]{1,0:T(8,128)S(1)}, f32[16,512]{1,0:T(8,128)}, f32[16,512]{1,0:T(8,128)}, f32[2,512]{1,0:T(2,128)S(1)}) custom-call(f32[512,256]{1,0:T(8,128)S(1)} %get-tuple-element.36.refs_0_, f32[72,256]{1,0:T(8,128)S(1)} %collective-permute-done.20.refs_1_, f32[72,256]{1,0:T(8,128)S(1)} %collective-permute-done.21.refs_2_, ...), custom_call_target="tpu_custom_call" | custom-call | tf_op jit(solution)/shard_map/deep/pallas_call | solution.py:205
  129.3 4.4 %collective-permute-start.27 = (f32[2,512]{1,0:T(2,128)S(1)}, f32[2,512]{1,0:T(2,128)S(1)}, u32[]{:S(2)}, u32[]{:S(2)}) collective-permute-start(f32[2,512]{1,0:T(2,128)S(1)} %get-tuple-element.42), channel_id=1, source_target_pairs={{0,15},{1,0},{2,1},{3,2},{4,3},{5,4},{6,5},{7,6},{8,7},{9,8},{10,9... | collective-permute-start | bytes 12296 | tf_op jit(solution)/shard_map/ppermute | solution.py:21
  133.8 1.3 collective-permute-done.26
  135.1 5.0 %collective-permute-done.28 = f32[2,512]{1,0:T(2,128)S(1)} collective-permute-done((f32[2,512]{1,0:T(2,128)S(1)}, f32[2,512]{1,0:T(2,128)S(1)}, u32[]{:S(2)}, u32[]{:S(2)}) %collective-permute-start.28) | collective-permute-done | bytes 4128 | tf_op jit(solution)/shard_map/ppermute | solution.py:21
  140.2 0.2 collective-permute-start.30
  140.4 3.6 %collective-permute-start.31 = (f32[2,512]{1,0:T(2,128)S(1)}, f32[2,512]{1,0:T(2,128)S(1)}, u32[]{:S(2)}, u32[]{:S(2)}) collective-permute-start(f32[2,512]{1,0:T(2,128)S(1)} %pad_maximum_fusion.refs_3_), channel_id=1, source_target_pairs={{0,12},{1,13},{2,14},{3,15},{4,0},{5,1},{6,2},{7,3},{8,4},{9,5},{1... | collective-permute-start | bytes 12296 | tf_op jit(solution)/shard_map/ppermute | solution.py:21
  144.0 1.6 %collective-permute-done.29.refs_4_ = f32[2,512]{1,0:T(2,128)S(1)} collective-permute-done((f32[2,512]{1,0:T(2,128)S(1)}, f32[2,512]{1,0:T(2,128)S(1)}, u32[]{:S(2)}, u32[]{:S(2)}) %collective-permute-start.29) | collective-permute-done | bytes 4128 | tf_op jit(solution)/shard_map/ppermute | solution.py:21
  145.6 0.6 collective-permute-done.31.refs_6_
  146.1 0.8 last.1
  (133 shorter events, 3.3 us)
Async XLA Ops:
  4.1 19.7 %collective-permute-start.1 = (bf16[80,64]{1,0:T(8,128)(2,1)S(1)}, bf16[80,64]{1,0:T(8,128)(2,1)S(1)}, u32[]{:S(2)}, u32[]{:S(2)}) collective-permute-start(bf16[80,64]{1,0:T(8,128)(2,1)S(1)} %fusion.3), channel_id=1, source_target_pairs={{0,15},{1,0},{2,1},{3,2},{4,3},{5,4},{6,5},{7,6},{8,7},{9,8},{10,9... | collective-permute-start | bytes 30728 | tf_op jit(solution)/shard_map/ppermute | solution.py:21
  11.9 12.1 %collective-permute-start = (bf16[80,64]{1,0:T(8,128)(2,1)S(1)}, bf16[80,64]{1,0:T(8,128)(2,1)S(1)}, u32[]{:S(2)}, u32[]{:S(2)}) collective-permute-start(bf16[80,64]{1,0:T(8,128)(2,1)S(1)} %fusion.2), channel_id=1, source_target_pairs={{0,1},{1,2},{2,3},{3,4},{4,5},{5,6},{6,7},{7,8},{8,9},{9,10},{10,1... | collective-permute-start | bytes 30728 | tf_op jit(solution)/shard_map/ppermute | solution.py:21
  18.7 3.1 %copy-start.19 = (s32[9,512]{1,0:T(8,128)S(1)}, s32[9,512]{1,0:T(8,128)}, u32[]{:S(2)}) copy-start(s32[9,512]{1,0:T(8,128)} %param.25) | copy-start | bytes 55300
  21.0 3.1 %copy-start.8 = (bf16[9,64,128]{2,1,0:T(8,128)(2,1)S(1)}, bf16[9,64,128]{2,1,0:T(8,128)(2,1)}, u32[]{:S(2)}) copy-start(bf16[9,64,128]{2,1,0:T(8,128)(2,1)} %param.29) | copy-start | bytes 442372
  21.0 29.4 %copy-start.7 = (bf16[9,128,128]{2,1,0:T(8,128)(2,1)S(1)}, bf16[9,128,128]{2,1,0:T(8,128)(2,1)}, u32[]{:S(2)}) copy-start(bf16[9,128,128]{2,1,0:T(8,128)(2,1)} %param.32) | copy-start | bytes 884740
  21.0 29.4 %copy-start.15 = (f32[128]{0:T(128)S(1)}, f32[128]{0:T(128)}, u32[]{:S(2)}) copy-start(f32[128]{0:T(128)} %param.30) | copy-start | bytes 1540
  21.0 29.4 %copy-start.16 = (f32[128]{0:T(128)S(1)}, f32[128]{0:T(128)}, u32[]{:S(2)}) copy-start(f32[128]{0:T(128)} %param.31) | copy-start | bytes 1540
  23.7 54.3 %copy-start.4 = (bf16[9,128,256]{2,1,0:T(8,128)(2,1)S(1)}, bf16[9,128,256]{2,1,0:T(8,128)(2,1)}, u32[]{:S(2)}) copy-start(bf16[9,128,256]{2,1,0:T(8,128)(2,1)} %param.35) | copy-start | bytes 1769476
  23.7 54.3 %copy-start.17 = (f32[128]{0:T(128)S(1)}, f32[128]{0:T(128)}, u32[]{:S(2)}) copy-start(f32[128]{0:T(128)} %param.33) | copy-start | bytes 1540
  23.7 54.2 %copy-start.18 = (f32[128]{0:T(128)S(1)}, f32[128]{0:T(128)}, u32[]{:S(2)}) copy-start(f32[128]{0:T(128)} %param.34) | copy-start | bytes 1540
  33.6 57.2 %copy-start.20 = (s32[9,128]{1,0:T(8,128)S(1)}, s32[9,128]{1,0:T(8,128)}, u32[]{:S(2)}) copy-start(s32[9,128]{1,0:T(8,128)} %param.27) | copy-start | bytes 13828
  33.6 10.8 %collective-permute-start.2 = (f32[72,128]{1,0:T(8,128)S(1)}, f32[72,128]{1,0:T(8,128)S(1)}, u32[]{:S(2)}, u32[]{:S(2)}) collective-permute-start(f32[72,128]{1,0:T(8,128)S(1)} %get-tuple-element.24), channel_id=1, source_target_pairs={{0,1},{1,2},{2,3},{3,4},{4,5},{5,6},{6,7},{7,8},{8,9},{9,10},{10,1... | collective-permute-start | bytes 110600 | tf_op jit(solution)/shard_map/ppermute | solution.py:21
  33.6 10.8 %collective-permute-start.3 = (f32[72,128]{1,0:T(8,128)S(1)}, f32[72,128]{1,0:T(8,128)S(1)}, u32[]{:S(2)}, u32[]{:S(2)}) collective-permute-start(f32[72,128]{1,0:T(8,128)S(1)} %get-tuple-element.25), channel_id=1, source_target_pairs={{0,15},{1,0},{2,1},{3,2},{4,3},{5,4},{6,5},{7,6},{8,7},{9,8},{10,9... | collective-permute-start | bytes 110600 | tf_op jit(solution)/shard_map/ppermute | solution.py:21
  38.1 6.3 %collective-permute-start.4 = (f32[2,128]{1,0:T(2,128)S(1)}, f32[2,128]{1,0:T(2,128)S(1)}, u32[]{:S(2)}, u32[]{:S(2)}) collective-permute-start(f32[2,128]{1,0:T(2,128)S(1)} %get-tuple-element.26), channel_id=1, source_target_pairs={{0,2},{1,3},{2,4},{3,5},{4,6},{5,7},{6,8},{7,9},{8,10},{9,11},{10,... | collective-permute-start | bytes 3080 | tf_op jit(solution)/shard_map/ppermute | solution.py:21
  44.4 5.4 %collective-permute-start.5 = (f32[2,128]{1,0:T(2,128)S(1)}, f32[2,128]{1,0:T(2,128)S(1)}, u32[]{:S(2)}, u32[]{:S(2)}) collective-permute-start(f32[2,128]{1,0:T(2,128)S(1)} %pad_maximum_fusion.3.refs_9_), channel_id=1, source_target_pairs={{0,4},{1,5},{2,6},{3,7},{4,8},{5,9},{6,10},{7,11},{8,12},{9,13},{1... | collective-permute-start | bytes 3080 | tf_op jit(solution)/shard_map/ppermute | solution.py:21
  44.5 5.4 %collective-permute-start.6 = (f32[2,128]{1,0:T(2,128)S(1)}, f32[2,128]{1,0:T(2,128)S(1)}, u32[]{:S(2)}, u32[]{:S(2)}) collective-permute-start(f32[2,128]{1,0:T(2,128)S(1)} %pad_maximum_fusion.3.refs_9_), channel_id=1, source_target_pairs={{0,8},{1,9},{2,10},{3,11},{4,12},{5,13},{6,14},{7,15},{8,0},{9,1},... | collective-permute-start | bytes 3080 | tf_op jit(solution)/shard_map/ppermute | solution.py:21
  44.6 5.8 %collective-permute-start.7 = (f32[2,128]{1,0:T(2,128)S(1)}, f32[2,128]{1,0:T(2,128)S(1)}, u32[]{:S(2)}, u32[]{:S(2)}) collective-permute-start(f32[2,128]{1,0:T(2,128)S(1)} %pad_maximum_fusion.3.refs_9_), channel_id=1, source_target_pairs={{0,12},{1,13},{2,14},{3,15},{4,0},{5,1},{6,2},{7,3},{8,4},{9,5},{1... | collective-permute-start | bytes 3080 | tf_op jit(solution)/shard_map/ppermute | solution.py:21
  50.4 52.7 %copy-start.11 = (f32[256]{0:T(256)S(1)}, f32[256]{0:T(256)}, u32[]{:S(2)}) copy-start(f32[256]{0:T(256)} %param.36) | copy-start | bytes 3076
  50.4 52.7 %copy-start.12 = (f32[256]{0:T(256)S(1)}, f32[256]{0:T(256)}, u32[]{:S(2)}) copy-start(f32[256]{0:T(256)} %param.37) | copy-start | bytes 3076
  60.2 1.0 copy-start.2
  61.2 10.7 %collective-permute-start.8 = (f32[136,128]{1,0:T(8,128)S(1)}, f32[136,128]{1,0:T(8,128)S(1)}, u32[]{:S(2)}, u32[]{:S(2)}) collective-permute-start(f32[136,128]{1,0:T(8,128)S(1)} %get-tuple-element.28), channel_id=1, source_target_pairs={{0,1},{1,2},{2,3},{3,4},{4,5},{5,6},{6,7},{7,8},{8,9},{9,10},{10,1... | collective-permute-start | bytes 208904 | tf_op jit(solution)/shard_map/ppermute | solution.py:21
  61.2 10.7 %collective-permute-start.9 = (f32[136,128]{1,0:T(8,128)S(1)}, f32[136,128]{1,0:T(8,128)S(1)}, u32[]{:S(2)}, u32[]{:S(2)}) collective-permute-start(f32[136,128]{1,0:T(8,128)S(1)} %get-tuple-element.29), channel_id=1, source_target_pairs={{0,15},{1,0},{2,1},{3,2},{4,3},{5,4},{6,5},{7,6},{8,7},{9,8},{10,9... | collective-permute-start | bytes 208904 | tf_op jit(solution)/shard_map/ppermute | solution.py:21
  65.6 6.3 %collective-permute-start.10 = (f32[2,128]{1,0:T(2,128)S(1)}, f32[2,128]{1,0:T(2,128)S(1)}, u32[]{:S(2)}, u32[]{:S(2)}) collective-permute-start(f32[2,128]{1,0:T(2,128)S(1)} %get-tuple-element.30), channel_id=1, source_target_pairs={{0,2},{1,3},{2,4},{3,5},{4,6},{5,7},{6,8},{7,9},{8,10},{9,11},{10,... | collective-permute-start | bytes 3080 | tf_op jit(solution)/shard_map/ppermute | solution.py:21
  72.0 5.4 %collective-permute-start.11 = (f32[2,128]{1,0:T(2,128)S(1)}, f32[2,128]{1,0:T(2,128)S(1)}, u32[]{:S(2)}, u32[]{:S(2)}) collective-permute-start(f32[2,128]{1,0:T(2,128)S(1)} %pad_maximum_fusion.4.refs_9_), channel_id=1, source_target_pairs={{0,4},{1,5},{2,6},{3,7},{4,8},{5,9},{6,10},{7,11},{8,12},{9,13},{1... | collective-permute-start | bytes 3080 | tf_op jit(solution)/shard_map/ppermute | solution.py:21
  72.0 5.4 %collective-permute-start.12 = (f32[2,128]{1,0:T(2,128)S(1)}, f32[2,128]{1,0:T(2,128)S(1)}, u32[]{:S(2)}, u32[]{:S(2)}) collective-permute-start(f32[2,128]{1,0:T(2,128)S(1)} %pad_maximum_fusion.4.refs_9_), channel_id=1, source_target_pairs={{0,8},{1,9},{2,10},{3,11},{4,12},{5,13},{6,14},{7,15},{8,0},{9,1},... | collective-permute-start | bytes 3080 | tf_op jit(solution)/shard_map/ppermute | solution.py:21
  72.2 5.7 %collective-permute-start.13 = (f32[2,128]{1,0:T(2,128)S(1)}, f32[2,128]{1,0:T(2,128)S(1)}, u32[]{:S(2)}, u32[]{:S(2)}) collective-permute-start(f32[2,128]{1,0:T(2,128)S(1)} %pad_maximum_fusion.4.refs_9_), channel_id=1, source_target_pairs={{0,12},{1,13},{2,14},{3,15},{4,0},{5,1},{6,2},{7,3},{8,4},{9,5},{1... | collective-permute-start | bytes 3080 | tf_op jit(solution)/shard_map/ppermute | solution.py:21
  78.0 1.2 copy-start.3
  79.2 47.2 %copy-start = (bf16[9,256,512]{2,1,0:T(8,128)(2,1)S(1)}, bf16[9,256,512]{2,1,0:T(8,128)(2,1)}, u32[]{:S(2)}) copy-start(bf16[9,256,512]{2,1,0:T(8,128)(2,1)} %param.41) | copy-start | bytes 7077892
  79.2 47.2 %copy-start.13 = (f32[256]{0:T(256)S(1)}, f32[256]{0:T(256)}, u32[]{:S(2)}) copy-start(f32[256]{0:T(256)} %param.39) | copy-start | bytes 3076
  79.2 47.2 %copy-start.14 = (f32[256]{0:T(256)S(1)}, f32[256]{0:T(256)}, u32[]{:S(2)}) copy-start(f32[256]{0:T(256)} %param.40) | copy-start | bytes 3076
  85.5 0.8 copy-start.5
  86.3 10.7 %collective-permute-start.14 = (f32[40,256]{1,0:T(8,128)S(1)}, f32[40,256]{1,0:T(8,128)S(1)}, u32[]{:S(2)}, u32[]{:S(2)}) collective-permute-start(f32[40,256]{1,0:T(8,128)S(1)} %get-tuple-element.33), channel_id=1, source_target_pairs={{0,1},{1,2},{2,3},{3,4},{4,5},{5,6},{6,7},{7,8},{8,9},{9,10},{10,1... | collective-permute-start | bytes 122888 | tf_op jit(solution)/shard_map/ppermute | solution.py:21
  86.3 10.7 %collective-permute-start.15 = (f32[40,256]{1,0:T(8,128)S(1)}, f32[40,256]{1,0:T(8,128)S(1)}, u32[]{:S(2)}, u32[]{:S(2)}) collective-permute-start(f32[40,256]{1,0:T(8,128)S(1)} %get-tuple-element.34), channel_id=1, source_target_pairs={{0,15},{1,0},{2,1},{3,2},{4,3},{5,4},{6,5},{7,6},{8,7},{9,8},{10,9... | collective-permute-start | bytes 122888 | tf_op jit(solution)/shard_map/ppermute | solution.py:21
  90.8 6.3 %collective-permute-start.16 = (f32[2,256]{1,0:T(2,128)S(1)}, f32[2,256]{1,0:T(2,128)S(1)}, u32[]{:S(2)}, u32[]{:S(2)}) collective-permute-start(f32[2,256]{1,0:T(2,128)S(1)} %get-tuple-element.35), channel_id=1, source_target_pairs={{0,2},{1,3},{2,4},{3,5},{4,6},{5,7},{6,8},{7,9},{8,10},{9,11},{10,... | collective-permute-start | bytes 6152 | tf_op jit(solution)/shard_map/ppermute | solution.py:21
  97.1 5.4 %collective-permute-start.17 = (f32[2,256]{1,0:T(2,128)S(1)}, f32[2,256]{1,0:T(2,128)S(1)}, u32[]{:S(2)}, u32[]{:S(2)}) collective-permute-start(f32[2,256]{1,0:T(2,128)S(1)} %pad_maximum_fusion.1.refs_9_), channel_id=1, source_target_pairs={{0,4},{1,5},{2,6},{3,7},{4,8},{5,9},{6,10},{7,11},{8,12},{9,13},{1... | collective-permute-start | bytes 6152 | tf_op jit(solution)/shard_map/ppermute | solution.py:21
  97.1 5.4 %collective-permute-start.18 = (f32[2,256]{1,0:T(2,128)S(1)}, f32[2,256]{1,0:T(2,128)S(1)}, u32[]{:S(2)}, u32[]{:S(2)}) collective-permute-start(f32[2,256]{1,0:T(2,128)S(1)} %pad_maximum_fusion.1.refs_9_), channel_id=1, source_target_pairs={{0,8},{1,9},{2,10},{3,11},{4,12},{5,13},{6,14},{7,15},{8,0},{9,1},... | collective-permute-start | bytes 6152 | tf_op jit(solution)/shard_map/ppermute | solution.py:21
  97.4 5.7 %collective-permute-start.19 = (f32[2,256]{1,0:T(2,128)S(1)}, f32[2,256]{1,0:T(2,128)S(1)}, u32[]{:S(2)}, u32[]{:S(2)}) collective-permute-start(f32[2,256]{1,0:T(2,128)S(1)} %pad_maximum_fusion.1.refs_9_), channel_id=1, source_target_pairs={{0,12},{1,13},{2,14},{3,15},{4,0},{5,1},{6,2},{7,3},{8,4},{9,5},{1... | collective-permute-start | bytes 6152 | tf_op jit(solution)/shard_map/ppermute | solution.py:21
  103.1 1.3 copy-start.1
  104.4 1.0 copy-start.6
  105.4 40.7 %copy-start.9 = (f32[512]{0:T(512)S(1)}, f32[512]{0:T(512)}, u32[]{:S(2)}) copy-start(f32[512]{0:T(512)} %param.42) | copy-start | bytes 6148
  105.4 40.7 %copy-start.10 = (f32[512]{0:T(512)S(1)}, f32[512]{0:T(512)}, u32[]{:S(2)}) copy-start(f32[512]{0:T(512)} %param.43) | copy-start | bytes 6148
  108.8 11.5 %collective-permute-start.20 = (f32[72,256]{1,0:T(8,128)S(1)}, f32[72,256]{1,0:T(8,128)S(1)}, u32[]{:S(2)}, u32[]{:S(2)}) collective-permute-start(f32[72,256]{1,0:T(8,128)S(1)} %get-tuple-element.37), channel_id=1, source_target_pairs={{0,1},{1,2},{2,3},{3,4},{4,5},{5,6},{6,7},{7,8},{8,9},{9,10},{10,1... | collective-permute-start | bytes 221192 | tf_op jit(solution)/shard_map/ppermute | solution.py:21
  108.9 11.4 %collective-permute-start.21 = (f32[72,256]{1,0:T(8,128)S(1)}, f32[72,256]{1,0:T(8,128)S(1)}, u32[]{:S(2)}, u32[]{:S(2)}) collective-permute-start(f32[72,256]{1,0:T(8,128)S(1)} %get-tuple-element.38), channel_id=1, source_target_pairs={{0,15},{1,0},{2,1},{3,2},{4,3},{5,4},{6,5},{7,6},{8,7},{9,8},{10,9... | collective-permute-start | bytes 221192 | tf_op jit(solution)/shard_map/ppermute | solution.py:21
  114.0 6.3 %collective-permute-start.22 = (f32[2,256]{1,0:T(2,128)S(1)}, f32[2,256]{1,0:T(2,128)S(1)}, u32[]{:S(2)}, u32[]{:S(2)}) collective-permute-start(f32[2,256]{1,0:T(2,128)S(1)} %get-tuple-element.39), channel_id=1, source_target_pairs={{0,2},{1,3},{2,4},{3,5},{4,6},{5,7},{6,8},{7,9},{8,10},{9,11},{10,... | collective-permute-start | bytes 6152 | tf_op jit(solution)/shard_map/ppermute | solution.py:21
  120.3 5.4 %collective-permute-start.23 = (f32[2,256]{1,0:T(2,128)S(1)}, f32[2,256]{1,0:T(2,128)S(1)}, u32[]{:S(2)}, u32[]{:S(2)}) collective-permute-start(f32[2,256]{1,0:T(2,128)S(1)} %pad_maximum_fusion.2.refs_9_), channel_id=1, source_target_pairs={{0,4},{1,5},{2,6},{3,7},{4,8},{5,9},{6,10},{7,11},{8,12},{9,13},{1... | collective-permute-start | bytes 6152 | tf_op jit(solution)/shard_map/ppermute | solution.py:21
  120.4 5.4 %collective-permute-start.24 = (f32[2,256]{1,0:T(2,128)S(1)}, f32[2,256]{1,0:T(2,128)S(1)}, u32[]{:S(2)}, u32[]{:S(2)}) collective-permute-start(f32[2,256]{1,0:T(2,128)S(1)} %pad_maximum_fusion.2.refs_9_), channel_id=1, source_target_pairs={{0,8},{1,9},{2,10},{3,11},{4,12},{5,13},{6,14},{7,15},{8,0},{9,1},... | collective-permute-start | bytes 6152 | tf_op jit(solution)/shard_map/ppermute | solution.py:21
  121.4 5.0 %collective-permute-start.25 = (f32[2,256]{1,0:T(2,128)S(1)}, f32[2,256]{1,0:T(2,128)S(1)}, u32[]{:S(2)}, u32[]{:S(2)}) collective-permute-start(f32[2,256]{1,0:T(2,128)S(1)} %pad_maximum_fusion.2.refs_9_), channel_id=1, source_target_pairs={{0,12},{1,13},{2,14},{3,15},{4,0},{5,1},{6,2},{7,3},{8,4},{9,5},{1... | collective-permute-start | bytes 6152 | tf_op jit(solution)/shard_map/ppermute | solution.py:21
  129.3 5.7 %collective-permute-start.26 = (f32[2,512]{1,0:T(2,128)S(1)}, f32[2,512]{1,0:T(2,128)S(1)}, u32[]{:S(2)}, u32[]{:S(2)}) collective-permute-start(f32[2,512]{1,0:T(2,128)S(1)} %get-tuple-element.42), channel_id=1, source_target_pairs={{0,1},{1,2},{2,3},{3,4},{4,5},{5,6},{6,7},{7,8},{8,9},{9,10},{10,1... | collective-permute-start | bytes 12296 | tf_op jit(solution)/shard_map/ppermute | solution.py:21
  129.3 5.8 %collective-permute-start.27 = (f32[2,512]{1,0:T(2,128)S(1)}, f32[2,512]{1,0:T(2,128)S(1)}, u32[]{:S(2)}, u32[]{:S(2)}) collective-permute-start(f32[2,512]{1,0:T(2,128)S(1)} %get-tuple-element.42), channel_id=1, source_target_pairs={{0,15},{1,0},{2,1},{3,2},{4,3},{5,4},{6,5},{7,6},{8,7},{9,8},{10,9... | collective-permute-start | bytes 12296 | tf_op jit(solution)/shard_map/ppermute | solution.py:21
  133.8 6.3 %collective-permute-start.28 = (f32[2,512]{1,0:T(2,128)S(1)}, f32[2,512]{1,0:T(2,128)S(1)}, u32[]{:S(2)}, u32[]{:S(2)}) collective-permute-start(f32[2,512]{1,0:T(2,128)S(1)} %get-tuple-element.42), channel_id=1, source_target_pairs={{0,2},{1,3},{2,4},{3,5},{4,6},{5,7},{6,8},{7,9},{8,10},{9,11},{10,... | collective-permute-start | bytes 12296 | tf_op jit(solution)/shard_map/ppermute | solution.py:21
  140.1 5.5 %collective-permute-start.29 = (f32[2,512]{1,0:T(2,128)S(1)}, f32[2,512]{1,0:T(2,128)S(1)}, u32[]{:S(2)}, u32[]{:S(2)}) collective-permute-start(f32[2,512]{1,0:T(2,128)S(1)} %pad_maximum_fusion.refs_3_), channel_id=1, source_target_pairs={{0,4},{1,5},{2,6},{3,7},{4,8},{5,9},{6,10},{7,11},{8,12},{9,13},{1... | collective-permute-start | bytes 12296 | tf_op jit(solution)/shard_map/ppermute | solution.py:21
  140.2 5.4 %collective-permute-start.30 = (f32[2,512]{1,0:T(2,128)S(1)}, f32[2,512]{1,0:T(2,128)S(1)}, u32[]{:S(2)}, u32[]{:S(2)}) collective-permute-start(f32[2,512]{1,0:T(2,128)S(1)} %pad_maximum_fusion.refs_3_), channel_id=1, source_target_pairs={{0,8},{1,9},{2,10},{3,11},{4,12},{5,13},{6,14},{7,15},{8,0},{9,1},... | collective-permute-start | bytes 12296 | tf_op jit(solution)/shard_map/ppermute | solution.py:21
  140.4 5.7 %collective-permute-start.31 = (f32[2,512]{1,0:T(2,128)S(1)}, f32[2,512]{1,0:T(2,128)S(1)}, u32[]{:S(2)}, u32[]{:S(2)}) collective-permute-start(f32[2,512]{1,0:T(2,128)S(1)} %pad_maximum_fusion.refs_3_), channel_id=1, source_target_pairs={{0,12},{1,13},{2,14},{3,15},{4,0},{5,1},{6,2},{7,3},{8,4},{9,5},{1... | collective-permute-start | bytes 12296 | tf_op jit(solution)/shard_map/ppermute | solution.py:21

commit v2 on v1

v2 whole, which is shorter than its diff:
```python
import functools

import jax
import jax.numpy as jnp
from jax import lax
from jax.experimental import pallas as pl
from jax.experimental.pallas import tpu as pltpu
from jax.sharding import PartitionSpec as P


AXES = ("face", "sub")
BLOCK = 128
WINDOW = 256
TAPS = 9
EPS = 1e-05
VM = pl.BlockSpec(memory_space=pltpu.VMEM)
HERE = pl.BlockSpec(memory_space=pltpu.HBM)


def shifted(value, steps):
    count = lax.axis_size(AXES)
    return lax.ppermute(value, AXES, [(source, (source + steps) % count) for source in range(count)])


def swapped(value, mask):
    count = lax.axis_size(AXES)
    return lax.ppermute(value, AXES, [(source, source ^ mask) for source in range(count)])


def hots(near, width):
    places = lax.broadcasted_iota(jnp.int32, (near.shape[0], width), 1)
    return [jnp.where(near[:, tap : tap + 1] == places, 1.0, 0.0).astype(jnp.bfloat16) for tap in range(TAPS - 1)]


def listed(rows, order, start):
    halo = rows.shape[0]
    column = jnp.transpose(jnp.broadcast_to(order, (BLOCK, BLOCK)))[start : start + halo, :halo]
    places = lax.broadcasted_iota(jnp.int32, (halo, halo), 1).astype(jnp.float32)
    chosen = jnp.where(column == places, 1.0, 0.0).astype(jnp.bfloat16)
    return jnp.dot(chosen, rows, preferred_element_type=jnp.float32).astype(jnp.bfloat16)


def dot(a, b):
    return jnp.dot(a, b, preferred_element_type=jnp.float32)


def picked(sources, near, start, width):
    hot = hots(near, width)
    if len(sources) == 1:
        window = sources[0][pl.ds(start, width), :]
        rows = dot(jnp.concatenate(hot, axis=0), window).astype(jnp.bfloat16)
        return [rows[i * BLOCK : (i + 1) * BLOCK] for i in range(TAPS - 1)]
    low = dot(jnp.concatenate(hot[1::2], axis=0), sources[0][pl.ds(start, width), :])
    high = dot(jnp.concatenate(hot[0::2], axis=0), sources[1][pl.ds(start, width), :])
    low = [low[i * BLOCK : (i + 1) * BLOCK] for i in range(4)]
    high = [high[i * BLOCK : (i + 1) * BLOCK] for i in range(4)]
    pieces = [high[0]] + [low[i] + high[i + 1] for i in range(3)] + [low[3]]
    return [piece.astype(jnp.bfloat16) for piece in pieces]


def convolve(sources, links, weights, total, columns, halo):
    rows, depth = total.shape[0], weights.shape[0]
    padded, lanes = sources[0].shape
    paired = len(sources) == 2

    def places(block):
        link = links[1:, pl.ds(pl.multiple_of(block * BLOCK, BLOCK), BLOCK)]
        place = jnp.where(link < rows, link + halo, jnp.where(link < rows + halo, link - rows, link))
        return jnp.transpose(place)

    def main(block, far):
        start = pl.multiple_of(block * BLOCK, BLOCK)
        near = places(block) - start
        own = sources[0][pl.ds(pl.multiple_of(start + halo, 16), BLOCK), :]
        pieces = picked(sources, near, start, WINDOW)
        pieces = [pieces[0] + own] + pieces[1:] if paired else [own] + pieces
        for i, piece in enumerate(pieces):
            columns[pl.ds(start, BLOCK), i * lanes : (i + 1) * lanes] = piece
        return jnp.maximum(far, jnp.where((near < 0) | (near >= WINDOW), 1, 0))

    far = lax.fori_loop(0, rows // BLOCK, main, jnp.zeros((BLOCK, TAPS - 1), jnp.int32), unroll=min(2, rows // BLOCK))
    step = min(rows, 512)

    def multiply(i, carry):
        part = pl.ds(pl.multiple_of(i * step, step), step)
        total[part, :] = dot(columns[part, :depth], weights[...])
        return carry

    lax.fori_loop(0, rows // step, multiply, 0)
    if padded <= WINDOW:
        return

    @pl.when(jnp.max(far) > 0)
    def _():
        def rest(block, carry):
            start = pl.multiple_of(block * BLOCK, BLOCK)

            def chunk(place, inner):
                @pl.when((place < block) | (place > block + 1))
                def _():
                    first = pl.multiple_of(place * BLOCK, BLOCK)
                    pieces = picked(sources, places(block) - first, first, BLOCK)
                    pieces = pieces if paired else [jnp.zeros_like(pieces[0])] + pieces
                    gathered = jnp.concatenate(pieces, axis=1)[:, :depth]
                    total[pl.ds(start, BLOCK), :] += dot(gathered, weights[...])

                return inner

            return lax.fori_loop(0, padded // BLOCK, chunk, carry)

        lax.fori_loop(0, rows // BLOCK, rest, 0)


def summarize(total, stats, *edges):
    rows, _ = total.shape
    pieces = 8
    size = rows // pieces
    sums = [jnp.sum(total[i * size : (i + 1) * size, :], axis=0, keepdims=True) for i in range(pieces)]
    mean = functools.reduce(jnp.add, sums) / rows
    squares = []
    for i in range(pieces):
        centred = total[i * size : (i + 1) * size, :] - mean
        squares.append(jnp.sum(centred * centred, axis=0, keepdims=True))
    stats[...] = jnp.concatenate([mean, functools.reduce(jnp.add, squares)], axis=0)
    for target, start in zip(edges, (0, rows)):
        edge = target.shape[0]
        target[...] = total[start - edge if start else 0 : start or edge, :]


def start_copies(pairs, sems):
    copies = [pltpu.make_async_copy(source, target, sems.at[i]) for i, (source, target) in enumerate(pairs)]
    for copy in copies:
        copy.start()
    return copies


def pack_kernel(inner, feat, sends_a, sends_b, sends_c, to_last, to_next, first, final, *scratch):
    held, sems = scratch[:3], scratch[3]
    width, rows = feat.shape
    pairs = [(feat.at[:, :BLOCK], first), (feat.at[:, rows - BLOCK :], final)]
    for copy in start_copies(pairs + list(zip((sends_a, sends_b, sends_c), held)), sems):
        copy.wait()
    halo = to_next.shape[0] - 16
    for target, edge, side in ((to_last, first, 0), (to_next, final, 1)):
        turned = jnp.transpose(edge[...].astype(jnp.float32))
        turned = turned[BLOCK - halo :] if side else turned[:halo]
        lists = [sends[0, side : side + 1, :] - before * side for sends, before in zip(held, inner)]
        used = sum(part.shape[1] for part in lists)
        order = jnp.concatenate(lists + [jnp.zeros((1, BLOCK - used), jnp.int32)], axis=1).astype(jnp.float32)
        blank = jnp.zeros((halo, BLOCK - width), jnp.float32)
        target[:halo, :] = jnp.concatenate([turned, blank], axis=1).astype(jnp.bfloat16)
        target[halo:, :] = jnp.broadcast_to(order, (16, BLOCK)).astype(jnp.bfloat16)


def stage_kernel(count, *refs):
    after, feat = refs[:2]
    sources, targets = refs[2 : 2 + count], refs[2 + count : 2 + 2 * count]
    turned, flat, sems = refs[2 + 2 * count :]
    del after
    copies = start_copies([(feat, flat)] + list(zip(sources, targets)), sems)
    copies[0].wait()
    for i in range(turned.shape[0] // BLOCK):
        part = flat[:, i * BLOCK : (i + 1) * BLOCK].astype(jnp.float32)
        turned[i * BLOCK : (i + 1) * BLOCK, :] = jnp.transpose(part).astype(jnp.bfloat16)
    for copy in copies[1:]:
        copy.wait()


def enter_kernel(halo, feat, left, right, links, weights, total, stats, to_last, to_next, order, low, high, columns):
    rows, width = feat.shape
    blank = jnp.zeros((rows, width), jnp.bfloat16)
    edge = jnp.zeros((halo, width), jnp.bfloat16)
    order[...] = jnp.concatenate([left[halo : halo + 1, :], right[halo : halo + 1, :]], axis=0).astype(jnp.float32)
    before = listed(left[:halo, :width], order[0:1, :], 0)
    after = listed(right[:halo, :width], order[1:2, :], 0)
    low[halo : halo + rows, :] = jnp.concatenate([feat[...], blank], axis=1)
    high[halo : halo + rows, :] = jnp.concatenate([blank, feat[...]], axis=1)
    low[:halo, :] = jnp.concatenate([before, edge], axis=1)
    high[:halo, :] = jnp.concatenate([edge, before], axis=1)
    low[halo + rows :, :] = jnp.concatenate([after, edge], axis=1)
    high[halo + rows :, :] = jnp.concatenate([edge, after], axis=1)
    convolve((low, high), links, weights, total, columns, halo)
    summarize(total, stats, to_last, to_next)


def combined(pairs, count):
    mean = functools.reduce(jnp.add, [pair[0:1, :] for pair in pairs]) / len(pairs)
    spread = functools.reduce(jnp.add, [(pair[0:1, :] - mean) * (pair[0:1, :] - mean) for pair in pairs])
    squares = functools.reduce(jnp.add, [pair[1:2, :] for pair in pairs]) + count * spread
    return mean, squares


def norm_of(pairs, count, gain, shift):
    mean, squares = combined([pair[...] for pair in pairs], count)
    scale = lax.rsqrt(squares / (count * len(pairs)) + EPS) * gain[...]
    offset = shift[...]

    def act(raw):
        normed = (raw - mean) * scale + offset
        return (normed * (1.0 + lax.erf(normed * 0.7071067811865476)) * 0.5).astype(jnp.bfloat16)

    return act


def pooled(act):
    rows = act.shape[0]
    row = lax.broadcasted_iota(jnp.int32, (rows // 4, rows), 0)
    col = lax.broadcasted_iota(jnp.int32, (rows // 4, rows), 1)
    quarter = jnp.where((col >= 4 * row) & (col < 4 * row + 4), 0.25, 0.0).astype(jnp.bfloat16)
    return jnp.dot(quarter, act, preferred_element_type=jnp.float32).astype(jnp.bfloat16)


def layer_kernel(halo, listing, pool, count, parts, *refs):
    raw, left, right, order, gain, shift, links, weights = refs[:8]
    pairs = refs[8 : 8 + parts]
    outs = refs[8 + parts :]
    if pool:
        skip, outs = outs[0], outs[1:]
    total, stats, *edges, source, columns = outs
    act = norm_of(pairs, count, gain, shift)
    rows = total.shape[0]
    fold = pooled if pool else (lambda value: value)
    reach = halo * 4 if pool else halo
    source[:halo, :] = listed(fold(act(left[:reach, :])), order[0:1, :], listing)
    source[halo + rows : rows + 2 * halo, :] = listed(fold(act(right[:reach, :])), order[1:2, :], listing)
    if source.shape[0] > rows + 2 * halo:
        source[rows + 2 * halo :, :] = jnp.zeros((source.shape[0] - rows - 2 * halo, source.shape[1]), jnp.bfloat16)
    step = BLOCK
    out_step = step // 4 if pool else step

    def one(i, carry):
        start = pl.multiple_of(i * step, step)
        value = act(raw[pl.ds(start, step), :])
        if pool:
            skip[pl.ds(start, step), :] = value
        source[pl.ds(pl.multiple_of(i * out_step + halo, 16), out_step), :] = fold(value)
        return carry

    lax.fori_loop(0, raw.shape[0] // step, one, 0, unroll=2)
    convolve((source,), links, weights, total, columns, halo)
    summarize(total, stats, *edges)


def last_kernel(count, parts, *refs):
    raw, gain, shift = refs[:3]
    out = refs[3 + parts]
    out[...] = norm_of(refs[3 : 3 + parts], count, gain, shift)(raw[...])


def call(body, outs, scratch, *args, here=(), flops=0, traffic=0):
    args = [pltpu.with_memory_space_constraint(arg, pltpu.HBM) if i in here else arg for i, arg in enumerate(args)]
    return pl.pallas_call(
        body,
        out_shape=outs,
        in_specs=[HERE if i in here else VM for i in range(len(args))],
        out_specs=[VM] * len(outs) if isinstance(outs, (list, tuple)) else VM,
        scratch_shapes=scratch,
        compiler_params=pltpu.CompilerParams(vmem_limit_bytes=16 * 1024 * 1024),
        cost_estimate=pl.CostEstimate(flops=flops, bytes_accessed=traffic, transcendentals=0) if traffic else None,
    )(*args)


def gather_stats(stats, rows):
    count = lax.axis_size(AXES)
    pairs, held, stride = [stats], rows, 1
    while stride < count:
        if stride > 1:
            mean, squares = combined(pairs, held)
            held = held * len(pairs)
            pairs = [jnp.concatenate([mean, squares], axis=0)]
        radix = min(4, count // stride)
        pairs = pairs + [swapped(pairs[0], stride * i) for i in range(1, radix)]
        stride = stride * radix
    return pairs, held


def exchange(stats, to_last, to_next, rows):
    from_left, from_right = shifted(to_next, 1), shifted(to_last, -1)
    pairs, held = gather_stats(stats, rows)
    return from_left, from_right, pairs, held


def f32(*shape):
    return jax.ShapeDtypeStruct(shape, jnp.float32)


def bf16(*shape):
    return jax.ShapeDtypeStruct(shape, jnp.bfloat16)


def conv_outs(rows, channels, edge):
    return [f32(rows, channels), f32(2, channels)] + [f32(edge, channels)] * (2 if edge else 0)


def round_up(value, unit):
    return -(-value // unit) * unit


def per_device(
    features,
    links_fine,
    sends_fine,
    links_mid,
    sends_mid,
    links_coarse,
    sends_coarse,
    kernel_enter,
    gain_enter,
    shift_enter,
    kernel_fine,
    gain_fine,
    shift_fine,
    kernel_widen,
    gain_widen,
    shift_widen,
    kernel_mid,
    gain_mid,
    shift_mid,
    kernel_deep,
    gain_deep,
    shift_deep,
):
    rows_a, rows_b, rows_c = links_fine.shape[1], links_mid.shape[1], links_coarse.shape[1]
    halo_a, halo_b, halo_c = sends_fine.shape[2], sends_mid.shape[2], sends_coarse.shape[2]
    c_a, c_c = kernel_enter.shape[2], kernel_deep.shape[2]

    inner = (rows_a - halo_a, rows_b - halo_b, rows_c - halo_c)
    width = features.shape[1]
    flat = jnp.transpose(features)
    to_last, to_next = call(
        functools.partial(pack_kernel, inner),
        [bf16(halo_a + 16, BLOCK)] * 2,
        [pltpu.VMEM((width, BLOCK), jnp.bfloat16)] * 2
        + [pltpu.VMEM(sends.shape, jnp.int32) for sends in (sends_fine, sends_mid, sends_coarse)]
        + [pltpu.SemaphoreType.DMA((5,))],
        flat,
        sends_fine,
        sends_mid,
        sends_coarse,
        here=range(4),
    )
    left, right = shifted(to_next, 1), shifted(to_last, -1)
    kernels = (kernel_enter, kernel_fine, kernel_widen, kernel_mid, kernel_deep)
    norms = (gain_enter, shift_enter, gain_fine, shift_fine, gain_widen, shift_widen, gain_mid, shift_mid, gain_deep, shift_deep)
    held = [kernel.reshape(TAPS * kernel.shape[1], kernel.shape[2]) for kernel in kernels]
    held = held + list(norms) + [links_fine, links_mid, links_coarse]
    *held, turned = call(
        functools.partial(stage_kernel, len(held)),
        [jax.ShapeDtypeStruct(value.shape, value.dtype) for value in held] + [bf16(rows_a, width)],
        [pltpu.VMEM(flat.shape, jnp.bfloat16), pltpu.SemaphoreType.DMA((len(held) + 1,))],
        to_next,
        flat,
        *held,
        here=range(1, len(held) + 2),
        traffic=8 * 1024 * 1024,
    )
    weights, norms, links = held[:5], held[5:15], held[15:]
    source_a = pltpu.VMEM((round_up(rows_a + 2 * halo_a, BLOCK), 2 * width), jnp.bfloat16)
    *state, order = call(
        functools.partial(enter_kernel, halo_a),
        conv_outs(rows_a, c_a, halo_a) + [f32(2, BLOCK)],
        [source_a, source_a, pltpu.VMEM((rows_a, 5 * BLOCK), jnp.bfloat16)],
        turned,
        left,
        right,
        links[0],
        weights[0],
    )

    def layer(at, state, level, pool, out_edge):
        total, stats, to_last, to_next = state
        rows, halo, listing, links = level
        kernel, gain, shift = weights[at], norms[2 * at - 2], norms[2 * at - 1]
        raw_rows, channels = total.shape
        from_left, from_right, pairs, held = exchange(stats, to_last, to_next, raw_rows)
        outs = conv_outs(rows, kernel.shape[1], out_edge)
        if pool:
            outs = [bf16(raw_rows, channels)] + outs
        return call(
            functools.partial(layer_kernel, halo, listing, pool, held, len(pairs)),
            outs,
            [
                pltpu.VMEM((max(round_up(rows + 2 * halo, BLOCK), WINDOW), channels), jnp.bfloat16),
                pltpu.VMEM((rows, TAPS * channels), jnp.bfloat16),
            ],
            total,
            from_left,
            from_right,
            order,
            gain.reshape(1, -1),
            shift.reshape(1, -1),
            links,
            kernel,
            *pairs,
        )

    level_a = (rows_a, halo_a, 0, links[0])
    level_b = (rows_b, halo_b, halo_a, links[1])
    level_c = (rows_c, halo_c, halo_a + halo_b, links[2])
    state = layer(1, state, level_a, False, 4 * halo_b)
    skip_fine, *state = layer(2, state, level_b, True, halo_b)
    state = layer(3, state, level_b, False, 4 * halo_c)
    skip_mid, *state = layer(4, state, level_c, True, 0)
    total, stats = state
    pairs, count = gather_stats(stats, rows_c)
    bottleneck = call(
        functools.partial(last_kernel, count, len(pairs)),
        bf16(rows_c, c_c),
        [],
        total,
        norms[8].reshape(1, -1),
        norms[9].reshape(1, -1),
        *pairs,
    )
    return (skip_fine, skip_mid, bottleneck)


def solution(mesh):
    split = P(("groups", "face", "sub"), None)
    links, sends = P(None, AXES), P(AXES, None, None)
    return jax.shard_map(
        per_device,
        mesh=mesh,
        in_specs=(split, links, sends, links, sends, links, sends) + (P(),) * 15,
        out_specs=(split, split, split),
        check_vma=False,
    )
```

time: 147 us -> 99.7 us (0.68)
  waiting for transfers between devices: 34.6 us -> 14 us
  local copies, waits for them, and re-layouts: 13.4 us -> 0 us
  other arithmetic: 11.3 us -> 0.13 us
  starting transfers between devices: 47.3 us -> 55.1 us
  between operations: 7.64 us -> 0.85 us
  Pallas kernels: 32.7 us -> 29.4 us
    ppermute x0 -> x30, starting transfers between devices: none -> 31.8 us  [swapped(): lax.ppermute(value, AXES, [(source, source ^ mask) for source in range(co...]
    ppermute x32 -> x10, waiting for transfers between devices: 34.6 us -> 3.25 us  [shifted(): lax.ppermute(value, AXES, [(source, (source + steps) % count) for source...]
    ppermute x32 -> x10, starting transfers between devices: 47.3 us -> 23.3 us  [shifted(): lax.ppermute(value, AXES, [(source, (source + steps) % count) for source...]
    unnamed x58 -> x0, local copies, waits for them, and re-layouts: 11.7 us -> none
    ppermute x0 -> x30, waiting for transfers between devices: none -> 10.8 us  [swapped(): lax.ppermute(value, AXES, [(source, source ^ mask) for source in range(co...]
    pallas_call x6 -> x8, Pallas kernels: 32.7 us -> 29.4 us  [call(): pl.pallas_call(body, out_shape=outs, in_specs=[HERE if i in here else VM...]
    sub x6 -> x0, other arithmetic: 2.99 us -> none  [the longest x3 0.94 us: table(): links - rows]
    reduce_min x2 -> x0, other arithmetic: 2.48 us -> none  [table(): first = jnp.min(by_block, axis=(0, 2)) // BLOCK]
  transfers between devices with their start and end apart: 32 -> 40, of which waited for: 16 -> 14; matrix products, arithmetic and copies ran while one was open for 11% -> 0% of each run, Pallas kernels for 0% -> 3%
where the time goes in v2:
time: 99.7 us; the launch traced here: 99.5 us
  starting transfers between devices  55.1 us (55%)
  Pallas kernels  29.4 us (29%)
  waiting for transfers between devices  14 us (14%)
    ppermute x30, starting transfers between devices, swapped(): lax.ppermute(value, AXES, [(source, source ^ mask) for source in range(co...  31.8 us
    pallas_call x8, Pallas kernels, call(): pl.pallas_call(body, out_shape=outs, in_specs=[HERE if i in here else VM...  29.4 us
    ppermute x10, starting transfers between devices, shifted(): lax.ppermute(value, AXES, [(source, (source + steps) % count) for source...  23.3 us
    ppermute x30, waiting for transfers between devices, swapped(): lax.ppermute(value, AXES, [(source, source ^ mask) for source in range(co...  10.8 us
    ppermute x10, waiting for transfers between devices, shifted(): lax.ppermute(value, AXES, [(source, (source + steps) % count) for source...  3.25 us
  transfers between devices with their start and end apart: 40, of which 14 were waited for; matrix products, arithmetic and copies ran while one was open for 0% of the time, Pallas kernels for 3%

profile of v2, /device:TPU:0, one launch (start us, length us, event | category | flops | bytes accessed | tf_op | source)
XLA Modules:
  0.0 99.5 jit_solution(17918999691845376499)
XLA Ops:
  0.6 0.9 shard_map.229
  1.6 5.5 %collective-permute-start.1 = (bf16[80,128]{1,0:T(8,128)(2,1)S(1)}, bf16[80,128]{1,0:T(8,128)(2,1)S(1)}, u32[]{:S(2)}, u32[]{:S(2)}) collective-permute-start(bf16[80,128]{1,0:T(8,128)(2,1)S(1)} %get-tuple-element.47), channel_id=1, source_target_pairs={{0,15},{1,0},{2,1},{3,2},{4,3},{5,4},{6,5},{7,6},{8,7},{9,8},{10,9... | collective-permute-start | bytes 61448 | tf_op jit(solution)/shard_map/ppermute | solution.py:22
  7.1 2.7 %shard_map.230 = (bf16[576,128]{1,0:T(8,128)(2,1)S(1)}, bf16[1152,128]{1,0:T(8,128)(2,1)S(1)}, bf16[1152,256]{1,0:T(8,128)(2,1)S(1)}, bf16[2304,256]{1,0:T(8,128...) custom-call(bf16[80,128]{1,0:T(8,128)(2,1)S(1)} %get-tuple-element.4, ...), custom_call_target="tpu_custom_call" | custom-call | bytes 8388608 | tf_op jit(solution)/shard_map/pallas_call | solution.py:252
  9.8 3.2 %collective-permute-done.left = bf16[80,128]{1,0:T(8,128)(2,1)S(1)} collective-permute-done((bf16[80,128]{1,0:T(8,128)(2,1)S(1)}, bf16[80,128]{1,0:T(8,128)(2,1)S(1)}, u32[]{:S(2)}, u32[]{:S(2)}) %collective-permute-start) | collective-permute-done | bytes 20512 | tf_op jit(solution)/shard_map/ppermute | solution.py:22
  13.0 7.7 %shard_map.231 = (f32[2048,128]{1,0:T(8,128)S(1)}, f32[2,128]{1,0:T(2,128)S(1)}, f32[64,128]{1,0:T(8,128)S(1)}, f32[64,128]{1,0:T(8,128)S(1)}, f32[2,128]{1,0:T(2,128)S(1)}) custom-call(bf16[2048,64]{1,0:T(8,128)(2,1)S(1)} %get-tuple-element.46.feat, bf16[80,128]{1,0:T(8,128)(2,1)S(1)} %collective-permute-done.left, ...), custom_call_target="tpu_custom_call" | custom-call | tf_op jit(solution)/shard_map/pallas_call | solution.py:252
  20.7 0.1 collective-permute-start.6
  20.8 0.1 collective-permute-start.5
  20.8 1.8 %collective-permute-start.4 = (f32[2,128]{1,0:T(2,128)S(1)}, f32[2,128]{1,0:T(2,128)S(1)}, u32[]{:S(2)}, u32[]{:S(2)}) collective-permute-start(f32[2,128]{1,0:T(2,128)S(1)} %get-tuple-element.57), channel_id=1, source_target_pairs={{0,1},{1,0},{2,3},{3,2},{4,5},{5,4},{6,7},{7,6},{8,9},{9,8},{10,11... | collective-permute-start | bytes 3080 | tf_op jit(solution)/shard_map/ppermute | solution.py:27
  22.6 0.0 collective-permute-start.2
  22.6 4.4 %collective-permute-start.3 = (f32[64,128]{1,0:T(8,128)S(1)}, f32[64,128]{1,0:T(8,128)S(1)}, u32[]{:S(2)}, u32[]{:S(2)}) collective-permute-start(f32[64,128]{1,0:T(8,128)S(1)} %get-tuple-element.52), channel_id=1, source_target_pairs={{0,15},{1,0},{2,1},{3,2},{4,3},{5,4},{6,5},{7,6},{8,7},{9,8},{10,9... | collective-permute-start | bytes 98312 | tf_op jit(solution)/shard_map/ppermute | solution.py:22
  27.1 0.0 collective-permute-done.6
  27.1 0.0 collective-permute-done.5
  27.1 0.0 collective-permute-done.4
  27.1 0.1 collective-permute-start.9
  27.2 0.1 collective-permute-start.8
  27.3 4.3 %collective-permute-start.7 = (f32[2,128]{1,0:T(2,128)S(1)}, f32[2,128]{1,0:T(2,128)S(1)}, u32[]{:S(2)}, u32[]{:S(2)}) collective-permute-start(f32[2,128]{1,0:T(2,128)S(1)} %pad_maximum_fusion.3.refs_8_), channel_id=1, source_target_pairs={{0,4},{1,5},{2,6},{3,7},{4,0},{5,1},{6,2},{7,3},{8,12},{9,13},{10,... | collective-permute-start | bytes 3080 | tf_op jit(solution)/shard_map/ppermute | solution.py:27
  31.6 1.0 collective-permute-done.9.refs_11_
  32.5 0.0 collective-permute-done.8.refs_10_
  32.5 0.6 collective-permute-done.7.refs_9_
  33.1 8.6 %shard_map.232 = (f32[2048,128]{1,0:T(8,128)S(1)}, f32[2,128]{1,0:T(2,128)S(1)}, f32[128,128]{1,0:T(8,128)S(1)}, f32[128,128]{1,0:T(8,128)S(1)}) custom-call(f32[2048,128]{1,0:T(8,128)S(1)} %get-tuple-element.50.refs_0_, f32[64,128]{1,0:T(8,128)S(1)} %collective-permute-done.2.refs_1_, f32[64,128]{1,0:T(8,128)S(1)} %collective-permute-done.3.refs_2_, ...), custom_call_target="tpu_custom_call" | custom-call | tf_op jit(solution)/shard_map/pallas_call | solution.py:252
  41.7 0.1 collective-permute-start.14
  41.8 0.1 collective-permute-start.13
  41.9 1.8 %collective-permute-start.12 = (f32[2,128]{1,0:T(2,128)S(1)}, f32[2,128]{1,0:T(2,128)S(1)}, u32[]{:S(2)}, u32[]{:S(2)}) collective-permute-start(f32[2,128]{1,0:T(2,128)S(1)} %get-tuple-element.65), channel_id=1, source_target_pairs={{0,1},{1,0},{2,3},{3,2},{4,5},{5,4},{6,7},{7,6},{8,9},{9,8},{10,11... | collective-permute-start | bytes 3080 | tf_op jit(solution)/shard_map/ppermute | solution.py:27
  43.6 4.4 %collective-permute-start.11 = (f32[128,128]{1,0:T(8,128)S(1)}, f32[128,128]{1,0:T(8,128)S(1)}, u32[]{:S(2)}, u32[]{:S(2)}) collective-permute-start(f32[128,128]{1,0:T(8,128)S(1)} %get-tuple-element.60), channel_id=1, source_target_pairs={{0,15},{1,0},{2,1},{3,2},{4,3},{5,4},{6,5},{7,6},{8,7},{9,8},{10,9... | collective-permute-start | bytes 196616 | tf_op jit(solution)/shard_map/ppermute | solution.py:22
  48.1 0.0 collective-permute-done.14
  48.1 0.0 collective-permute-done.13
  48.1 0.6 collective-permute-start.17
  48.8 1.1 %collective-permute-start.16 = (f32[2,128]{1,0:T(2,128)S(1)}, f32[2,128]{1,0:T(2,128)S(1)}, u32[]{:S(2)}, u32[]{:S(2)}) collective-permute-start(f32[2,128]{1,0:T(2,128)S(1)} %pad_maximum_fusion.4.refs_8_), channel_id=1, source_target_pairs={{0,8},{1,9},{2,10},{3,11},{4,12},{5,13},{6,14},{7,15},{8,0},{9,1},... | collective-permute-start | bytes 3080 | tf_op jit(solution)/shard_map/ppermute | solution.py:27
  49.9 2.7 %collective-permute-start.15 = (f32[2,128]{1,0:T(2,128)S(1)}, f32[2,128]{1,0:T(2,128)S(1)}, u32[]{:S(2)}, u32[]{:S(2)}) collective-permute-start(f32[2,128]{1,0:T(2,128)S(1)} %pad_maximum_fusion.4.refs_8_), channel_id=1, source_target_pairs={{0,4},{1,5},{2,6},{3,7},{4,0},{5,1},{6,2},{7,3},{8,12},{9,13},{10,... | collective-permute-start | bytes 3080 | tf_op jit(solution)/shard_map/ppermute | solution.py:27
  52.6 1.0 collective-permute-done.17.refs_11_
  53.6 0.0 collective-permute-done.16.refs_10_
  53.6 0.6 collective-permute-done.15.refs_9_
  54.1 4.5 %shard_map.233 = (bf16[2048,128]{1,0:T(8,128)(2,1)}, f32[512,256]{1,0:T(8,128)S(1)}, f32[2,256]{1,0:T(2,128)S(1)}, f32[32,256]{1,0:T(8,128)S(1)}, f32[32,256]{1,0:T(8,128)S(1)}) custom-call(f32[2048,128]{1,0:T(8,128)S(1)} %get-tuple-element.58.refs_0_, f32[128,128]{1,0:T(8,128)S(1)} %collective-permute-done.10.refs_1_, ...), custom_call_target="tpu_custom_call" | custom-call | tf_op jit(solution)/shard_map/pallas_call | solution.py:252
  58.6 0.0 collective-permute-start.22
  58.7 1.9 %collective-permute-start.20 = (f32[2,256]{1,0:T(2,128)S(1)}, f32[2,256]{1,0:T(2,128)S(1)}, u32[]{:S(2)}, u32[]{:S(2)}) collective-permute-start(f32[2,256]{1,0:T(2,128)S(1)} %get-tuple-element.73), channel_id=1, source_target_pairs={{0,1},{1,0},{2,3},{3,2},{4,5},{5,4},{6,7},{7,6},{8,9},{9,8},{10,11... | collective-permute-start | bytes 6152 | tf_op jit(solution)/shard_map/ppermute | solution.py:27
  60.5 4.4 %collective-permute-start.19 = (f32[32,256]{1,0:T(8,128)S(1)}, f32[32,256]{1,0:T(8,128)S(1)}, u32[]{:S(2)}, u32[]{:S(2)}) collective-permute-start(f32[32,256]{1,0:T(8,128)S(1)} %get-tuple-element.69), channel_id=1, source_target_pairs={{0,15},{1,0},{2,1},{3,2},{4,3},{5,4},{6,5},{7,6},{8,7},{9,8},{10,9... | collective-permute-start | bytes 98312 | tf_op jit(solution)/shard_map/ppermute | solution.py:22
  65.0 0.6 collective-permute-start.25
  65.6 1.1 %collective-permute-start.24 = (f32[2,256]{1,0:T(2,128)S(1)}, f32[2,256]{1,0:T(2,128)S(1)}, u32[]{:S(2)}, u32[]{:S(2)}) collective-permute-start(f32[2,256]{1,0:T(2,128)S(1)} %pad_maximum_fusion.1.refs_8_), channel_id=1, source_target_pairs={{0,8},{1,9},{2,10},{3,11},{4,12},{5,13},{6,14},{7,15},{8,0},{9,1},... | collective-permute-start | bytes 6152 | tf_op jit(solution)/shard_map/ppermute | solution.py:27
  66.7 2.7 %collective-permute-start.23 = (f32[2,256]{1,0:T(2,128)S(1)}, f32[2,256]{1,0:T(2,128)S(1)}, u32[]{:S(2)}, u32[]{:S(2)}) collective-permute-start(f32[2,256]{1,0:T(2,128)S(1)} %pad_maximum_fusion.1.refs_8_), channel_id=1, source_target_pairs={{0,4},{1,5},{2,6},{3,7},{4,0},{5,1},{6,2},{7,3},{8,12},{9,13},{10,... | collective-permute-start | bytes 6152 | tf_op jit(solution)/shard_map/ppermute | solution.py:27
  69.5 1.0 collective-permute-done.25.refs_11_
  70.5 0.6 collective-permute-done.23.refs_9_
  71.0 2.7 %shard_map.234 = (f32[512,256]{1,0:T(8,128)S(1)}, f32[2,256]{1,0:T(2,128)S(1)}, f32[64,256]{1,0:T(8,128)S(1)}, f32[64,256]{1,0:T(8,128)S(1)}) custom-call(f32[512,256]{1,0:T(8,128)S(1)} %get-tuple-element.67.refs_0_, f32[32,256]{1,0:T(8,128)S(1)} %collective-permute-done.18.refs_1_, f32[32,256]{1,0:T(8,128)S(1)} %collective-permute-done.19.refs_2_, ...), custom_call_target="tpu_custom_call" | custom-call | tf_op jit(solution)/shard_map/pallas_call | solution.py:252
  73.7 0.1 collective-permute-start.30
  73.8 0.1 collective-permute-start.29
  73.9 1.8 %collective-permute-start.28 = (f32[2,256]{1,0:T(2,128)S(1)}, f32[2,256]{1,0:T(2,128)S(1)}, u32[]{:S(2)}, u32[]{:S(2)}) collective-permute-start(f32[2,256]{1,0:T(2,128)S(1)} %get-tuple-element.81), channel_id=1, source_target_pairs={{0,1},{1,0},{2,3},{3,2},{4,5},{5,4},{6,7},{7,6},{8,9},{9,8},{10,11... | collective-permute-start | bytes 6152 | tf_op jit(solution)/shard_map/ppermute | solution.py:27
  75.7 4.4 %collective-permute-start.27 = (f32[64,256]{1,0:T(8,128)S(1)}, f32[64,256]{1,0:T(8,128)S(1)}, u32[]{:S(2)}, u32[]{:S(2)}) collective-permute-start(f32[64,256]{1,0:T(8,128)S(1)} %get-tuple-element.76), channel_id=1, source_target_pairs={{0,15},{1,0},{2,1},{3,2},{4,3},{5,4},{6,5},{7,6},{8,7},{9,8},{10,9... | collective-permute-start | bytes 196616 | tf_op jit(solution)/shard_map/ppermute | solution.py:22
  80.2 0.6 collective-permute-start.33
  80.8 1.1 %collective-permute-start.32 = (f32[2,256]{1,0:T(2,128)S(1)}, f32[2,256]{1,0:T(2,128)S(1)}, u32[]{:S(2)}, u32[]{:S(2)}) collective-permute-start(f32[2,256]{1,0:T(2,128)S(1)} %pad_maximum_fusion.2.refs_8_), channel_id=1, source_target_pairs={{0,8},{1,9},{2,10},{3,11},{4,12},{5,13},{6,14},{7,15},{8,0},{9,1},... | collective-permute-start | bytes 6152 | tf_op jit(solution)/shard_map/ppermute | solution.py:27
  81.9 2.7 %collective-permute-start.31 = (f32[2,256]{1,0:T(2,128)S(1)}, f32[2,256]{1,0:T(2,128)S(1)}, u32[]{:S(2)}, u32[]{:S(2)}) collective-permute-start(f32[2,256]{1,0:T(2,128)S(1)} %pad_maximum_fusion.2.refs_8_), channel_id=1, source_target_pairs={{0,4},{1,5},{2,6},{3,7},{4,0},{5,1},{6,2},{7,3},{8,12},{9,13},{10,... | collective-permute-start | bytes 6152 | tf_op jit(solution)/shard_map/ppermute | solution.py:27
  84.6 1.0 collective-permute-done.33.refs_11_
  85.6 0.6 collective-permute-done.31.refs_9_
  86.2 1.6 %shard_map.235 = (bf16[512,256]{1,0:T(8,128)(2,1)}, f32[128,512]{1,0:T(8,128)S(1)}, f32[2,512]{1,0:T(2,128)S(1)}) custom-call(f32[512,256]{1,0:T(8,128)S(1)} %get-tuple-element.74.refs_0_, f32[64,256]{1,0:T(8,128)S(1)} %collective-permute-done.26.refs_1_, f32[64,256]{1,0:T(8,128)S(1)} %collective-permute-done.27.refs_2_, ...), custom_call_target="tpu_custom_call" | custom-call | tf_op jit(solution)/shard_map/pallas_call | solution.py:252
  87.8 0.1 collective-permute-start.36
  87.9 0.1 collective-permute-start.35
  88.0 1.8 %collective-permute-start.34 = (f32[2,512]{1,0:T(2,128)S(1)}, f32[2,512]{1,0:T(2,128)S(1)}, u32[]{:S(2)}, u32[]{:S(2)}) collective-permute-start(f32[2,512]{1,0:T(2,128)S(1)} %get-tuple-element.86), channel_id=1, source_target_pairs={{0,1},{1,0},{2,3},{3,2},{4,5},{5,4},{6,7},{7,6},{8,9},{9,8},{10,11... | collective-permute-start | bytes 12296 | tf_op jit(solution)/shard_map/ppermute | solution.py:27
  89.7 1.2 %collective-permute-done.36 = f32[2,512]{1,0:T(2,128)S(1)} collective-permute-done((f32[2,512]{1,0:T(2,128)S(1)}, f32[2,512]{1,0:T(2,128)S(1)}, u32[]{:S(2)}, u32[]{:S(2)}) %collective-permute-start.36) | collective-permute-done | bytes 4128 | tf_op jit(solution)/shard_map/ppermute | solution.py:27
  90.9 0.7 collective-permute-done.35
  91.6 2.4 %collective-permute-start.39 = (f32[2,512]{1,0:T(2,128)S(1)}, f32[2,512]{1,0:T(2,128)S(1)}, u32[]{:S(2)}, u32[]{:S(2)}) collective-permute-start(f32[2,512]{1,0:T(2,128)S(1)} %pad_maximum_fusion.refs_3_), channel_id=1, source_target_pairs={{0,12},{1,13},{2,14},{3,15},{4,8},{5,9},{6,10},{7,11},{8,4},{9,5},... | collective-permute-start | bytes 12296 | tf_op jit(solution)/shard_map/ppermute | solution.py:27
  94.0 1.1 %collective-permute-start.38 = (f32[2,512]{1,0:T(2,128)S(1)}, f32[2,512]{1,0:T(2,128)S(1)}, u32[]{:S(2)}, u32[]{:S(2)}) collective-permute-start(f32[2,512]{1,0:T(2,128)S(1)} %pad_maximum_fusion.refs_3_), channel_id=1, source_target_pairs={{0,8},{1,9},{2,10},{3,11},{4,12},{5,13},{6,14},{7,15},{8,0},{9,1},... | collective-permute-start | bytes 12296 | tf_op jit(solution)/shard_map/ppermute | solution.py:27
  95.1 0.9 collective-permute-start.37
  96.0 1.0 %collective-permute-done.39.refs_6_ = f32[2,512]{1,0:T(2,128)S(1)} collective-permute-done((f32[2,512]{1,0:T(2,128)S(1)}, f32[2,512]{1,0:T(2,128)S(1)}, u32[]{:S(2)}, u32[]{:S(2)}) %collective-permute-start.39) | collective-permute-done | bytes 4128 | tf_op jit(solution)/shard_map/ppermute | solution.py:27
  97.1 1.5 %collective-permute-done.38.refs_5_ = f32[2,512]{1,0:T(2,128)S(1)} collective-permute-done((f32[2,512]{1,0:T(2,128)S(1)}, f32[2,512]{1,0:T(2,128)S(1)}, u32[]{:S(2)}, u32[]{:S(2)}) %collective-permute-start.38) | collective-permute-done | bytes 4128 | tf_op jit(solution)/shard_map/ppermute | solution.py:27
  98.5 0.2 collective-permute-done.37.refs_4_
  98.8 0.8 shard_map.236
  (34 shorter events, 0.2 us)
Async XLA Ops:
  1.6 8.2 %collective-permute-start.1 = (bf16[80,128]{1,0:T(8,128)(2,1)S(1)}, bf16[80,128]{1,0:T(8,128)(2,1)S(1)}, u32[]{:S(2)}, u32[]{:S(2)}) collective-permute-start(bf16[80,128]{1,0:T(8,128)(2,1)S(1)} %get-tuple-element.47), channel_id=1, source_target_pairs={{0,15},{1,0},{2,1},{3,2},{4,3},{5,4},{6,5},{7,6},{8,7},{9,8},{10,9... | collective-permute-start | bytes 61448 | tf_op jit(solution)/shard_map/ppermute | solution.py:22
  7.1 5.9 %collective-permute-start = (bf16[80,128]{1,0:T(8,128)(2,1)S(1)}, bf16[80,128]{1,0:T(8,128)(2,1)S(1)}, u32[]{:S(2)}, u32[]{:S(2)}) collective-permute-start(bf16[80,128]{1,0:T(8,128)(2,1)S(1)} %get-tuple-element.45.refs_0_), channel_id=1, source_target_pairs={{0,1},{1,2},{2,3},{3,4},{4,5},{5,6},{6,7},{7,8},{8,9},{9,10},{10,1... | collective-permute-start | bytes 61448 | tf_op jit(solution)/shard_map/ppermute | solution.py:22
  20.7 6.4 %collective-permute-start.6 = (f32[2,128]{1,0:T(2,128)S(1)}, f32[2,128]{1,0:T(2,128)S(1)}, u32[]{:S(2)}, u32[]{:S(2)}) collective-permute-start(f32[2,128]{1,0:T(2,128)S(1)} %get-tuple-element.57), channel_id=1, source_target_pairs={{0,3},{1,2},{2,1},{3,0},{4,7},{5,6},{6,5},{7,4},{8,11},{9,10},{10,... | collective-permute-start | bytes 3080 | tf_op jit(solution)/shard_map/ppermute | solution.py:27
  20.8 6.3 %collective-permute-start.5 = (f32[2,128]{1,0:T(2,128)S(1)}, f32[2,128]{1,0:T(2,128)S(1)}, u32[]{:S(2)}, u32[]{:S(2)}) collective-permute-start(f32[2,128]{1,0:T(2,128)S(1)} %get-tuple-element.57), channel_id=1, source_target_pairs={{0,2},{1,3},{2,0},{3,1},{4,6},{5,7},{6,4},{7,5},{8,10},{9,11},{10,... | collective-permute-start | bytes 3080 | tf_op jit(solution)/shard_map/ppermute | solution.py:27
  20.8 6.2 %collective-permute-start.4 = (f32[2,128]{1,0:T(2,128)S(1)}, f32[2,128]{1,0:T(2,128)S(1)}, u32[]{:S(2)}, u32[]{:S(2)}) collective-permute-start(f32[2,128]{1,0:T(2,128)S(1)} %get-tuple-element.57), channel_id=1, source_target_pairs={{0,1},{1,0},{2,3},{3,2},{4,5},{5,4},{6,7},{7,6},{8,9},{9,8},{10,11... | collective-permute-start | bytes 3080 | tf_op jit(solution)/shard_map/ppermute | solution.py:27
  22.6 10.5 %collective-permute-start.2 = (f32[64,128]{1,0:T(8,128)S(1)}, f32[64,128]{1,0:T(8,128)S(1)}, u32[]{:S(2)}, u32[]{:S(2)}) collective-permute-start(f32[64,128]{1,0:T(8,128)S(1)} %get-tuple-element.51), channel_id=1, source_target_pairs={{0,1},{1,2},{2,3},{3,4},{4,5},{5,6},{6,7},{7,8},{8,9},{9,10},{10,1... | collective-permute-start | bytes 98312 | tf_op jit(solution)/shard_map/ppermute | solution.py:22
  22.6 10.5 %collective-permute-start.3 = (f32[64,128]{1,0:T(8,128)S(1)}, f32[64,128]{1,0:T(8,128)S(1)}, u32[]{:S(2)}, u32[]{:S(2)}) collective-permute-start(f32[64,128]{1,0:T(8,128)S(1)} %get-tuple-element.52), channel_id=1, source_target_pairs={{0,15},{1,0},{2,1},{3,2},{4,3},{5,4},{6,5},{7,6},{8,7},{9,8},{10,9... | collective-permute-start | bytes 98312 | tf_op jit(solution)/shard_map/ppermute | solution.py:22
  27.1 5.4 %collective-permute-start.9 = (f32[2,128]{1,0:T(2,128)S(1)}, f32[2,128]{1,0:T(2,128)S(1)}, u32[]{:S(2)}, u32[]{:S(2)}) collective-permute-start(f32[2,128]{1,0:T(2,128)S(1)} %pad_maximum_fusion.3.refs_8_), channel_id=1, source_target_pairs={{0,12},{1,13},{2,14},{3,15},{4,8},{5,9},{6,10},{7,11},{8,4},{9,5},... | collective-permute-start | bytes 3080 | tf_op jit(solution)/shard_map/ppermute | solution.py:27
  27.2 5.4 %collective-permute-start.8 = (f32[2,128]{1,0:T(2,128)S(1)}, f32[2,128]{1,0:T(2,128)S(1)}, u32[]{:S(2)}, u32[]{:S(2)}) collective-permute-start(f32[2,128]{1,0:T(2,128)S(1)} %pad_maximum_fusion.3.refs_8_), channel_id=1, source_target_pairs={{0,8},{1,9},{2,10},{3,11},{4,12},{5,13},{6,14},{7,15},{8,0},{9,1},... | collective-permute-start | bytes 3080 | tf_op jit(solution)/shard_map/ppermute | solution.py:27
  27.3 5.8 %collective-permute-start.7 = (f32[2,128]{1,0:T(2,128)S(1)}, f32[2,128]{1,0:T(2,128)S(1)}, u32[]{:S(2)}, u32[]{:S(2)}) collective-permute-start(f32[2,128]{1,0:T(2,128)S(1)} %pad_maximum_fusion.3.refs_8_), channel_id=1, source_target_pairs={{0,4},{1,5},{2,6},{3,7},{4,0},{5,1},{6,2},{7,3},{8,12},{9,13},{10,... | collective-permute-start | bytes 3080 | tf_op jit(solution)/shard_map/ppermute | solution.py:27
  41.7 6.4 %collective-permute-start.14 = (f32[2,128]{1,0:T(2,128)S(1)}, f32[2,128]{1,0:T(2,128)S(1)}, u32[]{:S(2)}, u32[]{:S(2)}) collective-permute-start(f32[2,128]{1,0:T(2,128)S(1)} %get-tuple-element.65), channel_id=1, source_target_pairs={{0,3},{1,2},{2,1},{3,0},{4,7},{5,6},{6,5},{7,4},{8,11},{9,10},{10,... | collective-permute-start | bytes 3080 | tf_op jit(solution)/shard_map/ppermute | solution.py:27
  41.8 6.3 %collective-permute-start.13 = (f32[2,128]{1,0:T(2,128)S(1)}, f32[2,128]{1,0:T(2,128)S(1)}, u32[]{:S(2)}, u32[]{:S(2)}) collective-permute-start(f32[2,128]{1,0:T(2,128)S(1)} %get-tuple-element.65), channel_id=1, source_target_pairs={{0,2},{1,3},{2,0},{3,1},{4,6},{5,7},{6,4},{7,5},{8,10},{9,11},{10,... | collective-permute-start | bytes 3080 | tf_op jit(solution)/shard_map/ppermute | solution.py:27
  41.9 6.2 %collective-permute-start.12 = (f32[2,128]{1,0:T(2,128)S(1)}, f32[2,128]{1,0:T(2,128)S(1)}, u32[]{:S(2)}, u32[]{:S(2)}) collective-permute-start(f32[2,128]{1,0:T(2,128)S(1)} %get-tuple-element.65), channel_id=1, source_target_pairs={{0,1},{1,0},{2,3},{3,2},{4,5},{5,4},{6,7},{7,6},{8,9},{9,8},{10,11... | collective-permute-start | bytes 3080 | tf_op jit(solution)/shard_map/ppermute | solution.py:27
  43.6 10.5 %collective-permute-start.10 = (f32[128,128]{1,0:T(8,128)S(1)}, f32[128,128]{1,0:T(8,128)S(1)}, u32[]{:S(2)}, u32[]{:S(2)}) collective-permute-start(f32[128,128]{1,0:T(8,128)S(1)} %get-tuple-element.59), channel_id=1, source_target_pairs={{0,1},{1,2},{2,3},{3,4},{4,5},{5,6},{6,7},{7,8},{8,9},{9,10},{10,1... | collective-permute-start | bytes 196616 | tf_op jit(solution)/shard_map/ppermute | solution.py:22
  43.6 10.5 %collective-permute-start.11 = (f32[128,128]{1,0:T(8,128)S(1)}, f32[128,128]{1,0:T(8,128)S(1)}, u32[]{:S(2)}, u32[]{:S(2)}) collective-permute-start(f32[128,128]{1,0:T(8,128)S(1)} %get-tuple-element.60), channel_id=1, source_target_pairs={{0,15},{1,0},{2,1},{3,2},{4,3},{5,4},{6,5},{7,6},{8,7},{9,8},{10,9... | collective-permute-start | bytes 196616 | tf_op jit(solution)/shard_map/ppermute | solution.py:22
  48.1 5.4 %collective-permute-start.17 = (f32[2,128]{1,0:T(2,128)S(1)}, f32[2,128]{1,0:T(2,128)S(1)}, u32[]{:S(2)}, u32[]{:S(2)}) collective-permute-start(f32[2,128]{1,0:T(2,128)S(1)} %pad_maximum_fusion.4.refs_8_), channel_id=1, source_target_pairs={{0,12},{1,13},{2,14},{3,15},{4,8},{5,9},{6,10},{7,11},{8,4},{9,5},... | collective-permute-start | bytes 3080 | tf_op jit(solution)/shard_map/ppermute | solution.py:27
  48.8 4.8 %collective-permute-start.16 = (f32[2,128]{1,0:T(2,128)S(1)}, f32[2,128]{1,0:T(2,128)S(1)}, u32[]{:S(2)}, u32[]{:S(2)}) collective-permute-start(f32[2,128]{1,0:T(2,128)S(1)} %pad_maximum_fusion.4.refs_8_), channel_id=1, source_target_pairs={{0,8},{1,9},{2,10},{3,11},{4,12},{5,13},{6,14},{7,15},{8,0},{9,1},... | collective-permute-start | bytes 3080 | tf_op jit(solution)/shard_map/ppermute | solution.py:27
  49.9 4.2 %collective-permute-start.15 = (f32[2,128]{1,0:T(2,128)S(1)}, f32[2,128]{1,0:T(2,128)S(1)}, u32[]{:S(2)}, u32[]{:S(2)}) collective-permute-start(f32[2,128]{1,0:T(2,128)S(1)} %pad_maximum_fusion.4.refs_8_), channel_id=1, source_target_pairs={{0,4},{1,5},{2,6},{3,7},{4,0},{5,1},{6,2},{7,3},{8,12},{9,13},{10,... | collective-permute-start | bytes 3080 | tf_op jit(solution)/shard_map/ppermute | solution.py:27
  58.6 6.3 %collective-permute-start.22 = (f32[2,256]{1,0:T(2,128)S(1)}, f32[2,256]{1,0:T(2,128)S(1)}, u32[]{:S(2)}, u32[]{:S(2)}) collective-permute-start(f32[2,256]{1,0:T(2,128)S(1)} %get-tuple-element.73), channel_id=1, source_target_pairs={{0,3},{1,2},{2,1},{3,0},{4,7},{5,6},{6,5},{7,4},{8,11},{9,10},{10,... | collective-permute-start | bytes 6152 | tf_op jit(solution)/shard_map/ppermute | solution.py:27
  58.7 6.3 %collective-permute-start.21 = (f32[2,256]{1,0:T(2,128)S(1)}, f32[2,256]{1,0:T(2,128)S(1)}, u32[]{:S(2)}, u32[]{:S(2)}) collective-permute-start(f32[2,256]{1,0:T(2,128)S(1)} %get-tuple-element.73), channel_id=1, source_target_pairs={{0,2},{1,3},{2,0},{3,1},{4,6},{5,7},{6,4},{7,5},{8,10},{9,11},{10,... | collective-permute-start | bytes 6152 | tf_op jit(solution)/shard_map/ppermute | solution.py:27
  58.7 6.3 %collective-permute-start.20 = (f32[2,256]{1,0:T(2,128)S(1)}, f32[2,256]{1,0:T(2,128)S(1)}, u32[]{:S(2)}, u32[]{:S(2)}) collective-permute-start(f32[2,256]{1,0:T(2,128)S(1)} %get-tuple-element.73), channel_id=1, source_target_pairs={{0,1},{1,0},{2,3},{3,2},{4,5},{5,4},{6,7},{7,6},{8,9},{9,8},{10,11... | collective-permute-start | bytes 6152 | tf_op jit(solution)/shard_map/ppermute | solution.py:27
  60.5 10.5 %collective-permute-start.18 = (f32[32,256]{1,0:T(8,128)S(1)}, f32[32,256]{1,0:T(8,128)S(1)}, u32[]{:S(2)}, u32[]{:S(2)}) collective-permute-start(f32[32,256]{1,0:T(8,128)S(1)} %get-tuple-element.68), channel_id=1, source_target_pairs={{0,1},{1,2},{2,3},{3,4},{4,5},{5,6},{6,7},{7,8},{8,9},{9,10},{10,1... | collective-permute-start | bytes 98312 | tf_op jit(solution)/shard_map/ppermute | solution.py:22
  60.5 10.5 %collective-permute-start.19 = (f32[32,256]{1,0:T(8,128)S(1)}, f32[32,256]{1,0:T(8,128)S(1)}, u32[]{:S(2)}, u32[]{:S(2)}) collective-permute-start(f32[32,256]{1,0:T(8,128)S(1)} %get-tuple-element.69), channel_id=1, source_target_pairs={{0,15},{1,0},{2,1},{3,2},{4,3},{5,4},{6,5},{7,6},{8,7},{9,8},{10,9... | collective-permute-start | bytes 98312 | tf_op jit(solution)/shard_map/ppermute | solution.py:22
  65.0 5.4 %collective-permute-start.25 = (f32[2,256]{1,0:T(2,128)S(1)}, f32[2,256]{1,0:T(2,128)S(1)}, u32[]{:S(2)}, u32[]{:S(2)}) collective-permute-start(f32[2,256]{1,0:T(2,128)S(1)} %pad_maximum_fusion.1.refs_8_), channel_id=1, source_target_pairs={{0,12},{1,13},{2,14},{3,15},{4,8},{5,9},{6,10},{7,11},{8,4},{9,5},... | collective-permute-start | bytes 6152 | tf_op jit(solution)/shard_map/ppermute | solution.py:27
  65.6 4.8 %collective-permute-start.24 = (f32[2,256]{1,0:T(2,128)S(1)}, f32[2,256]{1,0:T(2,128)S(1)}, u32[]{:S(2)}, u32[]{:S(2)}) collective-permute-start(f32[2,256]{1,0:T(2,128)S(1)} %pad_maximum_fusion.1.refs_8_), channel_id=1, source_target_pairs={{0,8},{1,9},{2,10},{3,11},{4,12},{5,13},{6,14},{7,15},{8,0},{9,1},... | collective-permute-start | bytes 6152 | tf_op jit(solution)/shard_map/ppermute | solution.py:27
  66.7 4.3 %collective-permute-start.23 = (f32[2,256]{1,0:T(2,128)S(1)}, f32[2,256]{1,0:T(2,128)S(1)}, u32[]{:S(2)}, u32[]{:S(2)}) collective-permute-start(f32[2,256]{1,0:T(2,128)S(1)} %pad_maximum_fusion.1.refs_8_), channel_id=1, source_target_pairs={{0,4},{1,5},{2,6},{3,7},{4,0},{5,1},{6,2},{7,3},{8,12},{9,13},{10,... | collective-permute-start | bytes 6152 | tf_op jit(solution)/shard_map/ppermute | solution.py:27
  73.7 6.4 %collective-permute-start.30 = (f32[2,256]{1,0:T(2,128)S(1)}, f32[2,256]{1,0:T(2,128)S(1)}, u32[]{:S(2)}, u32[]{:S(2)}) collective-permute-start(f32[2,256]{1,0:T(2,128)S(1)} %get-tuple-element.81), channel_id=1, source_target_pairs={{0,3},{1,2},{2,1},{3,0},{4,7},{5,6},{6,5},{7,4},{8,11},{9,10},{10,... | collective-permute-start | bytes 6152 | tf_op jit(solution)/shard_map/ppermute | solution.py:27
  73.8 6.3 %collective-permute-start.29 = (f32[2,256]{1,0:T(2,128)S(1)}, f32[2,256]{1,0:T(2,128)S(1)}, u32[]{:S(2)}, u32[]{:S(2)}) collective-permute-start(f32[2,256]{1,0:T(2,128)S(1)} %get-tuple-element.81), channel_id=1, source_target_pairs={{0,2},{1,3},{2,0},{3,1},{4,6},{5,7},{6,4},{7,5},{8,10},{9,11},{10,... | collective-permute-start | bytes 6152 | tf_op jit(solution)/shard_map/ppermute | solution.py:27
  73.9 6.2 %collective-permute-start.28 = (f32[2,256]{1,0:T(2,128)S(1)}, f32[2,256]{1,0:T(2,128)S(1)}, u32[]{:S(2)}, u32[]{:S(2)}) collective-permute-start(f32[2,256]{1,0:T(2,128)S(1)} %get-tuple-element.81), channel_id=1, source_target_pairs={{0,1},{1,0},{2,3},{3,2},{4,5},{5,4},{6,7},{7,6},{8,9},{9,8},{10,11... | collective-permute-start | bytes 6152 | tf_op jit(solution)/shard_map/ppermute | solution.py:27
  75.7 10.5 %collective-permute-start.26 = (f32[64,256]{1,0:T(8,128)S(1)}, f32[64,256]{1,0:T(8,128)S(1)}, u32[]{:S(2)}, u32[]{:S(2)}) collective-permute-start(f32[64,256]{1,0:T(8,128)S(1)} %get-tuple-element.75), channel_id=1, source_target_pairs={{0,1},{1,2},{2,3},{3,4},{4,5},{5,6},{6,7},{7,8},{8,9},{9,10},{10,1... | collective-permute-start | bytes 196616 | tf_op jit(solution)/shard_map/ppermute | solution.py:22
  75.7 10.5 %collective-permute-start.27 = (f32[64,256]{1,0:T(8,128)S(1)}, f32[64,256]{1,0:T(8,128)S(1)}, u32[]{:S(2)}, u32[]{:S(2)}) collective-permute-start(f32[64,256]{1,0:T(8,128)S(1)} %get-tuple-element.76), channel_id=1, source_target_pairs={{0,15},{1,0},{2,1},{3,2},{4,3},{5,4},{6,5},{7,6},{8,7},{9,8},{10,9... | collective-permute-start | bytes 196616 | tf_op jit(solution)/shard_map/ppermute | solution.py:22
  80.2 5.4 %collective-permute-start.33 = (f32[2,256]{1,0:T(2,128)S(1)}, f32[2,256]{1,0:T(2,128)S(1)}, u32[]{:S(2)}, u32[]{:S(2)}) collective-permute-start(f32[2,256]{1,0:T(2,128)S(1)} %pad_maximum_fusion.2.refs_8_), channel_id=1, source_target_pairs={{0,12},{1,13},{2,14},{3,15},{4,8},{5,9},{6,10},{7,11},{8,4},{9,5},... | collective-permute-start | bytes 6152 | tf_op jit(solution)/shard_map/ppermute | solution.py:27
  80.8 4.8 %collective-permute-start.32 = (f32[2,256]{1,0:T(2,128)S(1)}, f32[2,256]{1,0:T(2,128)S(1)}, u32[]{:S(2)}, u32[]{:S(2)}) collective-permute-start(f32[2,256]{1,0:T(2,128)S(1)} %pad_maximum_fusion.2.refs_8_), channel_id=1, source_target_pairs={{0,8},{1,9},{2,10},{3,11},{4,12},{5,13},{6,14},{7,15},{8,0},{9,1},... | collective-permute-start | bytes 6152 | tf_op jit(solution)/shard_map/ppermute | solution.py:27
  81.9 4.3 %collective-permute-start.31 = (f32[2,256]{1,0:T(2,128)S(1)}, f32[2,256]{1,0:T(2,128)S(1)}, u32[]{:S(2)}, u32[]{:S(2)}) collective-permute-start(f32[2,256]{1,0:T(2,128)S(1)} %pad_maximum_fusion.2.refs_8_), channel_id=1, source_target_pairs={{0,4},{1,5},{2,6},{3,7},{4,0},{5,1},{6,2},{7,3},{8,12},{9,13},{10,... | collective-permute-start | bytes 6152 | tf_op jit(solution)/shard_map/ppermute | solution.py:27
  87.8 3.1 %collective-permute-start.36 = (f32[2,512]{1,0:T(2,128)S(1)}, f32[2,512]{1,0:T(2,128)S(1)}, u32[]{:S(2)}, u32[]{:S(2)}) collective-permute-start(f32[2,512]{1,0:T(2,128)S(1)} %get-tuple-element.86), channel_id=1, source_target_pairs={{0,3},{1,2},{2,1},{3,0},{4,7},{5,6},{6,5},{7,4},{8,11},{9,10},{10,... | collective-permute-start | bytes 12296 | tf_op jit(solution)/shard_map/ppermute | solution.py:27
  87.9 3.7 %collective-permute-start.35 = (f32[2,512]{1,0:T(2,128)S(1)}, f32[2,512]{1,0:T(2,128)S(1)}, u32[]{:S(2)}, u32[]{:S(2)}) collective-permute-start(f32[2,512]{1,0:T(2,128)S(1)} %get-tuple-element.86), channel_id=1, source_target_pairs={{0,2},{1,3},{2,0},{3,1},{4,6},{5,7},{6,4},{7,5},{8,10},{9,11},{10,... | collective-permute-start | bytes 12296 | tf_op jit(solution)/shard_map/ppermute | solution.py:27
  88.0 3.6 %collective-permute-start.34 = (f32[2,512]{1,0:T(2,128)S(1)}, f32[2,512]{1,0:T(2,128)S(1)}, u32[]{:S(2)}, u32[]{:S(2)}) collective-permute-start(f32[2,512]{1,0:T(2,128)S(1)} %get-tuple-element.86), channel_id=1, source_target_pairs={{0,1},{1,0},{2,3},{3,2},{4,5},{5,4},{6,7},{7,6},{8,9},{9,8},{10,11... | collective-permute-start | bytes 12296 | tf_op jit(solution)/shard_map/ppermute | solution.py:27
  91.6 5.5 %collective-permute-start.39 = (f32[2,512]{1,0:T(2,128)S(1)}, f32[2,512]{1,0:T(2,128)S(1)}, u32[]{:S(2)}, u32[]{:S(2)}) collective-permute-start(f32[2,512]{1,0:T(2,128)S(1)} %pad_maximum_fusion.refs_3_), channel_id=1, source_target_pairs={{0,12},{1,13},{2,14},{3,15},{4,8},{5,9},{6,10},{7,11},{8,4},{9,5},... | collective-permute-start | bytes 12296 | tf_op jit(solution)/shard_map/ppermute | solution.py:27
  94.0 4.5 %collective-permute-start.38 = (f32[2,512]{1,0:T(2,128)S(1)}, f32[2,512]{1,0:T(2,128)S(1)}, u32[]{:S(2)}, u32[]{:S(2)}) collective-permute-start(f32[2,512]{1,0:T(2,128)S(1)} %pad_maximum_fusion.refs_3_), channel_id=1, source_target_pairs={{0,8},{1,9},{2,10},{3,11},{4,12},{5,13},{6,14},{7,15},{8,0},{9,1},... | collective-permute-start | bytes 12296 | tf_op jit(solution)/shard_map/ppermute | solution.py:27
  95.1 3.6 %collective-permute-start.37 = (f32[2,512]{1,0:T(2,128)S(1)}, f32[2,512]{1,0:T(2,128)S(1)}, u32[]{:S(2)}, u32[]{:S(2)}) collective-permute-start(f32[2,512]{1,0:T(2,128)S(1)} %pad_maximum_fusion.refs_3_), channel_id=1, source_target_pairs={{0,4},{1,5},{2,6},{3,7},{4,0},{5,1},{6,2},{7,3},{8,12},{9,13},{10,... | collective-permute-start | bytes 12296 | tf_op jit(solution)/shard_map/ppermute | solution.py:27

commit v3 on v2

--- a/solution.py
+++ b/solution.py
@@ -13,6 +13,7 @@
 WINDOW = 256
 TAPS = 9
 EPS = 1e-05
+STEP = 512
 VM = pl.BlockSpec(memory_space=pltpu.VMEM)
 HERE = pl.BlockSpec(memory_space=pltpu.HBM)
 
@@ -28,8 +29,10 @@
 
 
 def hots(near, width):
-    places = lax.broadcasted_iota(jnp.int32, (near.shape[0], width), 1)
-    return [jnp.where(near[:, tap : tap + 1] == places, 1.0, 0.0).astype(jnp.bfloat16) for tap in range(TAPS - 1)]
+    place = jnp.where((near >= 0) & (near < width), near, -1).astype(jnp.float32).astype(jnp.bfloat16)
+    places = lax.broadcasted_iota(jnp.int32, (near.shape[0], width), 1).astype(jnp.float32).astype(jnp.bfloat16)
+    one, zero = jnp.bfloat16(1), jnp.bfloat16(0)
+    return [jnp.where(place[:, tap : tap + 1] == places, one, zero) for tap in range(TAPS - 1)]
 
 
 def listed(rows, order, start):
@@ -44,53 +47,75 @@
     return jnp.dot(a, b, preferred_element_type=jnp.float32)
 
 
-def picked(sources, near, start, width):
-    hot = hots(near, width)
+def spots(links, block, rows, halo):
+    link = links[1:, pl.ds(pl.multiple_of(block * BLOCK, BLOCK), BLOCK)]
+    place = jnp.where(link < rows, link + halo, jnp.where(link < rows + halo, link - rows, link))
+    return jnp.transpose(place)
+
+
+def mark(links, halo, marks, far):
+    rows = links.shape[1]
+
+    def one(block, outside):
+        near = spots(links, block, rows, halo) - block * BLOCK
+        hot = hots(near, WINDOW)
+        for i, part in enumerate(hot[0::2] + hot[1::2]):
+            start = pl.multiple_of((block * (TAPS - 1) + i) * BLOCK, BLOCK)
+            marks[pl.ds(start, BLOCK), :] = part
+        return jnp.maximum(outside, jnp.where((near < 0) | (near >= WINDOW), 1, 0))
+
+    none = jnp.zeros((BLOCK, TAPS - 1), jnp.int32)
+    outside = lax.fori_loop(0, rows // BLOCK, one, none, unroll=min(2, rows // BLOCK))
+    far[...] = jnp.broadcast_to(jnp.max(outside, axis=0, keepdims=True), far.shape)
+
+
+def split(rows):
+    return [rows[i * BLOCK : (i + 1) * BLOCK] for i in range(rows.shape[0] // BLOCK)]
+
+
+def picked(sources, even, odd, start, width):
     if len(sources) == 1:
         window = sources[0][pl.ds(start, width), :]
-        rows = dot(jnp.concatenate(hot, axis=0), window).astype(jnp.bfloat16)
-        return [rows[i * BLOCK : (i + 1) * BLOCK] for i in range(TAPS - 1)]
-    low = dot(jnp.concatenate(hot[1::2], axis=0), sources[0][pl.ds(start, width), :])
-    high = dot(jnp.concatenate(hot[0::2], axis=0), sources[1][pl.ds(start, width), :])
-    low = [low[i * BLOCK : (i + 1) * BLOCK] for i in range(4)]
-    high = [high[i * BLOCK : (i + 1) * BLOCK] for i in range(4)]
+        first = split(dot(even, window).astype(jnp.bfloat16))
+        second = split(dot(odd, window).astype(jnp.bfloat16))
+        return [part for pair in zip(first, second) for part in pair]
+    high = split(dot(even, sources[1][pl.ds(start, width), :]))
+    low = split(dot(odd, sources[0][pl.ds(start, width), :]))
     pieces = [high[0]] + [low[i] + high[i + 1] for i in range(3)] + [low[3]]
     return [piece.astype(jnp.bfloat16) for piece in pieces]
 
 
-def convolve(sources, links, weights, total, columns, halo):
+def convolve(sources, links, marks, far, weights, total, columns, halo):
     rows, depth = total.shape[0], weights.shape[0]
     padded, lanes = sources[0].shape
     paired = len(sources) == 2
-
-    def places(block):
-        link = links[1:, pl.ds(pl.multiple_of(block * BLOCK, BLOCK), BLOCK)]
-        place = jnp.where(link < rows, link + halo, jnp.where(link < rows + halo, link - rows, link))
-        return jnp.transpose(place)
-
-    def main(block, far):
-        start = pl.multiple_of(block * BLOCK, BLOCK)
-        near = places(block) - start
-        own = sources[0][pl.ds(pl.multiple_of(start + halo, 16), BLOCK), :]
-        pieces = picked(sources, near, start, WINDOW)
+    half = (TAPS - 1) // 2 * BLOCK
+
+    step = min(rows, STEP)
+
+    def gather(block):
+        start = block * BLOCK
+        own = sources[0][start + halo : start + halo + BLOCK, :]
+        even = marks[2 * block * half : (2 * block + 1) * half, :]
+        odd = marks[(2 * block + 1) * half : (2 * block + 2) * half, :]
+        pieces = picked(sources, even, odd, start, WINDOW)
         pieces = [pieces[0] + own] + pieces[1:] if paired else [own] + pieces
         for i, piece in enumerate(pieces):
-            columns[pl.ds(start, BLOCK), i * lanes : (i + 1) * lanes] = piece
-        return jnp.maximum(far, jnp.where((near < 0) | (near >= WINDOW), 1, 0))
-
-    far = lax.fori_loop(0, rows // BLOCK, main, jnp.zeros((BLOCK, TAPS - 1), jnp.int32), unroll=min(2, rows // BLOCK))
-    step = min(rows, 512)
-
-    def multiply(i, carry):
-        part = pl.ds(pl.multiple_of(i * step, step), step)
-        total[part, :] = dot(columns[part, :depth], weights[...])
-        return carry
-
-    lax.fori_loop(0, rows // step, multiply, 0)
+            columns[start : start + BLOCK, i * lanes : (i + 1) * lanes] = piece
+
+    def multiply(part):
+        total[part * step : (part + 1) * step, :] = dot(columns[part * step : (part + 1) * step, :depth], weights[...])
+
+    for part in range(rows // step):
+        for block in range(part * step // BLOCK, (part + 1) * step // BLOCK):
+            gather(block)
+        if part:
+            multiply(part - 1)
+    multiply(rows // step - 1)
     if padded <= WINDOW:
         return
 
-    @pl.when(jnp.max(far) > 0)
+    @pl.when(jnp.max(far[...]) > 0)
     def _():
         def rest(block, carry):
             start = pl.multiple_of(block * BLOCK, BLOCK)
@@ -99,7 +124,9 @@
                 @pl.when((place < block) | (place > block + 1))
                 def _():
                     first = pl.multiple_of(place * BLOCK, BLOCK)
-                    pieces = picked(sources, places(block) - first, first, BLOCK)
+                    hot = hots(spots(links, block, rows, halo) - first, BLOCK)
+                    even, odd = jnp.concatenate(hot[0::2], axis=0), jnp.concatenate(hot[1::2], axis=0)
+                    pieces = picked(sources, even, odd, first, BLOCK)
                     pieces = pieces if paired else [jnp.zeros_like(pieces[0])] + pieces
                     gathered = jnp.concatenate(pieces, axis=1)[:, :depth]
                     total[pl.ds(start, BLOCK), :] += dot(gathered, weights[...])
@@ -152,21 +179,29 @@
         target[halo:, :] = jnp.broadcast_to(order, (16, BLOCK)).astype(jnp.bfloat16)
 
 
-def stage_kernel(count, *refs):
+def stage_kernel(count, halo, *refs):
     after, feat = refs[:2]
     sources, targets = refs[2 : 2 + count], refs[2 + count : 2 + 2 * count]
-    turned, flat, sems = refs[2 + 2 * count :]
+    turned, marks, far, flat, sems = refs[2 + 2 * count :]
     del after
-    copies = start_copies([(feat, flat)] + list(zip(sources, targets)), sems)
+    copies = start_copies([(sources[0], targets[0]), (feat, flat)] + list(zip(sources[1:], targets[1:])), sems)
     copies[0].wait()
+    mark(targets[0], halo, marks, far)
+    copies[1].wait()
     for i in range(turned.shape[0] // BLOCK):
         part = flat[:, i * BLOCK : (i + 1) * BLOCK].astype(jnp.float32)
         turned[i * BLOCK : (i + 1) * BLOCK, :] = jnp.transpose(part).astype(jnp.bfloat16)
-    for copy in copies[1:]:
+    for copy in copies[2:]:
         copy.wait()
 
 
-def enter_kernel(halo, feat, left, right, links, weights, total, stats, to_last, to_next, order, low, high, columns):
+def mark_kernel(halos, *refs):
+    count = len(halos)
+    for i, halo in enumerate(halos):
+        mark(refs[i], halo, refs[count + 2 * i], refs[count + 2 * i + 1])
+
+
+def enter_kernel(halo, feat, left, right, links, marks, far, weights, total, stats, to_last, to_next, order, low, high, columns):
     rows, width = feat.shape
     blank = jnp.zeros((rows, width), jnp.bfloat16)
     edge = jnp.zeros((halo, width), jnp.bfloat16)
@@ -179,7 +214,7 @@
     high[:halo, :] = jnp.concatenate([edge, before], axis=1)
     low[halo + rows :, :] = jnp.concatenate([after, edge], axis=1)
     high[halo + rows :, :] = jnp.concatenate([edge, after], axis=1)
-    convolve((low, high), links, weights, total, columns, halo)
+    convolve((low, high), links, marks, far, weights, total, columns, halo)
     summarize(total, stats, to_last, to_next)
 
 
@@ -211,11 +246,11 @@
 
 
 def layer_kernel(halo, listing, pool, count, parts, *refs):
-    raw, left, right, order, gain, shift, links, weights = refs[:8]
-    pairs = refs[8 : 8 + parts]
-    outs = refs[8 + parts :]
+    raw, left, right, order, gain, shift, links, marks, far, weights = refs[:10]
+    pairs = refs[10 : 10 + parts]
+    outs = refs[10 + parts :]
     if pool:
-        skip, outs = outs[0], outs[1:]
+        outer, *outs, skip, sem = outs
     total, stats, *edges, source, columns = outs
     act = norm_of(pairs, count, gain, shift)
     rows = total.shape[0]
@@ -237,8 +272,13 @@
         return carry
 
     lax.fori_loop(0, raw.shape[0] // step, one, 0, unroll=2)
-    convolve((source,), links, weights, total, columns, halo)
+    if pool:
+        copy = pltpu.make_async_copy(skip, outer, sem)
+        copy.start()
+    convolve((source,), links, marks, far, weights, total, columns, halo)
     summarize(total, stats, *edges)
+    if pool:
+        copy.wait()
 
 
 def last_kernel(count, parts, *refs):
@@ -247,13 +287,13 @@
     out[...] = norm_of(refs[3 : 3 + parts], count, gain, shift)(raw[...])
 
 
-def call(body, outs, scratch, *args, here=(), flops=0, traffic=0):
+def call(body, outs, scratch, *args, here=(), out_here=(), flops=0, traffic=0):
     args = [pltpu.with_memory_space_constraint(arg, pltpu.HBM) if i in here else arg for i, arg in enumerate(args)]
     return pl.pallas_call(
         body,
         out_shape=outs,
         in_specs=[HERE if i in here else VM for i in range(len(args))],
-        out_specs=[VM] * len(outs) if isinstance(outs, (list, tuple)) else VM,
+        out_specs=[HERE if i in out_here else VM for i in range(len(outs))] if isinstance(outs, (list, tuple)) else VM,
         scratch_shapes=scratch,
         compiler_params=pltpu.CompilerParams(vmem_limit_bytes=16 * 1024 * 1024),
         cost_estimate=pl.CostEstimate(flops=flops, bytes_accessed=traffic, transcendentals=0) if traffic else None,
@@ -290,6 +330,10 @@
 
 def conv_outs(rows, channels, edge):
     return [f32(rows, channels), f32(2, channels)] + [f32(edge, channels)] * (2 if edge else 0)
+
+
+def mark_outs(rows):
+    return [bf16(rows * (TAPS - 1), WINDOW), jax.ShapeDtypeStruct((8, TAPS - 1), jnp.int32)]
 
 
 def round_up(value, unit):
@@ -343,10 +387,12 @@
     kernels = (kernel_enter, kernel_fine, kernel_widen, kernel_mid, kernel_deep)
     norms = (gain_enter, shift_enter, gain_fine, shift_fine, gain_widen, shift_widen, gain_mid, shift_mid, gain_deep, shift_deep)
     held = [kernel.reshape(TAPS * kernel.shape[1], kernel.shape[2]) for kernel in kernels]
-    held = held + list(norms) + [links_fine, links_mid, links_coarse]
-    *held, turned = call(
-        functools.partial(stage_kernel, len(held)),
-        [jax.ShapeDtypeStruct(value.shape, value.dtype) for value in held] + [bf16(rows_a, width)],
+    held = [links_fine, links_mid, links_coarse] + held + list(norms)
+    *held, turned, marks_a, far_a = call(
+        functools.partial(stage_kernel, len(held), halo_a),
+        [jax.ShapeDtypeStruct(value.shape, value.dtype) for value in held]
+        + [bf16(rows_a, width)]
+        + mark_outs(rows_a),
         [pltpu.VMEM(flat.shape, jnp.bfloat16), pltpu.SemaphoreType.DMA((len(held) + 1,))],
         to_next,
         flat,
@@ -354,7 +400,15 @@
         here=range(1, len(held) + 2),
         traffic=8 * 1024 * 1024,
     )
-    weights, norms, links = held[:5], held[5:15], held[15:]
+    links, weights, norms = held[:3], held[3:8], held[8:]
+    marks_b, far_b, marks_c, far_c = call(
+        functools.partial(mark_kernel, (halo_b, halo_c)),
+        mark_outs(rows_b) + mark_outs(rows_c),
+        [],
+        links[1],
+        links[2],
+        traffic=4 * 1024 * 1024,
+    )
     source_a = pltpu.VMEM((round_up(rows_a + 2 * halo_a, BLOCK), 2 * width), jnp.bfloat16)
     *state, order = call(
         functools.partial(enter_kernel, halo_a),
@@ -364,6 +418,8 @@
         left,
         right,
         links[0],
+        marks_a,
+        far_a,
         weights[0],
     )
 
@@ -382,21 +438,23 @@
             [
                 pltpu.VMEM((max(round_up(rows + 2 * halo, BLOCK), WINDOW), channels), jnp.bfloat16),
                 pltpu.VMEM((rows, TAPS * channels), jnp.bfloat16),
-            ],
+            ]
+            + ([pltpu.VMEM((raw_rows, channels), jnp.bfloat16), pltpu.SemaphoreType.DMA] if pool else []),
             total,
             from_left,
             from_right,
             order,
             gain.reshape(1, -1),
             shift.reshape(1, -1),
-            links,
+            *links,
             kernel,
             *pairs,
+            out_here=(0,) if pool else (),
         )
 
-    level_a = (rows_a, halo_a, 0, links[0])
-    level_b = (rows_b, halo_b, halo_a, links[1])
-    level_c = (rows_c, halo_c, halo_a + halo_b, links[2])
+    level_a = (rows_a, halo_a, 0, (links[0], marks_a, far_a))
+    level_b = (rows_b, halo_b, halo_a, (links[1], marks_b, far_b))
+    level_c = (rows_c, halo_c, halo_a + halo_b, (links[2], marks_c, far_c))
     state = layer(1, state, level_a, False, 4 * halo_b)
     skip_fine, *state = layer(2, state, level_b, True, halo_b)
     state = layer(3, state, level_b, False, 4 * halo_c)

time: 99.7 us -> 90.4 us (0.907)
  Pallas kernels: 29.4 us -> 22.3 us
  waiting for transfers between devices: 14 us -> 11.7 us
    pallas_call x8 -> x9, Pallas kernels: 29.4 us -> 22.3 us  [call(): pl.pallas_call(body, out_shape=outs, in_specs=[HERE if i in here else VM...]
    ppermute x10, waiting for transfers between devices: 3.25 us -> 1.9 us  [shifted(): lax.ppermute(value, AXES, [(source, (source + steps) % count) for source...]
  transfers between devices with their start and end apart: 40 -> 40, of which waited for: 14 -> 13; matrix products, arithmetic and copies ran while one was open for 0% -> 0% of each run, Pallas kernels for 3% -> 5%
where the time goes in v3:
time: 90.4 us; the launch traced here: 90.2 us
  starting transfers between devices  55.1 us (61%)
  Pallas kernels  22.3 us (25%)
  waiting for transfers between devices  11.7 us (13%)
    ppermute x30, starting transfers between devices, swapped(): lax.ppermute(value, AXES, [(source, source ^ mask) for source in range(co...  31.8 us
    ppermute x10, starting transfers between devices, shifted(): lax.ppermute(value, AXES, [(source, (source + steps) % count) for source...  23.3 us
    pallas_call x9, Pallas kernels, call(): pl.pallas_call(body, out_shape=outs, in_specs=[HERE if i in here else VM...  22.3 us
    ppermute x30, waiting for transfers between devices, swapped(): lax.ppermute(value, AXES, [(source, source ^ mask) for source in range(co...  9.84 us
    ppermute x10, waiting for transfers between devices, shifted(): lax.ppermute(value, AXES, [(source, (source + steps) % count) for source...  1.9 us
  transfers between devices with their start and end apart: 40, of which 13 were waited for; matrix products, arithmetic and copies ran while one was open for 0% of the time, Pallas kernels for 5%

profile of v3, /device:TPU:0, one launch (start us, length us, event | category | flops | bytes accessed | tf_op | source)
XLA Modules:
  0.0 90.2 jit_solution(10435278429149771717)
XLA Ops:
  0.6 0.9 %shard_map.229 = (bf16[80,128]{1,0:T(8,128)(2,1)S(1)}, bf16[80,128]{1,0:T(8,128)(2,1)S(1)}) custom-call(bf16[64,2048]{1,0:T(8,128)(2,1)} %bitcast.28, s32[1,2,64]{2,1,0:T(2,128)} %sends_a.1, s32[1,2,32]{2,1,0:T(2,128)} %sends_b.1, s32[1,2,16]{2,1,0:T(2,128)} %sends_c.1), custom_call_target="tpu_custom_call" | custom-call | tf_op jit(solution)/shard_map/pallas_call | solution.py:292
  1.6 5.5 %collective-permute-start.1 = (bf16[80,128]{1,0:T(8,128)(2,1)S(1)}, bf16[80,128]{1,0:T(8,128)(2,1)S(1)}, u32[]{:S(2)}, u32[]{:S(2)}) collective-permute-start(bf16[80,128]{1,0:T(8,128)(2,1)S(1)} %get-tuple-element.53), channel_id=1, source_target_pairs={{0,15},{1,0},{2,1},{3,2},{4,3},{5,4},{6,5},{7,6},{8,7},{9,8},{10,9... | collective-permute-start | bytes 61448 | tf_op jit(solution)/shard_map/ppermute | solution.py:23
  7.1 4.0 %shard_map.230 = (s32[9,2048]{1,0:T(8,128)S(1)}, s32[9,512]{1,0:T(8,128)S(1)}, s32[9,128]{1,0:T(8,128)S(1)}, bf16[576,128]{1,0:T(8,128)(2,1)S(1)}, bf16[1152,128...) custom-call(bf16[80,128]{1,0:T(8,128)(2,1)S(1)} %get-tuple-element.5, ...), custom_call_target="tpu_custom_call" | custom-call | bytes 8388608 | tf_op jit(solution)/shard_map/pallas_call | solution.py:292
  11.1 1.9 %collective-permute-done.left = bf16[80,128]{1,0:T(8,128)(2,1)S(1)} collective-permute-done((bf16[80,128]{1,0:T(8,128)(2,1)S(1)}, bf16[80,128]{1,0:T(8,128)(2,1)S(1)}, u32[]{:S(2)}, u32[]{:S(2)}) %collective-permute-start) | collective-permute-done | bytes 20512 | tf_op jit(solution)/shard_map/ppermute | solution.py:23
  13.0 3.7 %shard_map.231 = (f32[2048,128]{1,0:T(8,128)S(1)}, f32[2,128]{1,0:T(2,128)S(1)}, f32[64,128]{1,0:T(8,128)S(1)}, f32[64,128]{1,0:T(8,128)S(1)}, f32[2,128]{1,0:T(2,128)S(1)}) custom-call(bf16[2048,64]{1,0:T(8,128)(2,1)S(1)} %get-tuple-element.52.feat, bf16[80,128]{1,0:T(8,128)(2,1)S(1)} %collective-permute-done.left, ...), custom_call_target="tpu_custom_call" | custom-call | tf_op jit(solution)/shard_map/pallas_call | solution.py:292
  16.7 0.1 collective-permute-start.6
  16.8 0.1 collective-permute-start.5
  16.8 1.8 %collective-permute-start.4 = (f32[2,128]{1,0:T(2,128)S(1)}, f32[2,128]{1,0:T(2,128)S(1)}, u32[]{:S(2)}, u32[]{:S(2)}) collective-permute-start(f32[2,128]{1,0:T(2,128)S(1)} %get-tuple-element.65), channel_id=1, source_target_pairs={{0,1},{1,0},{2,3},{3,2},{4,5},{5,4},{6,7},{7,6},{8,9},{9,8},{10,11... | collective-permute-start | bytes 3080 | tf_op jit(solution)/shard_map/ppermute | solution.py:28
  18.6 4.4 %collective-permute-start.3 = (f32[64,128]{1,0:T(8,128)S(1)}, f32[64,128]{1,0:T(8,128)S(1)}, u32[]{:S(2)}, u32[]{:S(2)}) collective-permute-start(f32[64,128]{1,0:T(8,128)S(1)} %get-tuple-element.60), channel_id=1, source_target_pairs={{0,15},{1,0},{2,1},{3,2},{4,3},{5,4},{6,5},{7,6},{8,7},{9,8},{10,9... | collective-permute-start | bytes 98312 | tf_op jit(solution)/shard_map/ppermute | solution.py:23
  23.1 0.5 collective-permute-start.9
  23.6 4.0 %collective-permute-start.7 = (f32[2,128]{1,0:T(2,128)S(1)}, f32[2,128]{1,0:T(2,128)S(1)}, u32[]{:S(2)}, u32[]{:S(2)}) collective-permute-start(f32[2,128]{1,0:T(2,128)S(1)} %pad_maximum_fusion.3.refs_10_), channel_id=1, source_target_pairs={{0,4},{1,5},{2,6},{3,7},{4,0},{5,1},{6,2},{7,3},{8,12},{9,13},{10,... | collective-permute-start | bytes 3080 | tf_op jit(solution)/shard_map/ppermute | solution.py:28
  27.6 1.0 %collective-permute-done.9.refs_13_ = f32[2,128]{1,0:T(2,128)S(1)} collective-permute-done((f32[2,128]{1,0:T(2,128)S(1)}, f32[2,128]{1,0:T(2,128)S(1)}, u32[]{:S(2)}, u32[]{:S(2)}) %collective-permute-start.9) | collective-permute-done | bytes 1056 | tf_op jit(solution)/shard_map/ppermute | solution.py:28
  28.5 0.6 collective-permute-done.7.refs_11_
  29.1 0.0 collective-permute-done.2.refs_1_
  29.1 0.0 collective-permute-done.3.refs_2_
  29.1 4.4 %shard_map.232 = (f32[2048,128]{1,0:T(8,128)S(1)}, f32[2,128]{1,0:T(2,128)S(1)}, f32[128,128]{1,0:T(8,128)S(1)}, f32[128,128]{1,0:T(8,128)S(1)}) custom-call(f32[2048,128]{1,0:T(8,128)S(1)} %get-tuple-element.58.refs_0_, f32[64,128]{1,0:T(8,128)S(1)} %collective-permute-done.2.refs_1_, f32[64,128]{1,0:T(8,128)S(1)} %collective-permute-done.3.refs_2_, ...), custom_call_target="tpu_custom_call" | custom-call | tf_op jit(solution)/shard_map/pallas_call | solution.py:292
  33.5 0.1 collective-permute-start.14
  33.5 0.1 collective-permute-start.13
  33.6 1.8 %collective-permute-start.12 = (f32[2,128]{1,0:T(2,128)S(1)}, f32[2,128]{1,0:T(2,128)S(1)}, u32[]{:S(2)}, u32[]{:S(2)}) collective-permute-start(f32[2,128]{1,0:T(2,128)S(1)} %get-tuple-element.76), channel_id=1, source_target_pairs={{0,1},{1,0},{2,3},{3,2},{4,5},{5,4},{6,7},{7,6},{8,9},{9,8},{10,11... | collective-permute-start | bytes 3080 | tf_op jit(solution)/shard_map/ppermute | solution.py:28
  35.4 4.4 %collective-permute-start.11 = (f32[128,128]{1,0:T(8,128)S(1)}, f32[128,128]{1,0:T(8,128)S(1)}, u32[]{:S(2)}, u32[]{:S(2)}) collective-permute-start(f32[128,128]{1,0:T(8,128)S(1)} %get-tuple-element.68), channel_id=1, source_target_pairs={{0,15},{1,0},{2,1},{3,2},{4,3},{5,4},{6,5},{7,6},{8,7},{9,8},{10,9... | collective-permute-start | bytes 196616 | tf_op jit(solution)/shard_map/ppermute | solution.py:23
  39.8 0.0 collective-permute-done.14
  39.9 0.6 collective-permute-start.17
  40.5 1.1 %collective-permute-start.16 = (f32[2,128]{1,0:T(2,128)S(1)}, f32[2,128]{1,0:T(2,128)S(1)}, u32[]{:S(2)}, u32[]{:S(2)}) collective-permute-start(f32[2,128]{1,0:T(2,128)S(1)} %pad_maximum_fusion.4.refs_10_), channel_id=1, source_target_pairs={{0,8},{1,9},{2,10},{3,11},{4,12},{5,13},{6,14},{7,15},{8,0},{9,1},... | collective-permute-start | bytes 3080 | tf_op jit(solution)/shard_map/ppermute | solution.py:28
  41.6 2.7 %collective-permute-start.15 = (f32[2,128]{1,0:T(2,128)S(1)}, f32[2,128]{1,0:T(2,128)S(1)}, u32[]{:S(2)}, u32[]{:S(2)}) collective-permute-start(f32[2,128]{1,0:T(2,128)S(1)} %pad_maximum_fusion.4.refs_10_), channel_id=1, source_target_pairs={{0,4},{1,5},{2,6},{3,7},{4,0},{5,1},{6,2},{7,3},{8,12},{9,13},{10,... | collective-permute-start | bytes 3080 | tf_op jit(solution)/shard_map/ppermute | solution.py:28
  44.3 0.9 %shard_map.233 = (bf16[4096,256]{1,0:T(8,128)(2,1)S(1)}, s32[8,8]{1,0:T(8,128)S(1)}, bf16[1024,256]{1,0:T(8,128)(2,1)S(1)}, s32[8,8]{1,0:T(8,128)S(1)}) custom-call(s32[9,512]{1,0:T(8,128)S(1)} %get-tuple-element.71.refs_0_.refs_6_, s32[9,128]{1,0:T(8,128)S(1)} %get-tuple-element.72.refs_1_.refs_6_), custom_call_target="tpu_custom_call" | custom-call | bytes 4194304 | tf_op jit(solution)/shard_map/pallas_call | solution.py:292
  45.3 0.0 collective-permute-done.17.refs_13_
  45.3 0.0 collective-permute-done.16.refs_12_
  45.3 0.6 collective-permute-done.15.refs_11_
  45.9 0.0 collective-permute-done.11.refs_2_
  45.9 3.6 %shard_map.234 = (bf16[2048,128]{1,0:T(8,128)(2,1)}, f32[512,256]{1,0:T(8,128)S(1)}, f32[2,256]{1,0:T(2,128)S(1)}, f32[32,256]{1,0:T(8,128)S(1)}, f32[32,256]{1,0:T(8,128)S(1)}) custom-call(f32[2048,128]{1,0:T(8,128)S(1)} %get-tuple-element.66.refs_0_, f32[128,128]{1,0:T(8,128)S(1)} %collective-permute-done.10.refs_1_, ...), custom_call_target="tpu_custom_call" | custom-call | tf_op jit(solution)/shard_map/pallas_call | solution.py:292
  49.5 0.1 collective-permute-start.22
  49.5 0.1 collective-permute-start.21
  49.6 1.8 %collective-permute-start.20 = (f32[2,256]{1,0:T(2,128)S(1)}, f32[2,256]{1,0:T(2,128)S(1)}, u32[]{:S(2)}, u32[]{:S(2)}) collective-permute-start(f32[2,256]{1,0:T(2,128)S(1)} %get-tuple-element.84), channel_id=1, source_target_pairs={{0,1},{1,0},{2,3},{3,2},{4,5},{5,4},{6,7},{7,6},{8,9},{9,8},{10,11... | collective-permute-start | bytes 6152 | tf_op jit(solution)/shard_map/ppermute | solution.py:28
  51.4 0.0 collective-permute-start.18
  51.4 4.4 %collective-permute-start.19 = (f32[32,256]{1,0:T(8,128)S(1)}, f32[32,256]{1,0:T(8,128)S(1)}, u32[]{:S(2)}, u32[]{:S(2)}) collective-permute-start(f32[32,256]{1,0:T(8,128)S(1)} %get-tuple-element.80), channel_id=1, source_target_pairs={{0,15},{1,0},{2,1},{3,2},{4,3},{5,4},{6,5},{7,6},{8,7},{9,8},{10,9... | collective-permute-start | bytes 98312 | tf_op jit(solution)/shard_map/ppermute | solution.py:23
  55.8 0.0 collective-permute-done.22
  55.9 0.6 collective-permute-start.25
  56.5 1.1 %collective-permute-start.24 = (f32[2,256]{1,0:T(2,128)S(1)}, f32[2,256]{1,0:T(2,128)S(1)}, u32[]{:S(2)}, u32[]{:S(2)}) collective-permute-start(f32[2,256]{1,0:T(2,128)S(1)} %pad_maximum_fusion.1.refs_10_), channel_id=1, source_target_pairs={{0,8},{1,9},{2,10},{3,11},{4,12},{5,13},{6,14},{7,15},{8,0},{9,1},... | collective-permute-start | bytes 6152 | tf_op jit(solution)/shard_map/ppermute | solution.py:28
  57.6 2.7 %collective-permute-start.23 = (f32[2,256]{1,0:T(2,128)S(1)}, f32[2,256]{1,0:T(2,128)S(1)}, u32[]{:S(2)}, u32[]{:S(2)}) collective-permute-start(f32[2,256]{1,0:T(2,128)S(1)} %pad_maximum_fusion.1.refs_10_), channel_id=1, source_target_pairs={{0,4},{1,5},{2,6},{3,7},{4,0},{5,1},{6,2},{7,3},{8,12},{9,13},{10,... | collective-permute-start | bytes 6152 | tf_op jit(solution)/shard_map/ppermute | solution.py:28
  60.3 1.0 %collective-permute-done.25.refs_13_ = f32[2,256]{1,0:T(2,128)S(1)} collective-permute-done((f32[2,256]{1,0:T(2,128)S(1)}, f32[2,256]{1,0:T(2,128)S(1)}, u32[]{:S(2)}, u32[]{:S(2)}) %collective-permute-start.25) | collective-permute-done | bytes 2080 | tf_op jit(solution)/shard_map/ppermute | solution.py:28
  61.3 0.6 collective-permute-done.23.refs_11_
  61.9 2.6 %shard_map.235 = (f32[512,256]{1,0:T(8,128)S(1)}, f32[2,256]{1,0:T(2,128)S(1)}, f32[64,256]{1,0:T(8,128)S(1)}, f32[64,256]{1,0:T(8,128)S(1)}) custom-call(f32[512,256]{1,0:T(8,128)S(1)} %get-tuple-element.78.refs_0_, f32[32,256]{1,0:T(8,128)S(1)} %collective-permute-done.18.refs_1_, f32[32,256]{1,0:T(8,128)S(1)} %collective-permute-done.19.refs_2_, ...), custom_call_target="tpu_custom_call" | custom-call | tf_op jit(solution)/shard_map/pallas_call | solution.py:292
  64.5 0.1 collective-permute-start.30
  64.6 0.1 collective-permute-start.29
  64.7 1.8 %collective-permute-start.28 = (f32[2,256]{1,0:T(2,128)S(1)}, f32[2,256]{1,0:T(2,128)S(1)}, u32[]{:S(2)}, u32[]{:S(2)}) collective-permute-start(f32[2,256]{1,0:T(2,128)S(1)} %get-tuple-element.93), channel_id=1, source_target_pairs={{0,1},{1,0},{2,3},{3,2},{4,5},{5,4},{6,7},{7,6},{8,9},{9,8},{10,11... | collective-permute-start | bytes 6152 | tf_op jit(solution)/shard_map/ppermute | solution.py:28
  66.4 4.4 %collective-permute-start.27 = (f32[64,256]{1,0:T(8,128)S(1)}, f32[64,256]{1,0:T(8,128)S(1)}, u32[]{:S(2)}, u32[]{:S(2)}) collective-permute-start(f32[64,256]{1,0:T(8,128)S(1)} %get-tuple-element.87), channel_id=1, source_target_pairs={{0,15},{1,0},{2,1},{3,2},{4,3},{5,4},{6,5},{7,6},{8,7},{9,8},{10,9... | collective-permute-start | bytes 196616 | tf_op jit(solution)/shard_map/ppermute | solution.py:23
  70.9 0.6 collective-permute-start.33
  71.6 1.1 %collective-permute-start.32 = (f32[2,256]{1,0:T(2,128)S(1)}, f32[2,256]{1,0:T(2,128)S(1)}, u32[]{:S(2)}, u32[]{:S(2)}) collective-permute-start(f32[2,256]{1,0:T(2,128)S(1)} %pad_maximum_fusion.2.refs_10_), channel_id=1, source_target_pairs={{0,8},{1,9},{2,10},{3,11},{4,12},{5,13},{6,14},{7,15},{8,0},{9,1},... | collective-permute-start | bytes 6152 | tf_op jit(solution)/shard_map/ppermute | solution.py:28
  72.7 2.7 %collective-permute-start.31 = (f32[2,256]{1,0:T(2,128)S(1)}, f32[2,256]{1,0:T(2,128)S(1)}, u32[]{:S(2)}, u32[]{:S(2)}) collective-permute-start(f32[2,256]{1,0:T(2,128)S(1)} %pad_maximum_fusion.2.refs_10_), channel_id=1, source_target_pairs={{0,4},{1,5},{2,6},{3,7},{4,0},{5,1},{6,2},{7,3},{8,12},{9,13},{10,... | collective-permute-start | bytes 6152 | tf_op jit(solution)/shard_map/ppermute | solution.py:28
  75.4 1.0 %collective-permute-done.33.refs_13_ = f32[2,256]{1,0:T(2,128)S(1)} collective-permute-done((f32[2,256]{1,0:T(2,128)S(1)}, f32[2,256]{1,0:T(2,128)S(1)}, u32[]{:S(2)}, u32[]{:S(2)}) %collective-permute-start.33) | collective-permute-done | bytes 2080 | tf_op jit(solution)/shard_map/ppermute | solution.py:28
  76.4 0.6 collective-permute-done.31.refs_11_
  77.0 1.5 %shard_map.236 = (bf16[512,256]{1,0:T(8,128)(2,1)}, f32[128,512]{1,0:T(8,128)S(1)}, f32[2,512]{1,0:T(2,128)S(1)}) custom-call(f32[512,256]{1,0:T(8,128)S(1)} %get-tuple-element.85.refs_0_, f32[64,256]{1,0:T(8,128)S(1)} %collective-permute-done.26.refs_1_, f32[64,256]{1,0:T(8,128)S(1)} %collective-permute-done.27.refs_2_, ...), custom_call_target="tpu_custom_call" | custom-call | tf_op jit(solution)/shard_map/pallas_call | solution.py:292
  78.5 0.1 collective-permute-start.36
  78.6 0.1 collective-permute-start.35
  78.6 1.8 %collective-permute-start.34 = (f32[2,512]{1,0:T(2,128)S(1)}, f32[2,512]{1,0:T(2,128)S(1)}, u32[]{:S(2)}, u32[]{:S(2)}) collective-permute-start(f32[2,512]{1,0:T(2,128)S(1)} %get-tuple-element.98), channel_id=1, source_target_pairs={{0,1},{1,0},{2,3},{3,2},{4,5},{5,4},{6,7},{7,6},{8,9},{9,8},{10,11... | collective-permute-start | bytes 12296 | tf_op jit(solution)/shard_map/ppermute | solution.py:28
  80.4 1.2 %collective-permute-done.36 = f32[2,512]{1,0:T(2,128)S(1)} collective-permute-done((f32[2,512]{1,0:T(2,128)S(1)}, f32[2,512]{1,0:T(2,128)S(1)}, u32[]{:S(2)}, u32[]{:S(2)}) %collective-permute-start.36) | collective-permute-done | bytes 4128 | tf_op jit(solution)/shard_map/ppermute | solution.py:28
  81.6 0.7 collective-permute-done.35
  82.3 2.4 %collective-permute-start.39 = (f32[2,512]{1,0:T(2,128)S(1)}, f32[2,512]{1,0:T(2,128)S(1)}, u32[]{:S(2)}, u32[]{:S(2)}) collective-permute-start(f32[2,512]{1,0:T(2,128)S(1)} %pad_maximum_fusion.refs_3_), channel_id=1, source_target_pairs={{0,12},{1,13},{2,14},{3,15},{4,8},{5,9},{6,10},{7,11},{8,4},{9,5},... | collective-permute-start | bytes 12296 | tf_op jit(solution)/shard_map/ppermute | solution.py:28
  84.7 1.1 %collective-permute-start.38 = (f32[2,512]{1,0:T(2,128)S(1)}, f32[2,512]{1,0:T(2,128)S(1)}, u32[]{:S(2)}, u32[]{:S(2)}) collective-permute-start(f32[2,512]{1,0:T(2,128)S(1)} %pad_maximum_fusion.refs_3_), channel_id=1, source_target_pairs={{0,8},{1,9},{2,10},{3,11},{4,12},{5,13},{6,14},{7,15},{8,0},{9,1},... | collective-permute-start | bytes 12296 | tf_op jit(solution)/shard_map/ppermute | solution.py:28
  85.8 0.9 %collective-permute-start.37 = (f32[2,512]{1,0:T(2,128)S(1)}, f32[2,512]{1,0:T(2,128)S(1)}, u32[]{:S(2)}, u32[]{:S(2)}) collective-permute-start(f32[2,512]{1,0:T(2,128)S(1)} %pad_maximum_fusion.refs_3_), channel_id=1, source_target_pairs={{0,4},{1,5},{2,6},{3,7},{4,0},{5,1},{6,2},{7,3},{8,12},{9,13},{10,... | collective-permute-start | bytes 12296 | tf_op jit(solution)/shard_map/ppermute | solution.py:28
  86.7 1.0 %collective-permute-done.39.refs_6_ = f32[2,512]{1,0:T(2,128)S(1)} collective-permute-done((f32[2,512]{1,0:T(2,128)S(1)}, f32[2,512]{1,0:T(2,128)S(1)}, u32[]{:S(2)}, u32[]{:S(2)}) %collective-permute-start.39) | collective-permute-done | bytes 4128 | tf_op jit(solution)/shard_map/ppermute | solution.py:28
  87.8 1.5 %collective-permute-done.38.refs_5_ = f32[2,512]{1,0:T(2,128)S(1)} collective-permute-done((f32[2,512]{1,0:T(2,128)S(1)}, f32[2,512]{1,0:T(2,128)S(1)}, u32[]{:S(2)}, u32[]{:S(2)}) %collective-permute-start.38) | collective-permute-done | bytes 4128 | tf_op jit(solution)/shard_map/ppermute | solution.py:28
  89.2 0.2 collective-permute-done.37.refs_4_
  89.4 0.8 shard_map.237
  (35 shorter events, 0.2 us)
Async XLA Ops:
  1.6 9.6 %collective-permute-start.1 = (bf16[80,128]{1,0:T(8,128)(2,1)S(1)}, bf16[80,128]{1,0:T(8,128)(2,1)S(1)}, u32[]{:S(2)}, u32[]{:S(2)}) collective-permute-start(bf16[80,128]{1,0:T(8,128)(2,1)S(1)} %get-tuple-element.53), channel_id=1, source_target_pairs={{0,15},{1,0},{2,1},{3,2},{4,3},{5,4},{6,5},{7,6},{8,7},{9,8},{10,9... | collective-permute-start | bytes 61448 | tf_op jit(solution)/shard_map/ppermute | solution.py:23
  7.1 5.9 %collective-permute-start = (bf16[80,128]{1,0:T(8,128)(2,1)S(1)}, bf16[80,128]{1,0:T(8,128)(2,1)S(1)}, u32[]{:S(2)}, u32[]{:S(2)}) collective-permute-start(bf16[80,128]{1,0:T(8,128)(2,1)S(1)} %get-tuple-element.51.refs_0_), channel_id=1, source_target_pairs={{0,1},{1,2},{2,3},{3,4},{4,5},{5,6},{6,7},{7,8},{8,9},{9,10},{10,1... | collective-permute-start | bytes 61448 | tf_op jit(solution)/shard_map/ppermute | solution.py:23
  16.7 6.4 %collective-permute-start.6 = (f32[2,128]{1,0:T(2,128)S(1)}, f32[2,128]{1,0:T(2,128)S(1)}, u32[]{:S(2)}, u32[]{:S(2)}) collective-permute-start(f32[2,128]{1,0:T(2,128)S(1)} %get-tuple-element.65), channel_id=1, source_target_pairs={{0,3},{1,2},{2,1},{3,0},{4,7},{5,6},{6,5},{7,4},{8,11},{9,10},{10,... | collective-permute-start | bytes 3080 | tf_op jit(solution)/shard_map/ppermute | solution.py:28
  16.8 6.3 %collective-permute-start.5 = (f32[2,128]{1,0:T(2,128)S(1)}, f32[2,128]{1,0:T(2,128)S(1)}, u32[]{:S(2)}, u32[]{:S(2)}) collective-permute-start(f32[2,128]{1,0:T(2,128)S(1)} %get-tuple-element.65), channel_id=1, source_target_pairs={{0,2},{1,3},{2,0},{3,1},{4,6},{5,7},{6,4},{7,5},{8,10},{9,11},{10,... | collective-permute-start | bytes 3080 | tf_op jit(solution)/shard_map/ppermute | solution.py:28
  16.8 6.2 %collective-permute-start.4 = (f32[2,128]{1,0:T(2,128)S(1)}, f32[2,128]{1,0:T(2,128)S(1)}, u32[]{:S(2)}, u32[]{:S(2)}) collective-permute-start(f32[2,128]{1,0:T(2,128)S(1)} %get-tuple-element.65), channel_id=1, source_target_pairs={{0,1},{1,0},{2,3},{3,2},{4,5},{5,4},{6,7},{7,6},{8,9},{9,8},{10,11... | collective-permute-start | bytes 3080 | tf_op jit(solution)/shard_map/ppermute | solution.py:28
  18.6 10.5 %collective-permute-start.2 = (f32[64,128]{1,0:T(8,128)S(1)}, f32[64,128]{1,0:T(8,128)S(1)}, u32[]{:S(2)}, u32[]{:S(2)}) collective-permute-start(f32[64,128]{1,0:T(8,128)S(1)} %get-tuple-element.59), channel_id=1, source_target_pairs={{0,1},{1,2},{2,3},{3,4},{4,5},{5,6},{6,7},{7,8},{8,9},{9,10},{10,1... | collective-permute-start | bytes 98312 | tf_op jit(solution)/shard_map/ppermute | solution.py:23
  18.6 10.5 %collective-permute-start.3 = (f32[64,128]{1,0:T(8,128)S(1)}, f32[64,128]{1,0:T(8,128)S(1)}, u32[]{:S(2)}, u32[]{:S(2)}) collective-permute-start(f32[64,128]{1,0:T(8,128)S(1)} %get-tuple-element.60), channel_id=1, source_target_pairs={{0,15},{1,0},{2,1},{3,2},{4,3},{5,4},{6,5},{7,6},{8,7},{9,8},{10,9... | collective-permute-start | bytes 98312 | tf_op jit(solution)/shard_map/ppermute | solution.py:23
  23.1 5.4 %collective-permute-start.9 = (f32[2,128]{1,0:T(2,128)S(1)}, f32[2,128]{1,0:T(2,128)S(1)}, u32[]{:S(2)}, u32[]{:S(2)}) collective-permute-start(f32[2,128]{1,0:T(2,128)S(1)} %pad_maximum_fusion.3.refs_10_), channel_id=1, source_target_pairs={{0,12},{1,13},{2,14},{3,15},{4,8},{5,9},{6,10},{7,11},{8,4},{9,5},... | collective-permute-start | bytes 3080 | tf_op jit(solution)/shard_map/ppermute | solution.py:28
  23.6 5.0 %collective-permute-start.8 = (f32[2,128]{1,0:T(2,128)S(1)}, f32[2,128]{1,0:T(2,128)S(1)}, u32[]{:S(2)}, u32[]{:S(2)}) collective-permute-start(f32[2,128]{1,0:T(2,128)S(1)} %pad_maximum_fusion.3.refs_10_), channel_id=1, source_target_pairs={{0,8},{1,9},{2,10},{3,11},{4,12},{5,13},{6,14},{7,15},{8,0},{9,1},... | collective-permute-start | bytes 3080 | tf_op jit(solution)/shard_map/ppermute | solution.py:28
  23.6 5.5 %collective-permute-start.7 = (f32[2,128]{1,0:T(2,128)S(1)}, f32[2,128]{1,0:T(2,128)S(1)}, u32[]{:S(2)}, u32[]{:S(2)}) collective-permute-start(f32[2,128]{1,0:T(2,128)S(1)} %pad_maximum_fusion.3.refs_10_), channel_id=1, source_target_pairs={{0,4},{1,5},{2,6},{3,7},{4,0},{5,1},{6,2},{7,3},{8,12},{9,13},{10,... | collective-permute-start | bytes 3080 | tf_op jit(solution)/shard_map/ppermute | solution.py:28
  33.5 6.4 %collective-permute-start.14 = (f32[2,128]{1,0:T(2,128)S(1)}, f32[2,128]{1,0:T(2,128)S(1)}, u32[]{:S(2)}, u32[]{:S(2)}) collective-permute-start(f32[2,128]{1,0:T(2,128)S(1)} %get-tuple-element.76), channel_id=1, source_target_pairs={{0,3},{1,2},{2,1},{3,0},{4,7},{5,6},{6,5},{7,4},{8,11},{9,10},{10,... | collective-permute-start | bytes 3080 | tf_op jit(solution)/shard_map/ppermute | solution.py:28
  33.5 6.3 %collective-permute-start.13 = (f32[2,128]{1,0:T(2,128)S(1)}, f32[2,128]{1,0:T(2,128)S(1)}, u32[]{:S(2)}, u32[]{:S(2)}) collective-permute-start(f32[2,128]{1,0:T(2,128)S(1)} %get-tuple-element.76), channel_id=1, source_target_pairs={{0,2},{1,3},{2,0},{3,1},{4,6},{5,7},{6,4},{7,5},{8,10},{9,11},{10,... | collective-permute-start | bytes 3080 | tf_op jit(solution)/shard_map/ppermute | solution.py:28
  33.6 6.2 %collective-permute-start.12 = (f32[2,128]{1,0:T(2,128)S(1)}, f32[2,128]{1,0:T(2,128)S(1)}, u32[]{:S(2)}, u32[]{:S(2)}) collective-permute-start(f32[2,128]{1,0:T(2,128)S(1)} %get-tuple-element.76), channel_id=1, source_target_pairs={{0,1},{1,0},{2,3},{3,2},{4,5},{5,4},{6,7},{7,6},{8,9},{9,8},{10,11... | collective-permute-start | bytes 3080 | tf_op jit(solution)/shard_map/ppermute | solution.py:28
  35.4 10.5 %collective-permute-start.10 = (f32[128,128]{1,0:T(8,128)S(1)}, f32[128,128]{1,0:T(8,128)S(1)}, u32[]{:S(2)}, u32[]{:S(2)}) collective-permute-start(f32[128,128]{1,0:T(8,128)S(1)} %get-tuple-element.67), channel_id=1, source_target_pairs={{0,1},{1,2},{2,3},{3,4},{4,5},{5,6},{6,7},{7,8},{8,9},{9,10},{10,1... | collective-permute-start | bytes 196616 | tf_op jit(solution)/shard_map/ppermute | solution.py:23
  35.4 10.5 %collective-permute-start.11 = (f32[128,128]{1,0:T(8,128)S(1)}, f32[128,128]{1,0:T(8,128)S(1)}, u32[]{:S(2)}, u32[]{:S(2)}) collective-permute-start(f32[128,128]{1,0:T(8,128)S(1)} %get-tuple-element.68), channel_id=1, source_target_pairs={{0,15},{1,0},{2,1},{3,2},{4,3},{5,4},{6,5},{7,6},{8,7},{9,8},{10,9... | collective-permute-start | bytes 196616 | tf_op jit(solution)/shard_map/ppermute | solution.py:23
  39.9 5.4 %collective-permute-start.17 = (f32[2,128]{1,0:T(2,128)S(1)}, f32[2,128]{1,0:T(2,128)S(1)}, u32[]{:S(2)}, u32[]{:S(2)}) collective-permute-start(f32[2,128]{1,0:T(2,128)S(1)} %pad_maximum_fusion.4.refs_10_), channel_id=1, source_target_pairs={{0,12},{1,13},{2,14},{3,15},{4,8},{5,9},{6,10},{7,11},{8,4},{9,5},... | collective-permute-start | bytes 3080 | tf_op jit(solution)/shard_map/ppermute | solution.py:28
  40.5 4.8 %collective-permute-start.16 = (f32[2,128]{1,0:T(2,128)S(1)}, f32[2,128]{1,0:T(2,128)S(1)}, u32[]{:S(2)}, u32[]{:S(2)}) collective-permute-start(f32[2,128]{1,0:T(2,128)S(1)} %pad_maximum_fusion.4.refs_10_), channel_id=1, source_target_pairs={{0,8},{1,9},{2,10},{3,11},{4,12},{5,13},{6,14},{7,15},{8,0},{9,1},... | collective-permute-start | bytes 3080 | tf_op jit(solution)/shard_map/ppermute | solution.py:28
  41.6 4.3 %collective-permute-start.15 = (f32[2,128]{1,0:T(2,128)S(1)}, f32[2,128]{1,0:T(2,128)S(1)}, u32[]{:S(2)}, u32[]{:S(2)}) collective-permute-start(f32[2,128]{1,0:T(2,128)S(1)} %pad_maximum_fusion.4.refs_10_), channel_id=1, source_target_pairs={{0,4},{1,5},{2,6},{3,7},{4,0},{5,1},{6,2},{7,3},{8,12},{9,13},{10,... | collective-permute-start | bytes 3080 | tf_op jit(solution)/shard_map/ppermute | solution.py:28
  49.5 6.4 %collective-permute-start.22 = (f32[2,256]{1,0:T(2,128)S(1)}, f32[2,256]{1,0:T(2,128)S(1)}, u32[]{:S(2)}, u32[]{:S(2)}) collective-permute-start(f32[2,256]{1,0:T(2,128)S(1)} %get-tuple-element.84), channel_id=1, source_target_pairs={{0,3},{1,2},{2,1},{3,0},{4,7},{5,6},{6,5},{7,4},{8,11},{9,10},{10,... | collective-permute-start | bytes 6152 | tf_op jit(solution)/shard_map/ppermute | solution.py:28
  49.5 6.3 %collective-permute-start.21 = (f32[2,256]{1,0:T(2,128)S(1)}, f32[2,256]{1,0:T(2,128)S(1)}, u32[]{:S(2)}, u32[]{:S(2)}) collective-permute-start(f32[2,256]{1,0:T(2,128)S(1)} %get-tuple-element.84), channel_id=1, source_target_pairs={{0,2},{1,3},{2,0},{3,1},{4,6},{5,7},{6,4},{7,5},{8,10},{9,11},{10,... | collective-permute-start | bytes 6152 | tf_op jit(solution)/shard_map/ppermute | solution.py:28
  49.6 6.2 %collective-permute-start.20 = (f32[2,256]{1,0:T(2,128)S(1)}, f32[2,256]{1,0:T(2,128)S(1)}, u32[]{:S(2)}, u32[]{:S(2)}) collective-permute-start(f32[2,256]{1,0:T(2,128)S(1)} %get-tuple-element.84), channel_id=1, source_target_pairs={{0,1},{1,0},{2,3},{3,2},{4,5},{5,4},{6,7},{7,6},{8,9},{9,8},{10,11... | collective-permute-start | bytes 6152 | tf_op jit(solution)/shard_map/ppermute | solution.py:28
  51.4 10.5 %collective-permute-start.18 = (f32[32,256]{1,0:T(8,128)S(1)}, f32[32,256]{1,0:T(8,128)S(1)}, u32[]{:S(2)}, u32[]{:S(2)}) collective-permute-start(f32[32,256]{1,0:T(8,128)S(1)} %get-tuple-element.79), channel_id=1, source_target_pairs={{0,1},{1,2},{2,3},{3,4},{4,5},{5,6},{6,7},{7,8},{8,9},{9,10},{10,1... | collective-permute-start | bytes 98312 | tf_op jit(solution)/shard_map/ppermute | solution.py:23
  51.4 10.5 %collective-permute-start.19 = (f32[32,256]{1,0:T(8,128)S(1)}, f32[32,256]{1,0:T(8,128)S(1)}, u32[]{:S(2)}, u32[]{:S(2)}) collective-permute-start(f32[32,256]{1,0:T(8,128)S(1)} %get-tuple-element.80), channel_id=1, source_target_pairs={{0,15},{1,0},{2,1},{3,2},{4,3},{5,4},{6,5},{7,6},{8,7},{9,8},{10,9... | collective-permute-start | bytes 98312 | tf_op jit(solution)/shard_map/ppermute | solution.py:23
  55.9 5.4 %collective-permute-start.25 = (f32[2,256]{1,0:T(2,128)S(1)}, f32[2,256]{1,0:T(2,128)S(1)}, u32[]{:S(2)}, u32[]{:S(2)}) collective-permute-start(f32[2,256]{1,0:T(2,128)S(1)} %pad_maximum_fusion.1.refs_10_), channel_id=1, source_target_pairs={{0,12},{1,13},{2,14},{3,15},{4,8},{5,9},{6,10},{7,11},{8,4},{9,5},... | collective-permute-start | bytes 6152 | tf_op jit(solution)/shard_map/ppermute | solution.py:28
  56.5 4.8 %collective-permute-start.24 = (f32[2,256]{1,0:T(2,128)S(1)}, f32[2,256]{1,0:T(2,128)S(1)}, u32[]{:S(2)}, u32[]{:S(2)}) collective-permute-start(f32[2,256]{1,0:T(2,128)S(1)} %pad_maximum_fusion.1.refs_10_), channel_id=1, source_target_pairs={{0,8},{1,9},{2,10},{3,11},{4,12},{5,13},{6,14},{7,15},{8,0},{9,1},... | collective-permute-start | bytes 6152 | tf_op jit(solution)/shard_map/ppermute | solution.py:28
  57.6 4.3 %collective-permute-start.23 = (f32[2,256]{1,0:T(2,128)S(1)}, f32[2,256]{1,0:T(2,128)S(1)}, u32[]{:S(2)}, u32[]{:S(2)}) collective-permute-start(f32[2,256]{1,0:T(2,128)S(1)} %pad_maximum_fusion.1.refs_10_), channel_id=1, source_target_pairs={{0,4},{1,5},{2,6},{3,7},{4,0},{5,1},{6,2},{7,3},{8,12},{9,13},{10,... | collective-permute-start | bytes 6152 | tf_op jit(solution)/shard_map/ppermute | solution.py:28
  64.5 6.4 %collective-permute-start.30 = (f32[2,256]{1,0:T(2,128)S(1)}, f32[2,256]{1,0:T(2,128)S(1)}, u32[]{:S(2)}, u32[]{:S(2)}) collective-permute-start(f32[2,256]{1,0:T(2,128)S(1)} %get-tuple-element.93), channel_id=1, source_target_pairs={{0,3},{1,2},{2,1},{3,0},{4,7},{5,6},{6,5},{7,4},{8,11},{9,10},{10,... | collective-permute-start | bytes 6152 | tf_op jit(solution)/shard_map/ppermute | solution.py:28
  64.6 6.3 %collective-permute-start.29 = (f32[2,256]{1,0:T(2,128)S(1)}, f32[2,256]{1,0:T(2,128)S(1)}, u32[]{:S(2)}, u32[]{:S(2)}) collective-permute-start(f32[2,256]{1,0:T(2,128)S(1)} %get-tuple-element.93), channel_id=1, source_target_pairs={{0,2},{1,3},{2,0},{3,1},{4,6},{5,7},{6,4},{7,5},{8,10},{9,11},{10,... | collective-permute-start | bytes 6152 | tf_op jit(solution)/shard_map/ppermute | solution.py:28
  64.7 6.2 %collective-permute-start.28 = (f32[2,256]{1,0:T(2,128)S(1)}, f32[2,256]{1,0:T(2,128)S(1)}, u32[]{:S(2)}, u32[]{:S(2)}) collective-permute-start(f32[2,256]{1,0:T(2,128)S(1)} %get-tuple-element.93), channel_id=1, source_target_pairs={{0,1},{1,0},{2,3},{3,2},{4,5},{5,4},{6,7},{7,6},{8,9},{9,8},{10,11... | collective-permute-start | bytes 6152 | tf_op jit(solution)/shard_map/ppermute | solution.py:28
  66.4 10.5 %collective-permute-start.26 = (f32[64,256]{1,0:T(8,128)S(1)}, f32[64,256]{1,0:T(8,128)S(1)}, u32[]{:S(2)}, u32[]{:S(2)}) collective-permute-start(f32[64,256]{1,0:T(8,128)S(1)} %get-tuple-element.86), channel_id=1, source_target_pairs={{0,1},{1,2},{2,3},{3,4},{4,5},{5,6},{6,7},{7,8},{8,9},{9,10},{10,1... | collective-permute-start | bytes 196616 | tf_op jit(solution)/shard_map/ppermute | solution.py:23
  66.4 10.5 %collective-permute-start.27 = (f32[64,256]{1,0:T(8,128)S(1)}, f32[64,256]{1,0:T(8,128)S(1)}, u32[]{:S(2)}, u32[]{:S(2)}) collective-permute-start(f32[64,256]{1,0:T(8,128)S(1)} %get-tuple-element.87), channel_id=1, source_target_pairs={{0,15},{1,0},{2,1},{3,2},{4,3},{5,4},{6,5},{7,6},{8,7},{9,8},{10,9... | collective-permute-start | bytes 196616 | tf_op jit(solution)/shard_map/ppermute | solution.py:23
  70.9 5.4 %collective-permute-start.33 = (f32[2,256]{1,0:T(2,128)S(1)}, f32[2,256]{1,0:T(2,128)S(1)}, u32[]{:S(2)}, u32[]{:S(2)}) collective-permute-start(f32[2,256]{1,0:T(2,128)S(1)} %pad_maximum_fusion.2.refs_10_), channel_id=1, source_target_pairs={{0,12},{1,13},{2,14},{3,15},{4,8},{5,9},{6,10},{7,11},{8,4},{9,5},... | collective-permute-start | bytes 6152 | tf_op jit(solution)/shard_map/ppermute | solution.py:28
  71.6 4.8 %collective-permute-start.32 = (f32[2,256]{1,0:T(2,128)S(1)}, f32[2,256]{1,0:T(2,128)S(1)}, u32[]{:S(2)}, u32[]{:S(2)}) collective-permute-start(f32[2,256]{1,0:T(2,128)S(1)} %pad_maximum_fusion.2.refs_10_), channel_id=1, source_target_pairs={{0,8},{1,9},{2,10},{3,11},{4,12},{5,13},{6,14},{7,15},{8,0},{9,1},... | collective-permute-start | bytes 6152 | tf_op jit(solution)/shard_map/ppermute | solution.py:28
  72.7 4.3 %collective-permute-start.31 = (f32[2,256]{1,0:T(2,128)S(1)}, f32[2,256]{1,0:T(2,128)S(1)}, u32[]{:S(2)}, u32[]{:S(2)}) collective-permute-start(f32[2,256]{1,0:T(2,128)S(1)} %pad_maximum_fusion.2.refs_10_), channel_id=1, source_target_pairs={{0,4},{1,5},{2,6},{3,7},{4,0},{5,1},{6,2},{7,3},{8,12},{9,13},{10,... | collective-permute-start | bytes 6152 | tf_op jit(solution)/shard_map/ppermute | solution.py:28
  78.5 3.1 %collective-permute-start.36 = (f32[2,512]{1,0:T(2,128)S(1)}, f32[2,512]{1,0:T(2,128)S(1)}, u32[]{:S(2)}, u32[]{:S(2)}) collective-permute-start(f32[2,512]{1,0:T(2,128)S(1)} %get-tuple-element.98), channel_id=1, source_target_pairs={{0,3},{1,2},{2,1},{3,0},{4,7},{5,6},{6,5},{7,4},{8,11},{9,10},{10,... | collective-permute-start | bytes 12296 | tf_op jit(solution)/shard_map/ppermute | solution.py:28
  78.6 3.7 %collective-permute-start.35 = (f32[2,512]{1,0:T(2,128)S(1)}, f32[2,512]{1,0:T(2,128)S(1)}, u32[]{:S(2)}, u32[]{:S(2)}) collective-permute-start(f32[2,512]{1,0:T(2,128)S(1)} %get-tuple-element.98), channel_id=1, source_target_pairs={{0,2},{1,3},{2,0},{3,1},{4,6},{5,7},{6,4},{7,5},{8,10},{9,11},{10,... | collective-permute-start | bytes 12296 | tf_op jit(solution)/shard_map/ppermute | solution.py:28
  78.6 3.6 %collective-permute-start.34 = (f32[2,512]{1,0:T(2,128)S(1)}, f32[2,512]{1,0:T(2,128)S(1)}, u32[]{:S(2)}, u32[]{:S(2)}) collective-permute-start(f32[2,512]{1,0:T(2,128)S(1)} %get-tuple-element.98), channel_id=1, source_target_pairs={{0,1},{1,0},{2,3},{3,2},{4,5},{5,4},{6,7},{7,6},{8,9},{9,8},{10,11... | collective-permute-start | bytes 12296 | tf_op jit(solution)/shard_map/ppermute | solution.py:28
  82.3 5.5 %collective-permute-start.39 = (f32[2,512]{1,0:T(2,128)S(1)}, f32[2,512]{1,0:T(2,128)S(1)}, u32[]{:S(2)}, u32[]{:S(2)}) collective-permute-start(f32[2,512]{1,0:T(2,128)S(1)} %pad_maximum_fusion.refs_3_), channel_id=1, source_target_pairs={{0,12},{1,13},{2,14},{3,15},{4,8},{5,9},{6,10},{7,11},{8,4},{9,5},... | collective-permute-start | bytes 12296 | tf_op jit(solution)/shard_map/ppermute | solution.py:28
  84.7 4.5 %collective-permute-start.38 = (f32[2,512]{1,0:T(2,128)S(1)}, f32[2,512]{1,0:T(2,128)S(1)}, u32[]{:S(2)}, u32[]{:S(2)}) collective-permute-start(f32[2,512]{1,0:T(2,128)S(1)} %pad_maximum_fusion.refs_3_), channel_id=1, source_target_pairs={{0,8},{1,9},{2,10},{3,11},{4,12},{5,13},{6,14},{7,15},{8,0},{9,1},... | collective-permute-start | bytes 12296 | tf_op jit(solution)/shard_map/ppermute | solution.py:28
  85.8 3.6 %collective-permute-start.37 = (f32[2,512]{1,0:T(2,128)S(1)}, f32[2,512]{1,0:T(2,128)S(1)}, u32[]{:S(2)}, u32[]{:S(2)}) collective-permute-start(f32[2,512]{1,0:T(2,128)S(1)} %pad_maximum_fusion.refs_3_), channel_id=1, source_target_pairs={{0,4},{1,5},{2,6},{3,7},{4,0},{5,1},{6,2},{7,3},{8,12},{9,13},{10,... | collective-permute-start | bytes 12296 | tf_op jit(solution)/shard_map/ppermute | solution.py:28

commit v4 on v3

--- a/solution.py
+++ b/solution.py
@@ -65,7 +65,7 @@
         return jnp.maximum(outside, jnp.where((near < 0) | (near >= WINDOW), 1, 0))
 
     none = jnp.zeros((BLOCK, TAPS - 1), jnp.int32)
-    outside = lax.fori_loop(0, rows // BLOCK, one, none, unroll=min(2, rows // BLOCK))
+    outside = lax.fori_loop(0, rows // BLOCK, one, none, unroll=min(4, rows // BLOCK))
     far[...] = jnp.broadcast_to(jnp.max(outside, axis=0, keepdims=True), far.shape)
 
 
@@ -271,7 +271,7 @@
         source[pl.ds(pl.multiple_of(i * out_step + halo, 16), out_step), :] = fold(value)
         return carry
 
-    lax.fori_loop(0, raw.shape[0] // step, one, 0, unroll=2)
+    lax.fori_loop(0, raw.shape[0] // step, one, 0, unroll=min(8, raw.shape[0] // step))
     if pool:
         copy = pltpu.make_async_copy(skip, outer, sem)
         copy.start()
@@ -300,17 +300,24 @@
     )(*args)
 
 
+def phases(count):
+    steps, stride = [[1]], 2
+    while stride < count:
+        radix = 2 if ((count // stride).bit_length() - 1) % 2 else 4
+        steps.append([stride * i ^ 1 for i in range(1, radix)])
+        stride = stride * radix
+    return steps
+
+
 def gather_stats(stats, rows):
-    count = lax.axis_size(AXES)
-    pairs, held, stride = [stats], rows, 1
-    while stride < count:
-        if stride > 1:
+    pairs, held = [stats], rows
+    steps = phases(lax.axis_size(AXES))
+    for at, masks in enumerate(steps):
+        if at:
             mean, squares = combined(pairs, held)
             held = held * len(pairs)
             pairs = [jnp.concatenate([mean, squares], axis=0)]
-        radix = min(4, count // stride)
-        pairs = pairs + [swapped(pairs[0], stride * i) for i in range(1, radix)]
-        stride = stride * radix
+        pairs = pairs + [swapped(pairs[0], mask) for mask in masks]
     return pairs, held
 
 

time: 90.4 us -> 83.4 us (0.923)
  starting transfers between devices: 55.1 us -> 41.3 us
  waiting for transfers between devices: 11.7 us -> 20.3 us
  Pallas kernels: 22.3 us -> 20.6 us
    ppermute x30 -> x25, starting transfers between devices: 31.8 us -> 17.9 us  [swapped(): lax.ppermute(value, AXES, [(source, source ^ mask) for source in range(co...]
    ppermute x30 -> x25, waiting for transfers between devices: 9.84 us -> 18.4 us  [swapped(): lax.ppermute(value, AXES, [(source, source ^ mask) for source in range(co...]
    pallas_call x9, Pallas kernels: 22.3 us -> 20.6 us  [call(): pl.pallas_call(body, out_shape=outs, in_specs=[HERE if i in here else VM...]
  transfers between devices with their start and end apart: 40 -> 35, of which waited for: 13 -> 13; matrix products, arithmetic and copies ran while one was open for 0% -> 0% of each run, Pallas kernels for 5% -> 6%
where the time goes in v4:
time: 83.4 us; the launch traced here: 83.3 us
  starting transfers between devices  41.3 us (50%)
  Pallas kernels  20.6 us (25%)
  waiting for transfers between devices  20.3 us (24%)
  between operations  0.86 us (1%)
    ppermute x10, starting transfers between devices, shifted(): lax.ppermute(value, AXES, [(source, (source + steps) % count) for source...  23.4 us
    pallas_call x9, Pallas kernels, call(): pl.pallas_call(body, out_shape=outs, in_specs=[HERE if i in here else VM...  20.6 us
    ppermute x25, waiting for transfers between devices, swapped(): lax.ppermute(value, AXES, [(source, source ^ mask) for source in range(co...  18.4 us
    ppermute x25, starting transfers between devices, swapped(): lax.ppermute(value, AXES, [(source, source ^ mask) for source in range(co...  17.9 us
    ppermute x10, waiting for transfers between devices, shifted(): lax.ppermute(value, AXES, [(source, (source + steps) % count) for source...  1.9 us
  transfers between devices with their start and end apart: 35, of which 13 were waited for; matrix products, arithmetic and copies ran while one was open for 0% of the time, Pallas kernels for 6%

profile of v4, /device:TPU:0, one launch (start us, length us, event | category | flops | bytes accessed | tf_op | source)
XLA Modules:
  0.0 83.3 jit_solution(461997233548026484)
XLA Ops:
  0.6 0.9 %shard_map.229 = (bf16[80,128]{1,0:T(8,128)(2,1)S(1)}, bf16[80,128]{1,0:T(8,128)(2,1)S(1)}) custom-call(bf16[64,2048]{1,0:T(8,128)(2,1)} %bitcast.28, s32[1,2,64]{2,1,0:T(2,128)} %sends_a.1, s32[1,2,32]{2,1,0:T(2,128)} %sends_b.1, s32[1,2,16]{2,1,0:T(2,128)} %sends_c.1), custom_call_target="tpu_custom_call" | custom-call | tf_op jit(solution)/shard_map/pallas_call | solution.py:292
  1.6 5.5 %collective-permute-start.1 = (bf16[80,128]{1,0:T(8,128)(2,1)S(1)}, bf16[80,128]{1,0:T(8,128)(2,1)S(1)}, u32[]{:S(2)}, u32[]{:S(2)}) collective-permute-start(bf16[80,128]{1,0:T(8,128)(2,1)S(1)} %get-tuple-element.53), channel_id=1, source_target_pairs={{0,15},{1,0},{2,1},{3,2},{4,3},{5,4},{6,5},{7,6},{8,7},{9,8},{10,9... | collective-permute-start | bytes 61448 | tf_op jit(solution)/shard_map/ppermute | solution.py:23
  7.1 4.0 %shard_map.230 = (s32[9,2048]{1,0:T(8,128)S(1)}, s32[9,512]{1,0:T(8,128)S(1)}, s32[9,128]{1,0:T(8,128)S(1)}, bf16[576,128]{1,0:T(8,128)(2,1)S(1)}, bf16[1152,128...) custom-call(bf16[80,128]{1,0:T(8,128)(2,1)S(1)} %get-tuple-element.5, ...), custom_call_target="tpu_custom_call" | custom-call | bytes 8388608 | tf_op jit(solution)/shard_map/pallas_call | solution.py:292
  11.1 0.0 collective-permute-done.1.right
  11.1 1.9 %collective-permute-done.left = bf16[80,128]{1,0:T(8,128)(2,1)S(1)} collective-permute-done((bf16[80,128]{1,0:T(8,128)(2,1)S(1)}, bf16[80,128]{1,0:T(8,128)(2,1)S(1)}, u32[]{:S(2)}, u32[]{:S(2)}) %collective-permute-start) | collective-permute-done | bytes 20512 | tf_op jit(solution)/shard_map/ppermute | solution.py:23
  13.0 3.7 %shard_map.231 = (f32[2048,128]{1,0:T(8,128)S(1)}, f32[2,128]{1,0:T(2,128)S(1)}, f32[64,128]{1,0:T(8,128)S(1)}, f32[64,128]{1,0:T(8,128)S(1)}, f32[2,128]{1,0:T(2,128)S(1)}) custom-call(bf16[2048,64]{1,0:T(8,128)(2,1)S(1)} %get-tuple-element.52.feat, bf16[80,128]{1,0:T(8,128)(2,1)S(1)} %collective-permute-done.left, ...), custom_call_target="tpu_custom_call" | custom-call | tf_op jit(solution)/shard_map/pallas_call | solution.py:292
  16.7 0.1 collective-permute-start.4
  16.8 1.1 %collective-permute-done.4 = f32[2,128]{1,0:T(2,128)S(1)} collective-permute-done((f32[2,128]{1,0:T(2,128)S(1)}, f32[2,128]{1,0:T(2,128)S(1)}, u32[]{:S(2)}, u32[]{:S(2)}) %collective-permute-start.4) | collective-permute-done | bytes 1056 | tf_op jit(solution)/shard_map/ppermute | solution.py:28
  17.9 0.1 collective-permute-start.5
  18.0 0.2 collective-permute-start.2
  18.2 4.3 %collective-permute-start.3 = (f32[64,128]{1,0:T(8,128)S(1)}, f32[64,128]{1,0:T(8,128)S(1)}, u32[]{:S(2)}, u32[]{:S(2)}) collective-permute-start(f32[64,128]{1,0:T(8,128)S(1)} %get-tuple-element.60), channel_id=1, source_target_pairs={{0,15},{1,0},{2,1},{3,2},{4,3},{5,4},{6,5},{7,6},{8,7},{9,8},{10,9... | collective-permute-start | bytes 98312 | tf_op jit(solution)/shard_map/ppermute | solution.py:23
  22.5 0.1 collective-permute-start.8
  22.6 0.1 collective-permute-start.7
  22.7 2.3 %collective-permute-start.6 = (f32[2,128]{1,0:T(2,128)S(1)}, f32[2,128]{1,0:T(2,128)S(1)}, u32[]{:S(2)}, u32[]{:S(2)}) collective-permute-start(f32[2,128]{1,0:T(2,128)S(1)} %pad_maximum_fusion.7.refs_10_), channel_id=1, source_target_pairs={{0,5},{1,4},{2,7},{3,6},{4,1},{5,0},{6,3},{7,2},{8,13},{9,12},{10,... | collective-permute-start | bytes 3080 | tf_op jit(solution)/shard_map/ppermute | solution.py:28
  25.0 2.4 %collective-permute-done.8.refs_13_ = f32[2,128]{1,0:T(2,128)S(1)} collective-permute-done((f32[2,128]{1,0:T(2,128)S(1)}, f32[2,128]{1,0:T(2,128)S(1)}, u32[]{:S(2)}, u32[]{:S(2)}) %collective-permute-start.8) | collective-permute-done | bytes 1056 | tf_op jit(solution)/shard_map/ppermute | solution.py:28
  27.4 0.0 collective-permute-done.7.refs_12_
  27.4 0.0 collective-permute-done.6.refs_11_
  27.4 0.0 collective-permute-done.2.refs_1_
  27.4 0.0 collective-permute-done.3.refs_2_
  27.4 4.3 %shard_map.232 = (f32[2048,128]{1,0:T(8,128)S(1)}, f32[2,128]{1,0:T(2,128)S(1)}, f32[128,128]{1,0:T(8,128)S(1)}, f32[128,128]{1,0:T(8,128)S(1)}) custom-call(f32[2048,128]{1,0:T(8,128)S(1)} %get-tuple-element.58.refs_0_, f32[64,128]{1,0:T(8,128)S(1)} %collective-permute-done.2.refs_1_, f32[64,128]{1,0:T(8,128)S(1)} %collective-permute-done.3.refs_2_, ...), custom_call_target="tpu_custom_call" | custom-call | tf_op jit(solution)/shard_map/pallas_call | solution.py:292
  31.7 0.7 collective-permute-start.11
  32.5 0.8 collective-permute-done.11
  33.3 0.4 collective-permute-start.12
  33.7 0.4 collective-permute-start.9
  34.1 4.1 %collective-permute-start.10 = (f32[128,128]{1,0:T(8,128)S(1)}, f32[128,128]{1,0:T(8,128)S(1)}, u32[]{:S(2)}, u32[]{:S(2)}) collective-permute-start(f32[128,128]{1,0:T(8,128)S(1)} %get-tuple-element.68), channel_id=1, source_target_pairs={{0,15},{1,0},{2,1},{3,2},{4,3},{5,4},{6,5},{7,6},{8,7},{9,8},{10,9... | collective-permute-start | bytes 196616 | tf_op jit(solution)/shard_map/ppermute | solution.py:23
  38.2 0.6 collective-permute-start.15
  38.8 0.8 %collective-permute-start.14 = (f32[2,128]{1,0:T(2,128)S(1)}, f32[2,128]{1,0:T(2,128)S(1)}, u32[]{:S(2)}, u32[]{:S(2)}) collective-permute-start(f32[2,128]{1,0:T(2,128)S(1)} %pad_maximum_fusion.9.refs_10_), channel_id=1, source_target_pairs={{0,9},{1,8},{2,11},{3,10},{4,13},{5,12},{6,15},{7,14},{8,1},{9,0},... | collective-permute-start | bytes 3080 | tf_op jit(solution)/shard_map/ppermute | solution.py:28
  39.6 0.9 %collective-permute-start.13 = (f32[2,128]{1,0:T(2,128)S(1)}, f32[2,128]{1,0:T(2,128)S(1)}, u32[]{:S(2)}, u32[]{:S(2)}) collective-permute-start(f32[2,128]{1,0:T(2,128)S(1)} %pad_maximum_fusion.9.refs_10_), channel_id=1, source_target_pairs={{0,5},{1,4},{2,7},{3,6},{4,1},{5,0},{6,3},{7,2},{8,13},{9,12},{10,... | collective-permute-start | bytes 3080 | tf_op jit(solution)/shard_map/ppermute | solution.py:28
  40.5 0.7 shard_map.233
  41.2 1.8 %collective-permute-done.15.refs_13_ = f32[2,128]{1,0:T(2,128)S(1)} collective-permute-done((f32[2,128]{1,0:T(2,128)S(1)}, f32[2,128]{1,0:T(2,128)S(1)}, u32[]{:S(2)}, u32[]{:S(2)}) %collective-permute-start.15) | collective-permute-done | bytes 1056 | tf_op jit(solution)/shard_map/ppermute | solution.py:28
  43.1 0.0 collective-permute-done.14.refs_12_
  43.1 0.0 collective-permute-done.13.refs_11_
  43.1 0.0 collective-permute-done.9.refs_1_
  43.1 2.6 %shard_map.234 = (bf16[2048,128]{1,0:T(8,128)(2,1)}, f32[512,256]{1,0:T(8,128)S(1)}, f32[2,256]{1,0:T(2,128)S(1)}, f32[32,256]{1,0:T(8,128)S(1)}, f32[32,256]{1,0:T(8,128)S(1)}) custom-call(f32[2048,128]{1,0:T(8,128)S(1)} %get-tuple-element.66.refs_0_, f32[128,128]{1,0:T(8,128)S(1)} %collective-permute-done.9.refs_1_, ...), custom_call_target="tpu_custom_call" | custom-call | tf_op jit(solution)/shard_map/pallas_call | solution.py:292
  45.7 0.7 collective-permute-start.18
  46.5 0.8 collective-permute-done.18
  47.3 0.1 collective-permute-start.19
  47.4 0.4 collective-permute-start.16
  47.8 4.1 %collective-permute-start.17 = (f32[32,256]{1,0:T(8,128)S(1)}, f32[32,256]{1,0:T(8,128)S(1)}, u32[]{:S(2)}, u32[]{:S(2)}) collective-permute-start(f32[32,256]{1,0:T(8,128)S(1)} %get-tuple-element.80), channel_id=1, source_target_pairs={{0,15},{1,0},{2,1},{3,2},{4,3},{5,4},{6,5},{7,6},{8,7},{9,8},{10,9... | collective-permute-start | bytes 98312 | tf_op jit(solution)/shard_map/ppermute | solution.py:23
  51.9 0.9 %collective-permute-start.22 = (f32[2,256]{1,0:T(2,128)S(1)}, f32[2,256]{1,0:T(2,128)S(1)}, u32[]{:S(2)}, u32[]{:S(2)}) collective-permute-start(f32[2,256]{1,0:T(2,128)S(1)} %pad_maximum_fusion.3.refs_10_), channel_id=1, source_target_pairs={{0,13},{1,12},{2,15},{3,14},{4,9},{5,8},{6,11},{7,10},{8,5},{9,4},... | collective-permute-start | bytes 6152 | tf_op jit(solution)/shard_map/ppermute | solution.py:28
  52.8 0.8 %collective-permute-start.21 = (f32[2,256]{1,0:T(2,128)S(1)}, f32[2,256]{1,0:T(2,128)S(1)}, u32[]{:S(2)}, u32[]{:S(2)}) collective-permute-start(f32[2,256]{1,0:T(2,128)S(1)} %pad_maximum_fusion.3.refs_10_), channel_id=1, source_target_pairs={{0,9},{1,8},{2,11},{3,10},{4,13},{5,12},{6,15},{7,14},{8,1},{9,0},... | collective-permute-start | bytes 6152 | tf_op jit(solution)/shard_map/ppermute | solution.py:28
  53.6 0.9 %collective-permute-start.20 = (f32[2,256]{1,0:T(2,128)S(1)}, f32[2,256]{1,0:T(2,128)S(1)}, u32[]{:S(2)}, u32[]{:S(2)}) collective-permute-start(f32[2,256]{1,0:T(2,128)S(1)} %pad_maximum_fusion.3.refs_10_), channel_id=1, source_target_pairs={{0,5},{1,4},{2,7},{3,6},{4,1},{5,0},{6,3},{7,2},{8,13},{9,12},{10,... | collective-permute-start | bytes 6152 | tf_op jit(solution)/shard_map/ppermute | solution.py:28
  54.5 2.3 %collective-permute-done.22.refs_13_ = f32[2,256]{1,0:T(2,128)S(1)} collective-permute-done((f32[2,256]{1,0:T(2,128)S(1)}, f32[2,256]{1,0:T(2,128)S(1)}, u32[]{:S(2)}, u32[]{:S(2)}) %collective-permute-start.22) | collective-permute-done | bytes 2080 | tf_op jit(solution)/shard_map/ppermute | solution.py:28
  56.8 2.4 %shard_map.235 = (f32[512,256]{1,0:T(8,128)S(1)}, f32[2,256]{1,0:T(2,128)S(1)}, f32[64,256]{1,0:T(8,128)S(1)}, f32[64,256]{1,0:T(8,128)S(1)}) custom-call(f32[512,256]{1,0:T(8,128)S(1)} %get-tuple-element.78.refs_0_, f32[32,256]{1,0:T(8,128)S(1)} %collective-permute-done.16.refs_1_, f32[32,256]{1,0:T(8,128)S(1)} %collective-permute-done.17.refs_2_, ...), custom_call_target="tpu_custom_call" | custom-call | tf_op jit(solution)/shard_map/pallas_call | solution.py:292
  59.2 0.7 collective-permute-start.25
  60.0 0.8 collective-permute-done.25
  60.8 0.1 collective-permute-start.26
  61.0 0.3 collective-permute-start.23
  61.3 4.1 %collective-permute-start.24 = (f32[64,256]{1,0:T(8,128)S(1)}, f32[64,256]{1,0:T(8,128)S(1)}, u32[]{:S(2)}, u32[]{:S(2)}) collective-permute-start(f32[64,256]{1,0:T(8,128)S(1)} %get-tuple-element.87), channel_id=1, source_target_pairs={{0,15},{1,0},{2,1},{3,2},{4,3},{5,4},{6,5},{7,6},{8,7},{9,8},{10,9... | collective-permute-start | bytes 196616 | tf_op jit(solution)/shard_map/ppermute | solution.py:23
  65.4 0.9 %collective-permute-start.29 = (f32[2,256]{1,0:T(2,128)S(1)}, f32[2,256]{1,0:T(2,128)S(1)}, u32[]{:S(2)}, u32[]{:S(2)}) collective-permute-start(f32[2,256]{1,0:T(2,128)S(1)} %pad_maximum_fusion.5.refs_10_), channel_id=1, source_target_pairs={{0,13},{1,12},{2,15},{3,14},{4,9},{5,8},{6,11},{7,10},{8,5},{9,4},... | collective-permute-start | bytes 6152 | tf_op jit(solution)/shard_map/ppermute | solution.py:28
  66.3 0.8 %collective-permute-start.28 = (f32[2,256]{1,0:T(2,128)S(1)}, f32[2,256]{1,0:T(2,128)S(1)}, u32[]{:S(2)}, u32[]{:S(2)}) collective-permute-start(f32[2,256]{1,0:T(2,128)S(1)} %pad_maximum_fusion.5.refs_10_), channel_id=1, source_target_pairs={{0,9},{1,8},{2,11},{3,10},{4,13},{5,12},{6,15},{7,14},{8,1},{9,0},... | collective-permute-start | bytes 6152 | tf_op jit(solution)/shard_map/ppermute | solution.py:28
  67.1 0.9 %collective-permute-start.27 = (f32[2,256]{1,0:T(2,128)S(1)}, f32[2,256]{1,0:T(2,128)S(1)}, u32[]{:S(2)}, u32[]{:S(2)}) collective-permute-start(f32[2,256]{1,0:T(2,128)S(1)} %pad_maximum_fusion.5.refs_10_), channel_id=1, source_target_pairs={{0,5},{1,4},{2,7},{3,6},{4,1},{5,0},{6,3},{7,2},{8,13},{9,12},{10,... | collective-permute-start | bytes 6152 | tf_op jit(solution)/shard_map/ppermute | solution.py:28
  68.0 2.3 %collective-permute-done.29.refs_13_ = f32[2,256]{1,0:T(2,128)S(1)} collective-permute-done((f32[2,256]{1,0:T(2,128)S(1)}, f32[2,256]{1,0:T(2,128)S(1)}, u32[]{:S(2)}, u32[]{:S(2)}) %collective-permute-start.29) | collective-permute-done | bytes 2080 | tf_op jit(solution)/shard_map/ppermute | solution.py:28
  70.3 1.1 %shard_map.236 = (bf16[512,256]{1,0:T(8,128)(2,1)}, f32[128,512]{1,0:T(8,128)S(1)}, f32[2,512]{1,0:T(2,128)S(1)}) custom-call(f32[512,256]{1,0:T(8,128)S(1)} %get-tuple-element.85.refs_0_, f32[64,256]{1,0:T(8,128)S(1)} %collective-permute-done.23.refs_1_, f32[64,256]{1,0:T(8,128)S(1)} %collective-permute-done.24.refs_2_, ...), custom_call_target="tpu_custom_call" | custom-call | tf_op jit(solution)/shard_map/pallas_call | solution.py:292
  71.5 0.7 collective-permute-start.30
  72.2 0.8 collective-permute-done.30
  73.1 0.1 collective-permute-start.31
  73.2 3.0 %collective-permute-done.31 = f32[2,512]{1,0:T(2,128)S(1)} collective-permute-done((f32[2,512]{1,0:T(2,128)S(1)}, f32[2,512]{1,0:T(2,128)S(1)}, u32[]{:S(2)}, u32[]{:S(2)}) %collective-permute-start.31) | collective-permute-done | bytes 4128 | tf_op jit(solution)/shard_map/ppermute | solution.py:28
  76.2 2.4 %collective-permute-start.34 = (f32[2,512]{1,0:T(2,128)S(1)}, f32[2,512]{1,0:T(2,128)S(1)}, u32[]{:S(2)}, u32[]{:S(2)}) collective-permute-start(f32[2,512]{1,0:T(2,128)S(1)} %pad_maximum_fusion.1.refs_3_), channel_id=1, source_target_pairs={{0,13},{1,12},{2,15},{3,14},{4,9},{5,8},{6,11},{7,10},{8,5},{9,4},... | collective-permute-start | bytes 12296 | tf_op jit(solution)/shard_map/ppermute | solution.py:28
  78.6 0.8 %collective-permute-start.33 = (f32[2,512]{1,0:T(2,128)S(1)}, f32[2,512]{1,0:T(2,128)S(1)}, u32[]{:S(2)}, u32[]{:S(2)}) collective-permute-start(f32[2,512]{1,0:T(2,128)S(1)} %pad_maximum_fusion.1.refs_3_), channel_id=1, source_target_pairs={{0,9},{1,8},{2,11},{3,10},{4,13},{5,12},{6,15},{7,14},{8,1},{9,0},... | collective-permute-start | bytes 12296 | tf_op jit(solution)/shard_map/ppermute | solution.py:28
  79.4 0.9 %collective-permute-start.32 = (f32[2,512]{1,0:T(2,128)S(1)}, f32[2,512]{1,0:T(2,128)S(1)}, u32[]{:S(2)}, u32[]{:S(2)}) collective-permute-start(f32[2,512]{1,0:T(2,128)S(1)} %pad_maximum_fusion.1.refs_3_), channel_id=1, source_target_pairs={{0,5},{1,4},{2,7},{3,6},{4,1},{5,0},{6,3},{7,2},{8,13},{9,12},{10,... | collective-permute-start | bytes 12296 | tf_op jit(solution)/shard_map/ppermute | solution.py:28
  80.3 0.8 collective-permute-done.34.refs_6_
  81.1 1.4 %collective-permute-done.33.refs_5_ = f32[2,512]{1,0:T(2,128)S(1)} collective-permute-done((f32[2,512]{1,0:T(2,128)S(1)}, f32[2,512]{1,0:T(2,128)S(1)}, u32[]{:S(2)}, u32[]{:S(2)}) %collective-permute-start.33) | collective-permute-done | bytes 4128 | tf_op jit(solution)/shard_map/ppermute | solution.py:28
  82.5 0.8 shard_map.237
  (35 shorter events, 0.3 us)
Async XLA Ops:
  1.6 9.5 %collective-permute-start.1 = (bf16[80,128]{1,0:T(8,128)(2,1)S(1)}, bf16[80,128]{1,0:T(8,128)(2,1)S(1)}, u32[]{:S(2)}, u32[]{:S(2)}) collective-permute-start(bf16[80,128]{1,0:T(8,128)(2,1)S(1)} %get-tuple-element.53), channel_id=1, source_target_pairs={{0,15},{1,0},{2,1},{3,2},{4,3},{5,4},{6,5},{7,6},{8,7},{9,8},{10,9... | collective-permute-start | bytes 61448 | tf_op jit(solution)/shard_map/ppermute | solution.py:23
  7.1 5.9 %collective-permute-start = (bf16[80,128]{1,0:T(8,128)(2,1)S(1)}, bf16[80,128]{1,0:T(8,128)(2,1)S(1)}, u32[]{:S(2)}, u32[]{:S(2)}) collective-permute-start(bf16[80,128]{1,0:T(8,128)(2,1)S(1)} %get-tuple-element.51.refs_0_), channel_id=1, source_target_pairs={{0,1},{1,2},{2,3},{3,4},{4,5},{5,6},{6,7},{7,8},{8,9},{9,10},{10,1... | collective-permute-start | bytes 61448 | tf_op jit(solution)/shard_map/ppermute | solution.py:23
  16.7 1.2 %collective-permute-start.4 = (f32[2,128]{1,0:T(2,128)S(1)}, f32[2,128]{1,0:T(2,128)S(1)}, u32[]{:S(2)}, u32[]{:S(2)}) collective-permute-start(f32[2,128]{1,0:T(2,128)S(1)} %get-tuple-element.65), channel_id=1, source_target_pairs={{0,1},{1,0},{2,3},{3,2},{4,5},{5,4},{6,7},{7,6},{8,9},{9,8},{10,11... | collective-permute-start | bytes 3080 | tf_op jit(solution)/shard_map/ppermute | solution.py:28
  17.9 4.6 %collective-permute-start.5 = (f32[2,128]{1,0:T(2,128)S(1)}, f32[2,128]{1,0:T(2,128)S(1)}, u32[]{:S(2)}, u32[]{:S(2)}) collective-permute-start(f32[2,128]{1,0:T(2,128)S(1)} %pad_maximum_fusion.6), channel_id=1, source_target_pairs={{0,3},{1,2},{2,1},{3,0},{4,7},{5,6},{6,5},{7,4},{8,11},{9,10},{10,... | collective-permute-start | bytes 3080 | tf_op jit(solution)/shard_map/ppermute | solution.py:28
  18.0 9.4 %collective-permute-start.2 = (f32[64,128]{1,0:T(8,128)S(1)}, f32[64,128]{1,0:T(8,128)S(1)}, u32[]{:S(2)}, u32[]{:S(2)}) collective-permute-start(f32[64,128]{1,0:T(8,128)S(1)} %get-tuple-element.59), channel_id=1, source_target_pairs={{0,1},{1,2},{2,3},{3,4},{4,5},{5,6},{6,7},{7,8},{8,9},{9,10},{10,1... | collective-permute-start | bytes 98312 | tf_op jit(solution)/shard_map/ppermute | solution.py:23
  18.2 9.2 %collective-permute-start.3 = (f32[64,128]{1,0:T(8,128)S(1)}, f32[64,128]{1,0:T(8,128)S(1)}, u32[]{:S(2)}, u32[]{:S(2)}) collective-permute-start(f32[64,128]{1,0:T(8,128)S(1)} %get-tuple-element.60), channel_id=1, source_target_pairs={{0,15},{1,0},{2,1},{3,2},{4,3},{5,4},{6,5},{7,6},{8,7},{9,8},{10,9... | collective-permute-start | bytes 98312 | tf_op jit(solution)/shard_map/ppermute | solution.py:23
  22.5 4.9 %collective-permute-start.8 = (f32[2,128]{1,0:T(2,128)S(1)}, f32[2,128]{1,0:T(2,128)S(1)}, u32[]{:S(2)}, u32[]{:S(2)}) collective-permute-start(f32[2,128]{1,0:T(2,128)S(1)} %pad_maximum_fusion.7.refs_10_), channel_id=1, source_target_pairs={{0,13},{1,12},{2,15},{3,14},{4,9},{5,8},{6,11},{7,10},{8,5},{9,4},... | collective-permute-start | bytes 3080 | tf_op jit(solution)/shard_map/ppermute | solution.py:28
  22.6 4.8 %collective-permute-start.7 = (f32[2,128]{1,0:T(2,128)S(1)}, f32[2,128]{1,0:T(2,128)S(1)}, u32[]{:S(2)}, u32[]{:S(2)}) collective-permute-start(f32[2,128]{1,0:T(2,128)S(1)} %pad_maximum_fusion.7.refs_10_), channel_id=1, source_target_pairs={{0,9},{1,8},{2,11},{3,10},{4,13},{5,12},{6,15},{7,14},{8,1},{9,0},... | collective-permute-start | bytes 3080 | tf_op jit(solution)/shard_map/ppermute | solution.py:28
  22.7 4.7 %collective-permute-start.6 = (f32[2,128]{1,0:T(2,128)S(1)}, f32[2,128]{1,0:T(2,128)S(1)}, u32[]{:S(2)}, u32[]{:S(2)}) collective-permute-start(f32[2,128]{1,0:T(2,128)S(1)} %pad_maximum_fusion.7.refs_10_), channel_id=1, source_target_pairs={{0,5},{1,4},{2,7},{3,6},{4,1},{5,0},{6,3},{7,2},{8,13},{9,12},{10,... | collective-permute-start | bytes 3080 | tf_op jit(solution)/shard_map/ppermute | solution.py:28
  31.7 1.5 %collective-permute-start.11 = (f32[2,128]{1,0:T(2,128)S(1)}, f32[2,128]{1,0:T(2,128)S(1)}, u32[]{:S(2)}, u32[]{:S(2)}) collective-permute-start(f32[2,128]{1,0:T(2,128)S(1)} %get-tuple-element.76), channel_id=1, source_target_pairs={{0,1},{1,0},{2,3},{3,2},{4,5},{5,4},{6,7},{7,6},{8,9},{9,8},{10,11... | collective-permute-start | bytes 3080 | tf_op jit(solution)/shard_map/ppermute | solution.py:28
  33.3 4.8 %collective-permute-start.12 = (f32[2,128]{1,0:T(2,128)S(1)}, f32[2,128]{1,0:T(2,128)S(1)}, u32[]{:S(2)}, u32[]{:S(2)}) collective-permute-start(f32[2,128]{1,0:T(2,128)S(1)} %pad_maximum_fusion.8), channel_id=1, source_target_pairs={{0,3},{1,2},{2,1},{3,0},{4,7},{5,6},{6,5},{7,4},{8,11},{9,10},{10,... | collective-permute-start | bytes 3080 | tf_op jit(solution)/shard_map/ppermute | solution.py:28
  33.7 9.3 %collective-permute-start.9 = (f32[128,128]{1,0:T(8,128)S(1)}, f32[128,128]{1,0:T(8,128)S(1)}, u32[]{:S(2)}, u32[]{:S(2)}) collective-permute-start(f32[128,128]{1,0:T(8,128)S(1)} %get-tuple-element.67), channel_id=1, source_target_pairs={{0,1},{1,2},{2,3},{3,4},{4,5},{5,6},{6,7},{7,8},{8,9},{9,10},{10,1... | collective-permute-start | bytes 196616 | tf_op jit(solution)/shard_map/ppermute | solution.py:23
  34.1 9.0 %collective-permute-start.10 = (f32[128,128]{1,0:T(8,128)S(1)}, f32[128,128]{1,0:T(8,128)S(1)}, u32[]{:S(2)}, u32[]{:S(2)}) collective-permute-start(f32[128,128]{1,0:T(8,128)S(1)} %get-tuple-element.68), channel_id=1, source_target_pairs={{0,15},{1,0},{2,1},{3,2},{4,3},{5,4},{6,5},{7,6},{8,7},{9,8},{10,9... | collective-permute-start | bytes 196616 | tf_op jit(solution)/shard_map/ppermute | solution.py:23
  38.2 4.9 %collective-permute-start.15 = (f32[2,128]{1,0:T(2,128)S(1)}, f32[2,128]{1,0:T(2,128)S(1)}, u32[]{:S(2)}, u32[]{:S(2)}) collective-permute-start(f32[2,128]{1,0:T(2,128)S(1)} %pad_maximum_fusion.9.refs_10_), channel_id=1, source_target_pairs={{0,13},{1,12},{2,15},{3,14},{4,9},{5,8},{6,11},{7,10},{8,5},{9,4},... | collective-permute-start | bytes 3080 | tf_op jit(solution)/shard_map/ppermute | solution.py:28
  38.8 4.3 %collective-permute-start.14 = (f32[2,128]{1,0:T(2,128)S(1)}, f32[2,128]{1,0:T(2,128)S(1)}, u32[]{:S(2)}, u32[]{:S(2)}) collective-permute-start(f32[2,128]{1,0:T(2,128)S(1)} %pad_maximum_fusion.9.refs_10_), channel_id=1, source_target_pairs={{0,9},{1,8},{2,11},{3,10},{4,13},{5,12},{6,15},{7,14},{8,1},{9,0},... | collective-permute-start | bytes 3080 | tf_op jit(solution)/shard_map/ppermute | solution.py:28
  39.6 3.4 %collective-permute-start.13 = (f32[2,128]{1,0:T(2,128)S(1)}, f32[2,128]{1,0:T(2,128)S(1)}, u32[]{:S(2)}, u32[]{:S(2)}) collective-permute-start(f32[2,128]{1,0:T(2,128)S(1)} %pad_maximum_fusion.9.refs_10_), channel_id=1, source_target_pairs={{0,5},{1,4},{2,7},{3,6},{4,1},{5,0},{6,3},{7,2},{8,13},{9,12},{10,... | collective-permute-start | bytes 3080 | tf_op jit(solution)/shard_map/ppermute | solution.py:28
  45.7 1.6 %collective-permute-start.18 = (f32[2,256]{1,0:T(2,128)S(1)}, f32[2,256]{1,0:T(2,128)S(1)}, u32[]{:S(2)}, u32[]{:S(2)}) collective-permute-start(f32[2,256]{1,0:T(2,128)S(1)} %get-tuple-element.84), channel_id=1, source_target_pairs={{0,1},{1,0},{2,3},{3,2},{4,5},{5,4},{6,7},{7,6},{8,9},{9,8},{10,11... | collective-permute-start | bytes 6152 | tf_op jit(solution)/shard_map/ppermute | solution.py:28
  47.3 4.6 %collective-permute-start.19 = (f32[2,256]{1,0:T(2,128)S(1)}, f32[2,256]{1,0:T(2,128)S(1)}, u32[]{:S(2)}, u32[]{:S(2)}) collective-permute-start(f32[2,256]{1,0:T(2,128)S(1)} %pad_maximum_fusion.2), channel_id=1, source_target_pairs={{0,3},{1,2},{2,1},{3,0},{4,7},{5,6},{6,5},{7,4},{8,11},{9,10},{10,... | collective-permute-start | bytes 6152 | tf_op jit(solution)/shard_map/ppermute | solution.py:28
  47.4 9.4 %collective-permute-start.16 = (f32[32,256]{1,0:T(8,128)S(1)}, f32[32,256]{1,0:T(8,128)S(1)}, u32[]{:S(2)}, u32[]{:S(2)}) collective-permute-start(f32[32,256]{1,0:T(8,128)S(1)} %get-tuple-element.79), channel_id=1, source_target_pairs={{0,1},{1,2},{2,3},{3,4},{4,5},{5,6},{6,7},{7,8},{8,9},{9,10},{10,1... | collective-permute-start | bytes 98312 | tf_op jit(solution)/shard_map/ppermute | solution.py:23
  47.8 9.0 %collective-permute-start.17 = (f32[32,256]{1,0:T(8,128)S(1)}, f32[32,256]{1,0:T(8,128)S(1)}, u32[]{:S(2)}, u32[]{:S(2)}) collective-permute-start(f32[32,256]{1,0:T(8,128)S(1)} %get-tuple-element.80), channel_id=1, source_target_pairs={{0,15},{1,0},{2,1},{3,2},{4,3},{5,4},{6,5},{7,6},{8,7},{9,8},{10,9... | collective-permute-start | bytes 98312 | tf_op jit(solution)/shard_map/ppermute | solution.py:23
  51.9 4.9 %collective-permute-start.22 = (f32[2,256]{1,0:T(2,128)S(1)}, f32[2,256]{1,0:T(2,128)S(1)}, u32[]{:S(2)}, u32[]{:S(2)}) collective-permute-start(f32[2,256]{1,0:T(2,128)S(1)} %pad_maximum_fusion.3.refs_10_), channel_id=1, source_target_pairs={{0,13},{1,12},{2,15},{3,14},{4,9},{5,8},{6,11},{7,10},{8,5},{9,4},... | collective-permute-start | bytes 6152 | tf_op jit(solution)/shard_map/ppermute | solution.py:28
  52.8 4.0 %collective-permute-start.21 = (f32[2,256]{1,0:T(2,128)S(1)}, f32[2,256]{1,0:T(2,128)S(1)}, u32[]{:S(2)}, u32[]{:S(2)}) collective-permute-start(f32[2,256]{1,0:T(2,128)S(1)} %pad_maximum_fusion.3.refs_10_), channel_id=1, source_target_pairs={{0,9},{1,8},{2,11},{3,10},{4,13},{5,12},{6,15},{7,14},{8,1},{9,0},... | collective-permute-start | bytes 6152 | tf_op jit(solution)/shard_map/ppermute | solution.py:28
  53.6 3.2 %collective-permute-start.20 = (f32[2,256]{1,0:T(2,128)S(1)}, f32[2,256]{1,0:T(2,128)S(1)}, u32[]{:S(2)}, u32[]{:S(2)}) collective-permute-start(f32[2,256]{1,0:T(2,128)S(1)} %pad_maximum_fusion.3.refs_10_), channel_id=1, source_target_pairs={{0,5},{1,4},{2,7},{3,6},{4,1},{5,0},{6,3},{7,2},{8,13},{9,12},{10,... | collective-permute-start | bytes 6152 | tf_op jit(solution)/shard_map/ppermute | solution.py:28
  59.2 1.5 %collective-permute-start.25 = (f32[2,256]{1,0:T(2,128)S(1)}, f32[2,256]{1,0:T(2,128)S(1)}, u32[]{:S(2)}, u32[]{:S(2)}) collective-permute-start(f32[2,256]{1,0:T(2,128)S(1)} %get-tuple-element.93), channel_id=1, source_target_pairs={{0,1},{1,0},{2,3},{3,2},{4,5},{5,4},{6,7},{7,6},{8,9},{9,8},{10,11... | collective-permute-start | bytes 6152 | tf_op jit(solution)/shard_map/ppermute | solution.py:28
  60.8 4.6 %collective-permute-start.26 = (f32[2,256]{1,0:T(2,128)S(1)}, f32[2,256]{1,0:T(2,128)S(1)}, u32[]{:S(2)}, u32[]{:S(2)}) collective-permute-start(f32[2,256]{1,0:T(2,128)S(1)} %pad_maximum_fusion.4), channel_id=1, source_target_pairs={{0,3},{1,2},{2,1},{3,0},{4,7},{5,6},{6,5},{7,4},{8,11},{9,10},{10,... | collective-permute-start | bytes 6152 | tf_op jit(solution)/shard_map/ppermute | solution.py:28
  61.0 9.4 %collective-permute-start.23 = (f32[64,256]{1,0:T(8,128)S(1)}, f32[64,256]{1,0:T(8,128)S(1)}, u32[]{:S(2)}, u32[]{:S(2)}) collective-permute-start(f32[64,256]{1,0:T(8,128)S(1)} %get-tuple-element.86), channel_id=1, source_target_pairs={{0,1},{1,2},{2,3},{3,4},{4,5},{5,6},{6,7},{7,8},{8,9},{9,10},{10,1... | collective-permute-start | bytes 196616 | tf_op jit(solution)/shard_map/ppermute | solution.py:23
  61.3 9.0 %collective-permute-start.24 = (f32[64,256]{1,0:T(8,128)S(1)}, f32[64,256]{1,0:T(8,128)S(1)}, u32[]{:S(2)}, u32[]{:S(2)}) collective-permute-start(f32[64,256]{1,0:T(8,128)S(1)} %get-tuple-element.87), channel_id=1, source_target_pairs={{0,15},{1,0},{2,1},{3,2},{4,3},{5,4},{6,5},{7,6},{8,7},{9,8},{10,9... | collective-permute-start | bytes 196616 | tf_op jit(solution)/shard_map/ppermute | solution.py:23
  65.4 4.9 %collective-permute-start.29 = (f32[2,256]{1,0:T(2,128)S(1)}, f32[2,256]{1,0:T(2,128)S(1)}, u32[]{:S(2)}, u32[]{:S(2)}) collective-permute-start(f32[2,256]{1,0:T(2,128)S(1)} %pad_maximum_fusion.5.refs_10_), channel_id=1, source_target_pairs={{0,13},{1,12},{2,15},{3,14},{4,9},{5,8},{6,11},{7,10},{8,5},{9,4},... | collective-permute-start | bytes 6152 | tf_op jit(solution)/shard_map/ppermute | solution.py:28
  66.3 4.0 %collective-permute-start.28 = (f32[2,256]{1,0:T(2,128)S(1)}, f32[2,256]{1,0:T(2,128)S(1)}, u32[]{:S(2)}, u32[]{:S(2)}) collective-permute-start(f32[2,256]{1,0:T(2,128)S(1)} %pad_maximum_fusion.5.refs_10_), channel_id=1, source_target_pairs={{0,9},{1,8},{2,11},{3,10},{4,13},{5,12},{6,15},{7,14},{8,1},{9,0},... | collective-permute-start | bytes 6152 | tf_op jit(solution)/shard_map/ppermute | solution.py:28
  67.1 3.2 %collective-permute-start.27 = (f32[2,256]{1,0:T(2,128)S(1)}, f32[2,256]{1,0:T(2,128)S(1)}, u32[]{:S(2)}, u32[]{:S(2)}) collective-permute-start(f32[2,256]{1,0:T(2,128)S(1)} %pad_maximum_fusion.5.refs_10_), channel_id=1, source_target_pairs={{0,5},{1,4},{2,7},{3,6},{4,1},{5,0},{6,3},{7,2},{8,13},{9,12},{10,... | collective-permute-start | bytes 6152 | tf_op jit(solution)/shard_map/ppermute | solution.py:28
  71.5 1.6 %collective-permute-start.30 = (f32[2,512]{1,0:T(2,128)S(1)}, f32[2,512]{1,0:T(2,128)S(1)}, u32[]{:S(2)}, u32[]{:S(2)}) collective-permute-start(f32[2,512]{1,0:T(2,128)S(1)} %get-tuple-element.98), channel_id=1, source_target_pairs={{0,1},{1,0},{2,3},{3,2},{4,5},{5,4},{6,7},{7,6},{8,9},{9,8},{10,11... | collective-permute-start | bytes 12296 | tf_op jit(solution)/shard_map/ppermute | solution.py:28
  73.1 3.1 %collective-permute-start.31 = (f32[2,512]{1,0:T(2,128)S(1)}, f32[2,512]{1,0:T(2,128)S(1)}, u32[]{:S(2)}, u32[]{:S(2)}) collective-permute-start(f32[2,512]{1,0:T(2,128)S(1)} %pad_maximum_fusion), channel_id=1, source_target_pairs={{0,3},{1,2},{2,1},{3,0},{4,7},{5,6},{6,5},{7,4},{8,11},{9,10},{10,... | collective-permute-start | bytes 12296 | tf_op jit(solution)/shard_map/ppermute | solution.py:28
  76.2 4.9 %collective-permute-start.34 = (f32[2,512]{1,0:T(2,128)S(1)}, f32[2,512]{1,0:T(2,128)S(1)}, u32[]{:S(2)}, u32[]{:S(2)}) collective-permute-start(f32[2,512]{1,0:T(2,128)S(1)} %pad_maximum_fusion.1.refs_3_), channel_id=1, source_target_pairs={{0,13},{1,12},{2,15},{3,14},{4,9},{5,8},{6,11},{7,10},{8,5},{9,4},... | collective-permute-start | bytes 12296 | tf_op jit(solution)/shard_map/ppermute | solution.py:28
  78.6 3.9 %collective-permute-start.33 = (f32[2,512]{1,0:T(2,128)S(1)}, f32[2,512]{1,0:T(2,128)S(1)}, u32[]{:S(2)}, u32[]{:S(2)}) collective-permute-start(f32[2,512]{1,0:T(2,128)S(1)} %pad_maximum_fusion.1.refs_3_), channel_id=1, source_target_pairs={{0,9},{1,8},{2,11},{3,10},{4,13},{5,12},{6,15},{7,14},{8,1},{9,0},... | collective-permute-start | bytes 12296 | tf_op jit(solution)/shard_map/ppermute | solution.py:28
  79.4 3.1 %collective-permute-start.32 = (f32[2,512]{1,0:T(2,128)S(1)}, f32[2,512]{1,0:T(2,128)S(1)}, u32[]{:S(2)}, u32[]{:S(2)}) collective-permute-start(f32[2,512]{1,0:T(2,128)S(1)} %pad_maximum_fusion.1.refs_3_), channel_id=1, source_target_pairs={{0,5},{1,4},{2,7},{3,6},{4,1},{5,0},{6,3},{7,2},{8,13},{9,12},{10,... | collective-permute-start | bytes 12296 | tf_op jit(solution)/shard_map/ppermute | solution.py:28
